TPU v7x, 512 devices: a whole 4x4x16 slice. The times are simulated.
512 devices in a mesh: kv: 4 (over x), seq: 16 (over z), exp: 8 (over y, core).
Axes of the slice: x: 4, y: 4, z: 16, core: 2. Of those that a mesh axis runs over, the one named last changes fastest.
Arguments:
- queries: bfloat16 [64, 64, 2048], P(('kv', 'seq')), may hold values from -8 to 8
- draft_kv: bfloat16 [2, 64, 64, 2048], P(None, ('kv', 'seq'), 'exp'), may hold values from -12 to 12
- kv_pool: bfloat16 [2, 6144, 16, 2048], P(None, ('kv', 'seq', 'exp')), may hold values from -12 to 12
- page_table: int32 [64, 12, 8], P(('kv', 'seq'), None, 'exp'), may hold values from 0 to 11, as said below
- cache_lens: int32 [64], P(('kv', 'seq')), may hold values from 1 to 1536, as said below
- parents: int32 [64, 64], P(('kv', 'seq')), may hold values from -1 to 62, as said below
- hidden: bfloat16 [64, 64, 2048], P(('kv', 'seq')), may hold values from -36 to 36
- norm_gain: bfloat16 [2048], replicated, may hold values from 0.5 to 1.5
- out_proj: bfloat16 [2048, 2048], P('exp'), may hold values from -0.125 to 0.125
- router: bfloat16 [2048, 64], replicated, may hold values from -0.125 to 0.125
- routes: int32 [64, 64, 8], P(('kv', 'seq')), may hold values from 0 to 63, all different within a row; in each aligned block of 64 rows (0 to 63, 64 to 127, ..., all dimensions but the last counted through in order) at most 16 rows name the same one
- gate_w: bfloat16 [64, 2048, 1024], P(('kv', 'seq'), None, 'exp'), may hold values from -0.125 to 0.125
- up_w: bfloat16 [64, 2048, 1024], P(('kv', 'seq'), None, 'exp'), may hold values from -0.125 to 0.125
- down_w: bfloat16 [64, 1024, 2048], P(('kv', 'seq'), 'exp'), may hold values from -0.1875 to 0.1875
Outputs:
- output: bfloat16 [64, 64, 2048], P(('kv', 'seq'), None, 'exp')
Inputs may be any that keep to these rules, and one draw needn't show every extreme that they name: For one block of 1 request and one page set s, the entries page_table[r, j, s] over the block's requests r and all j are a permutation of 0 .. 11. `cache_lens`: some request has exactly 1536 cached positions. parents[r, 0] = -1; for i >= 1, parents[r, i] is an earlier draft position. `routes`: in each aligned block of 64 token rows (the rows of one device, requests in order), no expert is named by more than 16 rows.
All inputs are finite; a program needn't handle non-finite values.
Results may differ from a plain program's by a relative error of at most 0.02.
Values may be sent and summed in bfloat16 or wider, within the bound.
No kernel may reach another device: no remote copies, remote signals or barrier semaphores. Data moves between devices by JAX's collectives and lax.ppermute only.
A program may use at most 64 MiB of HBM per device.

v0:
```python
import jax
import jax.numpy as jnp
from jax import lax
from jax.sharding import PartitionSpec as P

D = 2048
H = 16
EXPERTS = 64
TOPK = 8
CAP = 16


NEG_FILL = -1e30
EPS_NORM = 1e-06


def merged(x, axis, combine):
    everything = jax.tree.map(
        lambda part, kind: lax.all_gather(part.astype(kind), axis),
        x,
        (jnp.bfloat16, jnp.bfloat16, jnp.bfloat16),
    )

    def take(k):
        return jax.tree.map(lambda part, own: part[k].astype(own.dtype), everything, x)

    return lax.fori_loop(
        1, lax.axis_size(axis), lambda k, so_far: combine(so_far, take(k)), take(0)
    )


def ancestry(parents, draft_len):
    positions = jnp.arange(draft_len, dtype=jnp.int32)
    linked = (parents[:, :, None] == positions[None, None, :]).astype(jnp.float32)
    linked = linked + jnp.eye(draft_len, dtype=jnp.float32)[None]
    for doubling in range((draft_len - 1).bit_length()):
        linked = jnp.minimum(
            jnp.einsum("nij,njk->nik", linked, linked, precision=lax.Precision.HIGHEST), 1.0
        )
    return linked


def slot_numbers(flat_routes):
    expert_ids = jnp.arange(EXPERTS, dtype=jnp.int32)
    picked = (flat_routes[:, None] == expert_ids[None, :]).astype(jnp.int32)
    earlier = jnp.cumsum(picked, axis=0) - picked
    return flat_routes * CAP + jnp.sum(earlier * picked, axis=1)


def merge_pair(former, latter):
    new_max = jnp.maximum(former[0], latter[0])
    former_scale = jnp.exp(former[0] - new_max)
    latter_scale = jnp.exp(latter[0] - new_max)
    return (
        new_max,
        former[1] * former_scale + latter[1] * latter_scale,
        former[2] * former_scale[..., None] + latter[2] * latter_scale[..., None],
    )


def send_out(outbound):
    return lax.all_to_all(outbound, ("kv", "seq"), split_axis=0, concat_axis=0, tiled=True)


def local(
    queries,
    draft_kv,
    kv_pool,
    page_table,
    cache_lens,
    parents,
    hidden,
    norm_gain,
    out_proj,
    router,
    routes,
    gate_w,
    up_w,
    down_w,
):
    set_count = lax.axis_size("exp")
    my_set = lax.axis_index("exp")
    req_count, draft_len, feature_width = queries.shape
    head_dim = feature_width // H
    head_share = H // set_count
    page_count = page_table.shape[1]
    page_len = kv_pool.shape[2]
    draft_share = draft_kv.shape[2]
    pool_slots = page_table[:, :, 0]
    cache_keys = kv_pool[0][pool_slots].reshape(req_count, page_count * page_len, feature_width)
    cache_values = kv_pool[1][pool_slots].reshape(req_count, page_count * page_len, feature_width)
    page_ids = jnp.arange(page_count, dtype=jnp.int32)[:, None] * set_count + my_set
    positions = (page_ids * page_len + jnp.arange(page_len, dtype=jnp.int32)[None, :]).reshape(-1)
    cache_seen = positions[None, :] < cache_lens[:, None]
    linked = ancestry(parents, draft_len)
    draft_seen = lax.dynamic_slice_in_dim(linked, my_set * draft_share, draft_share, 2) > 0.5
    visible = jnp.concatenate(
        [
            jnp.broadcast_to(cache_seen[:, None, :], (req_count, draft_len, page_count * page_len)),
            draft_seen,
        ],
        axis=2,
    )
    key_rows = jnp.concatenate([cache_keys, draft_kv[0]], axis=1).reshape(
        req_count, -1, H, head_dim
    )
    value_rows = jnp.concatenate([cache_values, draft_kv[1]], axis=1).reshape(
        req_count, -1, H, head_dim
    )
    query_rows = queries.reshape(req_count, draft_len, H, head_dim)
    scores = jnp.einsum(
        "rqhd,rkhd->rhqk", query_rows, key_rows, preferred_element_type=jnp.float32
    ) * head_dim ** (-0.5)
    scores = jnp.where(visible[:, None], scores, NEG_FILL)
    row_max = jnp.max(scores, axis=3)
    weights = jnp.where(visible[:, None], jnp.exp(scores - row_max[..., None]), 0.0)
    row_sum = jnp.sum(weights, axis=3)
    weighted = jnp.einsum(
        "rhqk,rkhd->rqhd",
        weights.astype(jnp.bfloat16),
        value_rows,
        preferred_element_type=jnp.float32,
    )
    row_max = jnp.transpose(row_max, (0, 2, 1))
    row_sum = jnp.transpose(row_sum, (0, 2, 1))
    row_max, row_sum, weighted = merged((row_max, row_sum, weighted), "exp", merge_pair)
    attended = (weighted / row_sum[..., None]).astype(jnp.bfloat16)
    attended = lax.dynamic_slice_in_dim(attended, my_set * head_share, head_share, 2)
    token_rows = req_count * draft_len
    attended = attended.reshape(token_rows, head_share * head_dim)
    partial_value = jnp.dot(attended, out_proj, preferred_element_type=jnp.float32)
    projected = lax.psum(partial_value.astype(jnp.bfloat16), "exp").astype(jnp.float32)
    residual = hidden.reshape(token_rows, D).astype(jnp.float32) + projected
    mean_sq = jnp.mean(residual * residual, axis=1, keepdims=True)
    normed = (
        residual * lax.rsqrt(mean_sq + EPS_NORM) * norm_gain.astype(jnp.float32)[None, :]
    ).astype(jnp.bfloat16)
    logits = jnp.dot(normed, router, preferred_element_type=jnp.float32)
    chosen = routes.reshape(token_rows, TOPK)
    gate_values = jax.nn.sigmoid(jnp.take_along_axis(logits, chosen, axis=1))
    slot_of = slot_numbers(chosen.reshape(-1)).reshape(token_rows, TOPK)
    slot_ids = jnp.arange(EXPERTS * CAP, dtype=jnp.int32)
    onehot = jnp.any(slot_of[None, :, :] == slot_ids[:, None, None], axis=2).astype(jnp.bfloat16)
    kv_count = lax.axis_size("kv")
    seq_count = lax.axis_size("seq")
    source_count = kv_count * seq_count
    local_experts = gate_w.shape[0]
    column_count = D // set_count
    buffer = jnp.dot(onehot, normed, preferred_element_type=jnp.float32).astype(jnp.bfloat16)
    received = send_out(buffer.reshape(source_count, local_experts, CAP, D))
    gate_pre = jnp.einsum("secd,edf->secf", received, gate_w, preferred_element_type=jnp.float32)
    up_pre = jnp.einsum("secd,edf->secf", received, up_w, preferred_element_type=jnp.float32)
    activity = (jax.nn.silu(gate_pre) * up_pre).astype(jnp.bfloat16)
    finished = jnp.einsum(
        "secf,efd->secd", activity, down_w, preferred_element_type=jnp.float32
    ).astype(jnp.bfloat16)
    returned = lax.all_to_all(finished, ("kv", "seq"), split_axis=0, concat_axis=0, tiled=True)
    flat_back = returned.reshape(EXPERTS * CAP, D)
    combined = jnp.zeros((token_rows, D), jnp.float32)
    for pick_index in range(TOPK):
        combined = combined + gate_values[:, pick_index : pick_index + 1] * flat_back[
            slot_of[:, pick_index]
        ].astype(jnp.float32)
    summed_share = lax.psum_scatter(
        combined.astype(jnp.bfloat16), "exp", scatter_dimension=1, tiled=True
    ).astype(jnp.float32)
    own_columns = lax.dynamic_slice_in_dim(residual, my_set * column_count, column_count, 1)
    return (
        (own_columns + summed_share)
        .astype(jnp.bfloat16)
        .reshape(req_count, draft_len, column_count)
    )


def solution(mesh):
    in_specs = (
        P(("kv", "seq"), None, None),
        P(None, ("kv", "seq"), "exp", None),
        P(None, ("kv", "seq", "exp"), None, None),
        P(("kv", "seq"), None, "exp"),
        P(("kv", "seq")),
        P(("kv", "seq"), None),
        P(("kv", "seq"), None, None),
        P(),
        P("exp", None),
        P(),
        P(("kv", "seq"), None, None),
        P(("kv", "seq"), None, "exp"),
        P(("kv", "seq"), None, "exp"),
        P(("kv", "seq"), "exp", None),
    )
    out_specs = P(("kv", "seq"), None, "exp")
    return jax.shard_map(local, mesh=mesh, in_specs=in_specs, out_specs=out_specs, check_vma=False)
```

profile of v0, /device:TPU:1, one launch (start us, length us, event | category | flops | bytes accessed | tf_op | source)
XLA Modules:
  0.0 631.2 jit_solution(8566334115093052938)
XLA Ops:
  10.7 1.7 copy.118
  17.0 1.9 fusion.80
  22.9 19.5 %all-gather.1 = bf16[8,64,16]{1,2,0:T(8,128)(2,1)S(1)} all-gather(bf16[1,64,16]{1,2,0:T(8,128)(2,1)S(1)} %bitcast.232), channel_id=3, replica_groups=mesh['kv'=4,'seq'=16,'exp'=8] {'exp'}, dimensions={0}, use_global_device_ids=true | all-gather | bytes 18432 | tf_op jit(solution)/shard_map/all_gather | solution.py:19
  42.3 12.8 %all-gather = bf16[8,64,16]{1,2,0:T(8,128)(2,1)S(1)} all-gather(bf16[1,64,16]{1,2,0:T(8,128)(2,1)S(1)} %convert_bitcast_fusion.2), channel_id=2, replica_groups=mesh['kv'=4,'seq'=16,'exp'=8] {'exp'}, dimensions={0}, use_global_device_ids=true | all-gather | bytes 18432 | tf_op jit(solution)/shard_map/all_gather | solution.py:19
  55.2 3.8 all-gather.5.cloned.1.call-done
  60.0 11.8 %while.19 = (s32[]{:T(128)}, f32[1,64,16]{1,2,0:T(8,128)S(1)}, f32[1,64,16]{1,2,0:T(8,128)S(1)}, f32[1,64,16,128]{3,2,1,0:T(8,128)S(1)}, bf16[8,1,64,16]{2,3,1,0...) while((s32[]{:T(128)}, f32[1,64,16]{1,2,0:T(8,128)S(1)}, ...), condition=%wide.region_3.4_spmd, body=%wide.region_2.3_spmd.sunk | while | flops 534533 | bytes 1382547 | solution.py:27
  73.8 73.4 %all-reduce.2.cloned.1.call-done = bf16[64,2048]{1,0:T(8,128)(2,1)} async-done(((bf16[64,2048]{1,0:T(8,128)(2,1)}), bf16[64,2048]{1,0:T(8,128)(2,1)}) %all-reduce.2.cloned.1.call-update) | async-done | bytes 262160 | tf_op jit(solution)/shard_map/psum | solution.py:132
  147.2 2.0 convert_add_fusion
  149.2 2.3 convolution_convert_fusion
  151.5 196.2 %all_to_all.10 = bf16[64,1,16,2048]{3,2,1,0:T(8,128)(2,1)S(1)} all-to-all(bf16[64,1,16,2048]{3,2,1,0:T(8,128)(2,1)S(1)} %bitcast.219), channel_id=1, replica_groups=mesh['kv'=4,'seq'=16,'exp'=8] {'kv','seq'}, dimensions={0} | all-to-all | bytes 8388608 | tf_op jit(solution)/shard_map/all_to_all | solution.py:62
  347.7 2.0 copy-done.1
  350.9 8.5 %convert_bitcast_fusion = bf16[64,1,16,2048]{3,2,1,0:T(8,128)(2,1)} fusion(bf16[64,1,16,2048]{3,2,1,0:T(8,128)(2,1)} %copy-done.1, bf16[1,128,2048]{2,1,0:T(8,128)(2,1)S(1)} %copy-done.5, bf16[1,2048,128]{2,1,0:T(8,128)(2,1)S(1)} %copy-done.6, f32[64,1,16,128]{3,2,0,1:T(8,128)S(1)} %fusion.12), kind=kOutput, calls=%fused_computation.25 | convolution fusion | flops 1076625408 | bytes 9961472 | tf_op jit(solution)/shard_map/secf,efd->secd/dot_general | solution.py:154
  359.4 12.8 %all-to-all-start.1 = ((bf16[64,1,16,2048]{3,2,1,0:T(8,128)(2,1)}), bf16[64,1,16,2048]{3,2,1,0:T(8,128)(2,1)}, u32[]{:S(2)}, u32[]{:S(2)}) async-start(bf16[64,1,16,2048]{3,2,1,0:T(8,128)(2,1)} %convert_bitcast_fusion), calls=%async_computation.1 | async-start | bytes 8388608 | tf_op jit(solution)/shard_map/all_to_all | solution.py:157
  373.3 3.8 gather_fusion.10
  377.5 175.2 %all-to-all-done.1 = bf16[64,1,16,2048]{3,2,1,0:T(8,128)(2,1)} async-done(((bf16[64,1,16,2048]{3,2,1,0:T(8,128)(2,1)}), bf16[64,1,16,2048]{3,2,1,0:T(8,128)(2,1)}, u32[]{:S(2)}, u32[]{:S(2)}) %all-to-all-start.1) | async-done | bytes 4194336 | tf_op jit(solution)/shard_map/all_to_all | solution.py:157
  552.8 3.7 gather_fusion.9
  556.5 3.7 gather_fusion.8
  560.2 3.7 gather_fusion.7
  563.9 3.7 gather_fusion.6
  567.6 3.7 gather_fusion.5
  571.4 3.7 gather_fusion.4
  575.1 3.7 gather_fusion.3
  578.8 3.7 gather_fusion.2
  583.7 39.5 %reduce-scatter.2.cloned.1.call-done = bf16[64,256]{1,0:T(8,128)(2,1)} async-done(((bf16[64,2048]{1,0:T(8,128)(2,1)}), bf16[64,256]{1,0:T(8,128)(2,1)}) %reduce-scatter.2.cloned.1.call-update) | async-done | bytes 32784 | tf_op jit(solution)/shard_map/reduce_scatter | solution.py:164
  (136 shorter events, 31.6 us)
Async XLA Ops:
  6.5 65.5 %copy-start = (bf16[256,2048]{1,0:T(8,128)(2,1)S(1)}, bf16[256,2048]{1,0:T(8,128)(2,1)}, u32[]{:S(2)}) copy-start(bf16[256,2048]{1,0:T(8,128)(2,1)} %param.24) | copy-start | bytes 3145732
  6.5 52.4 %all-gather.5.cloned.1.call-start = ((), (), s32[]{:S(2)}) async-start(), calls=%async_computation.5 | async-start | bytes 2359296 | tf_op jit(solution)/shard_map/all_gather | solution.py:19
  15.3 1.7 copy-start.7
  16.5 3.7 copy-start.8
  16.5 4.0 copy-start.9
  20.2 127.0 %all-reduce.2.cloned.1.call-start = ((), (), s32[]{:S(2)}) async-start(), calls=%async_computation.3 | async-start | bytes 524288 | tf_op jit(solution)/shard_map/psum | solution.py:132
  59.9 87.3 %copy-start.2 = (bf16[1,64,2048]{2,1,0:T(8,128)(2,1)S(1)}, bf16[1,64,2048]{2,1,0:T(8,128)(2,1)}, u32[]{:S(2)}) copy-start(bf16[1,64,2048]{2,1,0:T(8,128)(2,1)} %param.22) | copy-start | bytes 786436
  151.5 198.2 %copy-start.4 = (bf16[1,2048,128]{2,1,0:T(8,128)(2,1)S(1)}, bf16[1,2048,128]{2,1,0:T(8,128)(2,1)}, u32[]{:S(2)}) copy-start(bf16[1,2048,128]{2,1,0:T(8,128)(2,1)} %param.27) | copy-start | bytes 1572868
  347.7 2.0 copy-start.1
  349.7 1.3 copy-start.5
  349.7 1.3 copy-start.6
  359.4 13.6 %copy-start.3 = (bf16[64,2048]{1,0:T(8,128)(2,1)S(1)}, bf16[64,2048]{1,0:T(8,128)(2,1)}, u32[]{:S(2)}) copy-start(bf16[64,2048]{1,0:T(8,128)(2,1)} %all-reduce.2.cloned.1.call-done) | copy-start | bytes 786436
  359.4 13.6 %copy-start.10 = (bf16[2048,64]{0,1:T(8,128)(2,1)S(1)}, bf16[2048,64]{0,1:T(8,128)(2,1)}, u32[]{:S(2)}) copy-start(bf16[2048,64]{0,1:T(8,128)(2,1)} %param.25) | copy-start | bytes 786436
  359.4 193.4 %all-to-all-start.1 = ((bf16[64,1,16,2048]{3,2,1,0:T(8,128)(2,1)}), bf16[64,1,16,2048]{3,2,1,0:T(8,128)(2,1)}, u32[]{:S(2)}, u32[]{:S(2)}) async-start(bf16[64,1,16,2048]{3,2,1,0:T(8,128)(2,1)} %convert_bitcast_fusion), calls=%async_computation.1 | async-start | bytes 8388608 | tf_op jit(solution)/shard_map/all_to_all | solution.py:157
  372.2 251.0 %reduce-scatter.2.cloned.1.call-start = ((), (), s32[]{:S(2)}) async-start(), calls=%async_computation.4 | async-start | bytes 294912 | tf_op jit(solution)/shard_map/reduce_scatter | solution.py:164
Sparse Core Ops, SparseCore 0:
  20.3 38.6 all-gather.4
  73.2 73.9 all-reduce.1
  583.8 39.3 reduce-scatter.1
where the time goes:
time: 633 us; the launch traced here: 631 us
  waiting for transfers between devices  292 us (46%)
  blocking collectives  228 us (36%)
  local copies, waits for them, and re-layouts  46 us (7%)
  other arithmetic  20.7 us (3%)
  matrix products  16.5 us (3%)
  between operations  14.3 us (2%)
  starting transfers between devices  12.9 us (2%)
    all_to_all x1, blocking collectives, send_out(): lax.all_to_all(outbound, ('kv', 'seq'), split_axis=0, concat_axis=0, tile...  196 us
    all_to_all x1, waiting for transfers between devices, local(): lax.all_to_all(finished, ('kv', 'seq'), split_axis=0, concat_axis=0, tile...  175 us
    psum x1, waiting for transfers between devices, local(): lax.psum(partial_value.astype(jnp.bfloat16), 'exp').astype(jnp.float32)  73.4 us
    reduce_scatter x1, waiting for transfers between devices, local(): lax.psum_scatter(combined.astype(jnp.bfloat16), 'exp', scatter_dimension=...  39.5 us
    all_gather x2, blocking collectives, merged(): lax.all_gather(part.astype(kind), axis)  32.3 us
    gather x8, local copies, waits for them, and re-layouts, local(): flat_back[slot_of[:, pick_index]].astype(jnp.float32)  29.7 us
    all_to_all x1, starting transfers between devices, local(): lax.all_to_all(finished, ('kv', 'seq'), split_axis=0, concat_axis=0, tile...  12.8 us
  transfers between devices with their start and end apart: 4, of which 4 were waited for; matrix products, arithmetic and copies ran while one was open for 1% of the time, Pallas kernels for 0%

commit v1 on v0

v1 whole, which is shorter than its diff:
```python
import jax
import jax.numpy as jnp
from jax import lax
from jax.experimental import pallas as pl
from jax.experimental.pallas import tpu as pltpu
from jax.sharding import PartitionSpec as P

D = 2048
H = 16
HD = 128
FF = 1024
EXPERTS = 64
TOPK = 8
DRAFT = 64
PAGE = 16
PPD = 12
SETS = 8
KEYS = PPD * PAGE
ROWS = KEYS + 16
TOK = DRAFT // SETS
WIDE = D + 2 * EXPERTS
STAT = DRAFT + 8
BLK = FF // SETS

NEG_FILL = -1e30
EPS_NORM = 1e-06
VMEM_LIMIT = 56 * 1024 * 1024


def nt(a, b):
    return lax.dot_general(a, b, (((1,), (1,)), ((), ())), preferred_element_type=jnp.float32)


def tn(a, b):
    return lax.dot_general(a, b, (((0,), (0,)), ((), ())), preferred_element_type=jnp.float32)


def nn(a, b):
    return lax.dot_general(a, b, (((1,), (0,)), ((), ())), preferred_element_type=jnp.float32)


def attention_kernel(
    table, info, q_ref, parents_ref, draft_ref, pool_ref, out_ref, kbuf, vbuf, seen_ref, sems
):
    copies = []
    for page in range(PPD):
        slot = table[page]
        rows = pl.ds(page * PAGE, PAGE)
        copies.append(pltpu.make_async_copy(pool_ref.at[0, slot], kbuf.at[rows], sems.at[0, page]))
        copies.append(pltpu.make_async_copy(pool_ref.at[1, slot], vbuf.at[rows], sems.at[1, page]))
    for copy in copies:
        copy.start()
    length = info[0]
    my_set = info[1]
    pad = jnp.zeros((8, D), jnp.float32)
    kbuf[KEYS:ROWS, :] = jnp.concatenate([draft_ref[0, 0].astype(jnp.float32), pad], axis=0).astype(
        jnp.bfloat16
    )
    vbuf[KEYS:ROWS, :] = jnp.concatenate([draft_ref[1, 0].astype(jnp.float32), pad], axis=0).astype(
        jnp.bfloat16
    )
    ancestor = lax.broadcasted_iota(jnp.int32, (DRAFT, 2 * DRAFT), 0)
    token = lax.broadcasted_iota(jnp.int32, (DRAFT, 2 * DRAFT), 1) % DRAFT
    linked = jnp.where((parents_ref[...] == ancestor) | (ancestor == token), 1.0, 0.0)
    for doubling in range((DRAFT - 1).bit_length()):
        narrow = linked.astype(jnp.bfloat16)
        linked = jnp.minimum(nn(narrow[:, :DRAFT], narrow), 1.0)
    seen_ref[...] = linked
    draft_seen = seen_ref[pl.ds(pl.multiple_of(my_set * TOK, TOK), TOK), :]
    key_row = lax.broadcasted_iota(jnp.int32, (KEYS, 2 * DRAFT), 0)
    position = ((key_row // PAGE) * SETS + my_set) * PAGE + key_row % PAGE
    cache_seen = jnp.where(position < length, 1.0, 0.0)
    seen = (
        jnp.concatenate(
            [cache_seen, draft_seen, jnp.zeros((8, 2 * DRAFT), jnp.float32)], axis=0
        )
        > 0.5
    )
    own = (lax.broadcasted_iota(jnp.int32, (2 * DRAFT, 2 * HD), 0) < DRAFT) == (
        lax.broadcasted_iota(jnp.int32, (2 * DRAFT, 2 * HD), 1) < HD
    )
    stat_row = lax.broadcasted_iota(jnp.int32, (8, 2 * DRAFT), 0)
    for copy in copies:
        copy.wait()
    for pair in range(H // 2):
        cols = slice(pair * 2 * HD, (pair + 1) * 2 * HD)
        query = q_ref[0, :, cols]
        query = jnp.where(own, jnp.concatenate([query, query], axis=0), jnp.zeros((), jnp.bfloat16))
        scores = nt(kbuf[:, cols], query) * (HD**-0.5)
        scores = jnp.where(seen, scores, NEG_FILL)
        top = jnp.max(scores, axis=0, keepdims=True).astype(jnp.bfloat16).astype(jnp.float32)
        weights = jnp.where(seen, jnp.exp(scores - top), 0.0)
        total = jnp.sum(weights, axis=0, keepdims=True)
        acc = tn(weights.astype(jnp.bfloat16), vbuf[:, cols])
        total_high = total.astype(jnp.bfloat16).astype(jnp.float32)
        stats = jnp.where(
            stat_row == 0,
            top,
            jnp.where(stat_row == 1, total_high, jnp.where(stat_row == 2, total - total_high, 0.0)),
        )
        out_ref[pair, 0:DRAFT, 0:HD] = acc[:DRAFT, :HD].astype(jnp.bfloat16)
        out_ref[pair, 0:DRAFT, HD : 2 * HD] = acc[DRAFT:, HD:].astype(jnp.bfloat16)
        out_ref[pair, DRAFT:STAT, 0:HD] = stats.astype(jnp.bfloat16)
        out_ref[pair, DRAFT:STAT, HD : 2 * HD] = jnp.zeros((8, HD), jnp.bfloat16)


def attention(table, info, queries, parents, draft_kv, kv_pool):
    vmem = pl.BlockSpec(memory_space=pltpu.VMEM)
    return pl.pallas_call(
        attention_kernel,
        out_shape=jax.ShapeDtypeStruct((SETS, STAT, 2 * HD), jnp.bfloat16),
        in_specs=[
            pl.BlockSpec(memory_space=pltpu.SMEM),
            pl.BlockSpec(memory_space=pltpu.SMEM),
            vmem,
            vmem,
            vmem,
            pl.BlockSpec(memory_space=pl.ANY),
        ],
        out_specs=vmem,
        scratch_shapes=[
            pltpu.VMEM((ROWS, D), jnp.bfloat16),
            pltpu.VMEM((ROWS, D), jnp.bfloat16),
            pltpu.VMEM((DRAFT, 2 * DRAFT), jnp.float32),
            pltpu.SemaphoreType.DMA((2, PPD)),
        ],
        compiler_params=pltpu.CompilerParams(vmem_limit_bytes=VMEM_LIMIT),
        name="attention",
    )(table, info, queries, parents, draft_kv, kv_pool)


def merge_kernel(parts_ref, proj_ref, out_ref):
    stats = parts_ref[:, DRAFT:STAT, 0:HD].astype(jnp.float32)
    tops = stats[:, 0, :]
    totals = stats[:, 1, :] + stats[:, 2, :]
    scale = jnp.exp(tops - jnp.max(tops, axis=0, keepdims=True))
    scale = scale / jnp.sum(scale * totals, axis=0, keepdims=True)
    scale = jnp.transpose(scale)
    heads = []
    for head in range(2):
        joined = jnp.zeros((DRAFT, HD), jnp.float32)
        for source in range(SETS):
            part = parts_ref[source, 0:DRAFT, head * HD : (head + 1) * HD].astype(jnp.float32)
            joined = joined + part * scale[head * DRAFT : (head + 1) * DRAFT, source : source + 1]
        heads.append(joined.astype(jnp.bfloat16))
    out_ref[...] = nn(jnp.concatenate(heads, axis=1), proj_ref[...]).astype(jnp.bfloat16)


def merge(parts, out_proj):
    return pl.pallas_call(
        merge_kernel,
        out_shape=jax.ShapeDtypeStruct((DRAFT, D), jnp.bfloat16),
        compiler_params=pltpu.CompilerParams(vmem_limit_bytes=VMEM_LIMIT),
        name="merge",
    )(parts, out_proj)


def norm_kernel(my_set, parts_ref, hidden_ref, gain_ref, router_ref, routes_ref, residual_ref, row_ref):
    residual = hidden_ref[0].astype(jnp.float32)
    for source in range(SETS):
        residual = residual + parts_ref[source].astype(jnp.float32)
    residual_ref[...] = residual
    mean_sq = jnp.mean(residual * residual, axis=1, keepdims=True)
    normed = (residual * lax.rsqrt(mean_sq + EPS_NORM) * gain_ref[...].astype(jnp.float32)).astype(
        jnp.bfloat16
    )
    logits = nn(normed, router_ref[...])
    gates = 1.0 / (1.0 + jnp.exp(-logits))
    expert = lax.broadcasted_iota(jnp.int32, (TOK, EXPERTS), 1)
    routes = routes_ref[0]
    chosen = routes[:, 0:1] == expert
    for pick in range(1, TOPK):
        chosen = chosen | (routes[:, pick : pick + 1] == expert)
    gates = jnp.where(chosen, gates, 0.0)
    high = gates.astype(jnp.bfloat16).astype(jnp.float32)
    row_ref[:, 0:D] = normed
    row_ref[:, D:WIDE] = jnp.concatenate([high, gates - high], axis=1).astype(jnp.bfloat16)


def norm(my_set, parts, hidden, norm_gain, router, routes):
    whole = lambda *shape: pl.BlockSpec(shape, lambda i, s: (0,) * len(shape))
    return pl.pallas_call(
        norm_kernel,
        out_shape=(
            jax.ShapeDtypeStruct((TOK, D), jnp.float32),
            jax.ShapeDtypeStruct((TOK, WIDE), jnp.bfloat16),
        ),
        grid_spec=pltpu.PrefetchScalarGridSpec(
            num_scalar_prefetch=1,
            grid=(1,),
            in_specs=[
                whole(SETS, TOK, D),
                pl.BlockSpec((1, TOK, D), lambda i, s: (0, s[0], 0)),
                whole(1, D),
                whole(D, EXPERTS),
                pl.BlockSpec((1, TOK, TOPK), lambda i, s: (0, s[0], 0)),
            ],
            out_specs=(whole(TOK, D), whole(TOK, WIDE)),
        ),
        compiler_params=pltpu.CompilerParams(vmem_limit_bytes=VMEM_LIMIT),
        name="norm",
    )(my_set, parts, hidden, norm_gain, router, routes)


def expert_kernel(my_expert, rows_ref, in_ref, down_ref, out_ref, act_ref, gate_ref):
    step = pl.program_id(0)

    @pl.when(step == 0)
    def _():
        gates = rows_ref[:, D:WIDE].astype(jnp.float32)
        lane = lax.broadcasted_iota(jnp.int32, gates.shape, 1) % EXPERTS
        gate_ref[...] = jnp.sum(jnp.where(lane == my_expert[0], gates, 0.0), axis=1, keepdims=True)

    @pl.when(step < SETS)
    def _():
        both = nn(rows_ref[:, 0:D], in_ref[0])
        gate, up = both[:, :BLK], both[:, BLK:]
        act = gate / (1.0 + jnp.exp(-gate)) * up
        act_ref[:, pl.ds(pl.multiple_of(step * BLK, BLK), BLK)] = act.astype(jnp.bfloat16)

    @pl.when(step >= SETS)
    def _():
        down = down_ref[...].reshape(FF, D // SETS)
        out_ref[...] = (nn(act_ref[...], down) * gate_ref[...]).astype(jnp.bfloat16)


def expert(my_expert, rows, weights):
    count = rows.shape[0]
    width = D // SETS
    return pl.pallas_call(
        expert_kernel,
        out_shape=jax.ShapeDtypeStruct((count, D), jnp.bfloat16),
        grid_spec=pltpu.PrefetchScalarGridSpec(
            num_scalar_prefetch=1,
            grid=(2 * SETS,),
            in_specs=[
                pl.BlockSpec((count, WIDE), lambda i, e: (0, 0)),
                pl.BlockSpec((1, D, width), lambda i, e: (jnp.minimum(i, SETS - 1), 0, 0)),
                pl.BlockSpec(
                    (SETS, BLK, width), lambda i, e: (0, D // BLK + jnp.maximum(i - SETS, 0), 0)
                ),
            ],
            out_specs=pl.BlockSpec((count, width), lambda i, e: (0, jnp.maximum(i - SETS, 0))),
            scratch_shapes=[
                pltpu.VMEM((count, FF), jnp.bfloat16),
                pltpu.VMEM((count, 1), jnp.float32),
            ],
        ),
        compiler_params=pltpu.CompilerParams(vmem_limit_bytes=VMEM_LIMIT),
        name="expert",
    )(my_expert, rows, weights, weights)


def local(
    queries,
    draft_kv,
    kv_pool,
    page_table,
    cache_lens,
    parents,
    hidden,
    norm_gain,
    out_proj,
    router,
    routes,
    gate_w,
    up_w,
    down_w,
):
    my_set = lax.axis_index("exp").astype(jnp.int32)
    kv_count = lax.axis_size("kv")
    seq_count = lax.axis_size("seq")
    my_expert = (lax.axis_index("kv") * seq_count + lax.axis_index("seq")).astype(jnp.int32)
    width = D // SETS
    packed = jnp.concatenate(
        [
            jnp.concatenate([gate_w[0], up_w[0]], axis=1),
            jnp.transpose(down_w[0].reshape(BLK, SETS, width), (1, 0, 2)).reshape(SETS * BLK, width),
        ],
        axis=0,
    )
    weights = lax.all_gather(packed, "exp")
    info = jnp.concatenate([cache_lens, my_set.reshape(1)])
    partials = attention(
        page_table.reshape(PPD),
        info,
        queries,
        jnp.concatenate([parents, parents], axis=1),
        draft_kv,
        kv_pool,
    )
    parts = lax.all_to_all(partials, "exp", 0, 0, tiled=True)
    projected = merge(parts, out_proj)
    shares = lax.all_to_all(projected.reshape(SETS, TOK, D), "exp", 0, 0, tiled=True)
    residual, row = norm(
        my_set.reshape(1), shares, hidden, norm_gain.reshape(1, D), router, routes
    )
    along_seq = lax.all_gather(row, "seq").reshape(1, seq_count * TOK, WIDE)
    rows = lax.all_to_all(
        jnp.broadcast_to(along_seq, (kv_count, seq_count * TOK, WIDE)), "kv", 0, 0, tiled=True
    ).reshape(kv_count * seq_count * TOK, WIDE)
    finished = expert(my_expert.reshape(1), rows, weights)
    back = lax.all_to_all(finished.reshape(kv_count, seq_count * TOK, D), "kv", 0, 0, tiled=True)
    back = jnp.sum(back.astype(jnp.float32), axis=0).astype(jnp.bfloat16)
    back = lax.all_to_all(back.reshape(seq_count, TOK, D), "seq", 0, 0, tiled=True)
    total = (residual + jnp.sum(back.astype(jnp.float32), axis=0)).astype(jnp.bfloat16)
    columns = jnp.transpose(total.reshape(TOK, SETS, width), (1, 0, 2))
    return lax.all_to_all(columns, "exp", 0, 0, tiled=True).reshape(1, DRAFT, width)


def solution(mesh):
    in_specs = (
        P(("kv", "seq"), None, None),
        P(None, ("kv", "seq"), "exp", None),
        P(None, ("kv", "seq", "exp"), None, None),
        P(("kv", "seq"), None, "exp"),
        P(("kv", "seq")),
        P(("kv", "seq"), None),
        P(("kv", "seq"), None, None),
        P(),
        P("exp", None),
        P(),
        P(("kv", "seq"), None, None),
        P(("kv", "seq"), None, "exp"),
        P(("kv", "seq"), None, "exp"),
        P(("kv", "seq"), "exp", None),
    )
    out_specs = P(("kv", "seq"), None, "exp")
    return jax.shard_map(local, mesh=mesh, in_specs=in_specs, out_specs=out_specs, check_vma=False)
```

time: 633 us -> 206 us (0.33)
  waiting for transfers between devices: 292 us -> 30 us
  blocking collectives: 228 us -> 114 us
  local copies, waits for them, and re-layouts: 46 us -> 7.97 us
  Pallas kernels: 0 us -> 27.8 us
  other arithmetic: 20.7 us -> 3.05 us
  matrix products: 16.5 us -> 0 us
    all_to_all x1 -> x2, waiting for transfers between devices: 175 us -> 30 us  [the longest x1 22.6 us: local(): lax.all_to_all(jnp.broadcast_to(along_seq, (kv_count, seq_count * TOK, WI...]
    all_to_all x1 -> x4, blocking collectives: 196 us -> 84.3 us  [the longest x1 24.1 us: local(): lax.all_to_all(back.reshape(seq_count, TOK, D), 'seq', 0, 0, tiled=True)]
    psum x1 -> x0, waiting for transfers between devices: 73.4 us -> none  [local(): lax.psum(partial_value.astype(jnp.bfloat16), 'exp').astype(jnp.float32)]
    reduce_scatter x1 -> x0, waiting for transfers between devices: 39.5 us -> none  [local(): lax.psum_scatter(combined.astype(jnp.bfloat16), 'exp', scatter_dimension=...]
    gather x14 -> x0, local copies, waits for them, and re-layouts: 34.9 us -> none  [the longest x8 29.7 us: local(): flat_back[slot_of[:, pick_index]].astype(jnp.float32)]
    pallas_call x0 -> x4, Pallas kernels: none -> 27.8 us  [the longest x1 17.1 us: expert(): pl.pallas_call(expert_kernel, out_shape=jax.ShapeDtypeStruct((count, D),...]
    dot_general x13 -> x0, matrix products: 16.5 us -> none  [the longest x1 8.46 us: local(): jnp.einsum('secf,efd->secd', activity, down_w, preferred_element_type=jnp...]
    add x10 -> x0, other arithmetic: 12.8 us -> none  [the longest x7 10 us: merge_pair(): former[2] * former_scale[..., None] + latter[2] * latter_scale[..., None]]
  transfers between devices with their start and end apart: 4 -> 3, of which waited for: 4 -> 2; matrix products, arithmetic and copies ran while one was open for 1% -> 2% of each run, Pallas kernels for 0% -> 5%
where the time goes in v1:
time: 206 us; the launch traced here: 205 us
  blocking collectives  114 us (55%)
  waiting for transfers between devices  30 us (15%)
  Pallas kernels  27.8 us (13%)
  between operations  14.1 us (7%)
  local copies, waits for them, and re-layouts  7.97 us (4%)
  starting transfers between devices  7.7 us (4%)
  other arithmetic  3.05 us (1%)
    all_gather x1, blocking collectives, local(): along_seq = lax.all_gather(row, 'seq').reshape(1, seq_count * TOK, WIDE)  30.1 us
    all_to_all x1, blocking collectives, local(): lax.all_to_all(back.reshape(seq_count, TOK, D), 'seq', 0, 0, tiled=True)  24.1 us
    all_to_all x1, blocking collectives, local(): lax.all_to_all(finished.reshape(kv_count, seq_count * TOK, D), 'kv', 0, 0...  23.8 us
    all_to_all x1, waiting for transfers between devices, local(): lax.all_to_all(jnp.broadcast_to(along_seq, (kv_count, seq_count * TOK, WI...  22.6 us
    all_to_all x1, blocking collectives, local(): parts = lax.all_to_all(partials, 'exp', 0, 0, tiled=True)  18.2 us
    all_to_all x1, blocking collectives, local(): lax.all_to_all(columns, 'exp', 0, 0, tiled=True).reshape(1, DRAFT, width)  18.1 us
    pallas_call x1, Pallas kernels, expert(): pl.pallas_call(expert_kernel, out_shape=jax.ShapeDtypeStruct((count, D),...  17.1 us
    all_to_all x1, waiting for transfers between devices, local(): lax.all_to_all(projected.reshape(SETS, TOK, D), 'exp', 0, 0, tiled=True)  7.43 us
  transfers between devices with their start and end apart: 3, of which 2 were waited for; matrix products, arithmetic and copies ran while one was open for 2% of the time, Pallas kernels for 5%

profile of v1, /device:TPU:1, one launch (start us, length us, event | category | flops | bytes accessed | tf_op | source)
XLA Modules:
  0.0 205.0 jit_solution(998928964048100751)
XLA Ops:
  6.5 1.2 copy.21
  7.9 1.3 pad_maximum_fusion
  9.9 0.7 pad_add_fusion.1.parents_ref
  10.6 0.6 pad_add_fusion.info
  11.2 5.5 %attention.1 = bf16[8,72,256]{2,1,0:T(8,128)(2,1)} custom-call(s32[12]{0:T(128)} %bitcast.33, s32[2]{0:T(128)} %pad_add_fusion.info, bf16[1,64,2048]{2,1,0:T(8,128)(2,1)} %q_ref.1, s32[1,128]{1,0:T(1,128)} %pad_add_fusion.1.parents_ref, bf16[2,1,8,2048]{3,2,1,0:T(8,128)(2,1)} %draft_ref.1, bf16[2,12,16,2048]{3,2,1,0:T(8,128)(2,1)} %pool_ref.1), custom_call_target="tpu_custom_call" | custom-call | tf_op jit(solution)/shard_map/attention/pallas_call | solution.py:109
  16.7 18.2 %all_to_all.30.parts_ref = bf16[8,72,256]{2,1,0:T(8,128)(2,1)} all-to-all(bf16[8,72,256]{2,1,0:T(8,128)(2,1)} %attention.1), channel_id=1, replica_groups=mesh['kv'=4,'seq'=16,'exp'=8] {'exp'}, dimensions={0} | all-to-all | bytes 589824 | tf_op jit(solution)/shard_map/all_to_all | solution.py:292
  35.0 3.0 %merge.1 = bf16[64,2048]{1,0:T(8,128)(2,1)} custom-call(bf16[8,72,256]{2,1,0:T(8,128)(2,1)} %all_to_all.30.parts_ref, bf16[256,2048]{1,0:T(8,128)(2,1)} %proj_ref.1), custom_call_target="tpu_custom_call" | custom-call | tf_op jit(solution)/shard_map/merge/pallas_call | solution.py:150
  37.9 3.7 %all-to-all-start.1 = ((bf16[8,8,2048]{2,1,0:T(8,128)(2,1)}), bf16[8,8,2048]{2,1,0:T(8,128)(2,1)S(1)}, u32[]{:S(2)}, u32[]{:S(2)}) async-start(bf16[8,8,2048]{2,1,0:T(8,128)(2,1)} %bitcast.27), calls=%async_computation.1 | async-start | bytes 524288 | tf_op jit(solution)/shard_map/all_to_all | solution.py:294
  41.6 0.6 reshape.39.gain_ref
  42.2 1.0 copy.18.router_ref
  43.2 0.7 copy.19.routes_ref
  43.9 7.4 %all-to-all-done.1.parts_ref = bf16[8,8,2048]{2,1,0:T(8,128)(2,1)S(1)} async-done(((bf16[8,8,2048]{2,1,0:T(8,128)(2,1)}), bf16[8,8,2048]{2,1,0:T(8,128)(2,1)S(1)}, u32[]{:S(2)}, u32[]{:S(2)}) %all-to-all-start.1) | async-done | bytes 262176 | tf_op jit(solution)/shard_map/all_to_all | solution.py:294
  51.4 0.7 copy-done.1
  52.1 2.1 %norm.1 = (f32[8,2048]{1,0:T(8,128)}, bf16[8,2176]{1,0:T(8,128)(2,1)}) custom-call(s32[1]{0:T(128)} %bitcast.my_set, bf16[8,8,2048]{2,1,0:T(8,128)(2,1)} %copy-done.1, bf16[1,64,2048]{2,1,0:T(8,128)(2,1)} %hidden_ref.1, bf16[1,2048]{1,0:T(2,128)(2,1)} %reshape.39.gain_ref, bf16[2048,64]{1,0:T(8,128)(2,1)} %copy.18.router_ref, s32[1,64,8]{2,1,0:T(8,128)} %copy.19.routes_ref), custom_call_target="tpu_custom_call" | custom-call | tf_op jit(solution)/shard_map/norm/pallas_call | solution.py:182
  54.2 30.1 %all-gather = bf16[128,2176]{1,0:T(8,128)(2,1)S(1)} all-gather(bf16[8,2176]{1,0:T(8,128)(2,1)} %get-tuple-element.8), channel_id=2, replica_groups=mesh['kv'=4,'seq'=16,'exp'=8] {'seq'}, dimensions={0}, use_global_device_ids=true | all-gather | bytes 591872 | tf_op jit(solution)/shard_map/all_gather | solution.py:298
  84.3 1.6 broadcast_in_dim.8
  85.8 4.0 %all-to-all-start.2 = ((bf16[4,128,2176]{2,1,0:T(8,128)(2,1)}), bf16[4,128,2176]{2,1,0:T(8,128)(2,1)S(1)}, u32[]{:S(2)}, u32[]{:S(2)}) async-start(bf16[4,128,2176]{2,1,0:T(8,128)(2,1)} %broadcast_in_dim.8), calls=%async_computation.2 | async-start | bytes 4456448 | tf_op jit(solution)/shard_map/all_to_all | solution.py:299
  89.9 22.6 %all-to-all-done.2 = bf16[4,128,2176]{2,1,0:T(8,128)(2,1)S(1)} async-done(((bf16[4,128,2176]{2,1,0:T(8,128)(2,1)}), bf16[4,128,2176]{2,1,0:T(8,128)(2,1)S(1)}, u32[]{:S(2)}, u32[]{:S(2)}) %all-to-all-start.2) | async-done | bytes 2228256 | tf_op jit(solution)/shard_map/all_to_all | solution.py:299
  112.5 1.4 copy-done
  113.8 17.1 %expert.1 = bf16[512,2048]{1,0:T(8,128)(2,1)} custom-call(s32[1]{0:T(128)} %bitcast.3.my_expert, bf16[512,2176]{1,0:T(8,128)(2,1)} %bitcast.22, bf16[8,3072,256]{2,1,0:T(8,128)(2,1)} %bitcast.20, bf16[8,3072,256]{2,1,0:T(8,128)(2,1)} %bitcast.21), custom_call_target="tpu_custom_call" | custom-call | tf_op jit(solution)/shard_map/expert/pallas_call | solution.py:230
  131.0 23.8 %all_to_all.31 = bf16[4,128,2048]{2,1,0:T(8,128)(2,1)S(1)} all-to-all(bf16[4,128,2048]{2,1,0:T(8,128)(2,1)} %bitcast.23), channel_id=1, replica_groups=mesh['kv'=4,'seq'=16,'exp'=8] {'kv'}, dimensions={0} | all-to-all | bytes 4194304 | tf_op jit(solution)/shard_map/all_to_all | solution.py:303
  155.2 24.1 %all_to_all.32 = bf16[16,8,2048]{2,1,0:T(8,128)(2,1)S(1)} all-to-all(bf16[16,8,2048]{2,1,0:T(8,128)(2,1)S(1)} %bitcast.25), channel_id=1, replica_groups=mesh['kv'=4,'seq'=16,'exp'=8] {'seq'}, dimensions={0} | all-to-all | bytes 1048576 | tf_op jit(solution)/shard_map/all_to_all | solution.py:305
  179.5 18.1 %all_to_all.33 = bf16[8,8,256]{2,1,0:T(8,128)(2,1)S(1)} all-to-all(bf16[8,8,256]{2,1,0:T(8,128)(2,1)S(1)} %bitcast.31), channel_id=1, replica_groups=mesh['kv'=4,'seq'=16,'exp'=8] {'exp'}, dimensions={0} | all-to-all | bytes 65536 | tf_op jit(solution)/shard_map/all_to_all | solution.py:308
  197.5 0.6 copy.24
  (23 shorter events, 0.7 us)
Async XLA Ops:
  6.5 1.4 copy-start.2
  6.5 1.4 copy-start.3
  6.5 105.9 %all-gather.4.cloned.1.call-start = ((), (), s32[]{:S(2)}) async-start(), calls=%async_computation.6 | async-start | bytes 14155776 | tf_op jit(solution)/shard_map/all_gather | solution.py:282
  7.9 2.0 copy-start.8
  11.2 30.4 %copy-start.6 = (bf16[2048]{0:T(1024)(128)(2,1)S(1)}, bf16[2048]{0:T(1024)(128)(2,1)}, u32[]{:S(2)}) copy-start(bf16[2048]{0:T(1024)(128)(2,1)} %param.21) | copy-start | bytes 12292
  11.2 31.1 %copy-start.4 = (bf16[2048,64]{0,1:T(8,128)(2,1)S(1)}, bf16[2048,64]{0,1:T(8,128)(2,1)}, u32[]{:S(2)}) copy-start(bf16[2048,64]{0,1:T(8,128)(2,1)} %param.23) | copy-start | bytes 786436
  16.7 26.5 %copy-start.7 = (s32[1,64,8]{1,2,0:T(8,128)S(1)}, s32[1,64,8]{1,2,0:T(8,128)}, u32[]{:S(2)}) copy-start(s32[1,64,8]{1,2,0:T(8,128)} %param.24) | copy-start | bytes 6148
  37.9 13.4 %all-to-all-start.1 = ((bf16[8,8,2048]{2,1,0:T(8,128)(2,1)}), bf16[8,8,2048]{2,1,0:T(8,128)(2,1)S(1)}, u32[]{:S(2)}, u32[]{:S(2)}) async-start(bf16[8,8,2048]{2,1,0:T(8,128)(2,1)} %bitcast.27), calls=%async_computation.1 | async-start | bytes 524288 | tf_op jit(solution)/shard_map/all_to_all | solution.py:294
  51.4 0.7 copy-start.1
  85.8 26.6 %all-to-all-start.2 = ((bf16[4,128,2176]{2,1,0:T(8,128)(2,1)}), bf16[4,128,2176]{2,1,0:T(8,128)(2,1)S(1)}, u32[]{:S(2)}, u32[]{:S(2)}) async-start(bf16[4,128,2176]{2,1,0:T(8,128)(2,1)} %broadcast_in_dim.8), calls=%async_computation.2 | async-start | bytes 4456448 | tf_op jit(solution)/shard_map/all_to_all | solution.py:299
  112.4 1.4 copy-start
  154.8 24.6 %copy-start.5 = (f32[8,2048]{1,0:T(8,128)S(1)}, f32[8,2048]{1,0:T(8,128)}, u32[]{:S(2)}) copy-start(f32[8,2048]{1,0:T(8,128)} %get-tuple-element.7) | copy-start | bytes 196612
Sparse Core Ops, SparseCore 0:
  9.5 83.5 all-gather.3

commit v2 on v1

--- a/solution.py
+++ b/solution.py
@@ -1,3 +1,5 @@
+import functools
+
 import jax
 import jax.numpy as jnp
 from jax import lax
@@ -24,7 +26,8 @@
 
 NEG_FILL = -1e30
 EPS_NORM = 1e-06
-VMEM_LIMIT = 56 * 1024 * 1024
+VMEM_LIMIT = 16 * 1024 * 1024
+EXPERT_VMEM = 24 * 1024 * 1024
 
 
 def nt(a, b):
@@ -40,7 +43,7 @@
 
 
 def attention_kernel(
-    table, info, q_ref, parents_ref, draft_ref, pool_ref, out_ref, kbuf, vbuf, seen_ref, sems
+    table, lens, q_ref, parents_ref, draft_ref, pool_ref, out_ref, kbuf, vbuf, seen_ref, sems
 ):
     copies = []
     for page in range(PPD):
@@ -50,8 +53,8 @@
         copies.append(pltpu.make_async_copy(pool_ref.at[1, slot], vbuf.at[rows], sems.at[1, page]))
     for copy in copies:
         copy.start()
-    length = info[0]
-    my_set = info[1]
+    length = lens[0]
+    my_set = lax.axis_index("exp")
     pad = jnp.zeros((8, D), jnp.float32)
     kbuf[KEYS:ROWS, :] = jnp.concatenate([draft_ref[0, 0].astype(jnp.float32), pad], axis=0).astype(
         jnp.bfloat16
@@ -61,7 +64,8 @@
     )
     ancestor = lax.broadcasted_iota(jnp.int32, (DRAFT, 2 * DRAFT), 0)
     token = lax.broadcasted_iota(jnp.int32, (DRAFT, 2 * DRAFT), 1) % DRAFT
-    linked = jnp.where((parents_ref[...] == ancestor) | (ancestor == token), 1.0, 0.0)
+    parents = jnp.concatenate([parents_ref[...], parents_ref[...]], axis=1)
+    linked = jnp.where((parents == ancestor) | (ancestor == token), 1.0, 0.0)
     for doubling in range((DRAFT - 1).bit_length()):
         narrow = linked.astype(jnp.bfloat16)
         linked = jnp.minimum(nn(narrow[:, :DRAFT], narrow), 1.0)
@@ -104,7 +108,7 @@
         out_ref[pair, DRAFT:STAT, HD : 2 * HD] = jnp.zeros((8, HD), jnp.bfloat16)
 
 
-def attention(table, info, queries, parents, draft_kv, kv_pool):
+def attention(table, lens, queries, parents, draft_kv, kv_pool):
     vmem = pl.BlockSpec(memory_space=pltpu.VMEM)
     return pl.pallas_call(
         attention_kernel,
@@ -126,7 +130,7 @@
         ],
         compiler_params=pltpu.CompilerParams(vmem_limit_bytes=VMEM_LIMIT),
         name="attention",
-    )(table, info, queries, parents, draft_kv, kv_pool)
+    )(table, lens, queries, parents, draft_kv, kv_pool)
 
 
 def merge_kernel(parts_ref, proj_ref, out_ref):
@@ -202,53 +206,86 @@
     )(my_set, parts, hidden, norm_gain, router, routes)
 
 
-def expert_kernel(my_expert, rows_ref, in_ref, down_ref, out_ref, act_ref, gate_ref):
-    step = pl.program_id(0)
-
-    @pl.when(step == 0)
-    def _():
-        gates = rows_ref[:, D:WIDE].astype(jnp.float32)
-        lane = lax.broadcasted_iota(jnp.int32, gates.shape, 1) % EXPERTS
-        gate_ref[...] = jnp.sum(jnp.where(lane == my_expert[0], gates, 0.0), axis=1, keepdims=True)
-
-    @pl.when(step < SETS)
-    def _():
-        both = nn(rows_ref[:, 0:D], in_ref[0])
+def expert_rows(my_expert, rows_ref, weights_ref, out_ref, act_ref, before_block):
+    gates = rows_ref[:, D:WIDE].astype(jnp.float32)
+    lane = lax.broadcasted_iota(jnp.int32, gates.shape, 1) % EXPERTS
+    scale = jnp.sum(jnp.where(lane == my_expert, gates, 0.0), axis=1, keepdims=True)
+    for block in range(SETS):
+        before_block(block)
+        both = nn(rows_ref[:, 0:D], weights_ref[block, 0:D, :])
         gate, up = both[:, :BLK], both[:, BLK:]
         act = gate / (1.0 + jnp.exp(-gate)) * up
-        act_ref[:, pl.ds(pl.multiple_of(step * BLK, BLK), BLK)] = act.astype(jnp.bfloat16)
-
-    @pl.when(step >= SETS)
-    def _():
-        down = down_ref[...].reshape(FF, D // SETS)
-        out_ref[...] = (nn(act_ref[...], down) * gate_ref[...]).astype(jnp.bfloat16)
-
-
-def expert(my_expert, rows, weights):
+        act_ref[:, block * BLK : (block + 1) * BLK] = act.astype(jnp.bfloat16)
+    width = D // SETS
+    for block in range(SETS):
+        down = weights_ref[:, D + block * BLK : D + (block + 1) * BLK, :].reshape(FF, width)
+        out = nn(act_ref[...], down) * scale
+        out_ref[:, block * width : (block + 1) * width] = out.astype(jnp.bfloat16)
+
+
+def own_kernel(my_expert, rows_ref, weights_ref, out_ref, kept_ref, act_ref, sems):
+    copies = [
+        pltpu.make_async_copy(weights_ref.at[block], kept_ref.at[block], sems.at[block])
+        for block in range(SETS)
+    ]
+    for copy in copies:
+        copy.start()
+    expert_rows(
+        my_expert[0], rows_ref, kept_ref, out_ref, act_ref, lambda block: copies[block].wait()
+    )
+
+
+def other_kernel(count, my_expert, *refs):
+    rows_refs, weights_ref, out_refs, act_ref = (
+        refs[:count],
+        refs[count],
+        refs[count + 1 : 2 * count + 1],
+        refs[2 * count + 1],
+    )
+    for rows_ref, out_ref in zip(rows_refs, out_refs):
+        expert_rows(my_expert[0], rows_ref, weights_ref, out_ref, act_ref, lambda block: None)
+
+
+def own_expert(my_expert, rows, weights):
     count = rows.shape[0]
-    width = D // SETS
-    return pl.pallas_call(
-        expert_kernel,
-        out_shape=jax.ShapeDtypeStruct((count, D), jnp.bfloat16),
-        grid_spec=pltpu.PrefetchScalarGridSpec(
-            num_scalar_prefetch=1,
-            grid=(2 * SETS,),
-            in_specs=[
-                pl.BlockSpec((count, WIDE), lambda i, e: (0, 0)),
-                pl.BlockSpec((1, D, width), lambda i, e: (jnp.minimum(i, SETS - 1), 0, 0)),
-                pl.BlockSpec(
-                    (SETS, BLK, width), lambda i, e: (0, D // BLK + jnp.maximum(i - SETS, 0), 0)
-                ),
-            ],
-            out_specs=pl.BlockSpec((count, width), lambda i, e: (0, jnp.maximum(i - SETS, 0))),
-            scratch_shapes=[
-                pltpu.VMEM((count, FF), jnp.bfloat16),
-                pltpu.VMEM((count, 1), jnp.float32),
-            ],
+    vmem = pl.BlockSpec(memory_space=pltpu.VMEM)
+    return pl.pallas_call(
+        own_kernel,
+        out_shape=(
+            jax.ShapeDtypeStruct((count, D), jnp.bfloat16),
+            pltpu.VMEM(weights.shape, weights.dtype),
         ),
-        compiler_params=pltpu.CompilerParams(vmem_limit_bytes=VMEM_LIMIT),
-        name="expert",
-    )(my_expert, rows, weights, weights)
+        in_specs=[
+            pl.BlockSpec(memory_space=pltpu.SMEM),
+            vmem,
+            pl.BlockSpec(memory_space=pl.ANY),
+        ],
+        out_specs=(vmem, vmem),
+        scratch_shapes=[
+            pltpu.VMEM((count, FF), jnp.bfloat16),
+            pltpu.SemaphoreType.DMA((SETS,)),
+        ],
+        compiler_params=pltpu.CompilerParams(vmem_limit_bytes=EXPERT_VMEM),
+        name="own_expert",
+    )(my_expert, rows, pltpu.with_memory_space_constraint(weights, pltpu.HBM))
+
+
+def other_expert(my_expert, weights, *blocks):
+    rows = blocks[0].shape[0]
+    vmem = pl.BlockSpec(memory_space=pltpu.VMEM)
+    return pl.pallas_call(
+        functools.partial(other_kernel, len(blocks)),
+        out_shape=tuple(jax.ShapeDtypeStruct((rows, D), jnp.bfloat16) for block in blocks),
+        in_specs=[pl.BlockSpec(memory_space=pltpu.SMEM)] + [vmem] * (len(blocks) + 1),
+        out_specs=(vmem,) * len(blocks),
+        scratch_shapes=[pltpu.VMEM((rows, FF), jnp.bfloat16)],
+        compiler_params=pltpu.CompilerParams(vmem_limit_bytes=EXPERT_VMEM),
+        name="other_expert",
+    )(my_expert, *blocks, pltpu.with_memory_space_constraint(weights, pltpu.VMEM))
+
+
+def shifted(value, axis, count, by):
+    return lax.ppermute(value, axis, [(i, (i + by) % count) for i in range(count)])
 
 
 def local(
@@ -280,14 +317,8 @@
         axis=0,
     )
     weights = lax.all_gather(packed, "exp")
-    info = jnp.concatenate([cache_lens, my_set.reshape(1)])
     partials = attention(
-        page_table.reshape(PPD),
-        info,
-        queries,
-        jnp.concatenate([parents, parents], axis=1),
-        draft_kv,
-        kv_pool,
+        page_table.reshape(PPD), cache_lens, queries, parents, draft_kv, kv_pool
     )
     parts = lax.all_to_all(partials, "exp", 0, 0, tiled=True)
     projected = merge(parts, out_proj)
@@ -295,16 +326,25 @@
     residual, row = norm(
         my_set.reshape(1), shares, hidden, norm_gain.reshape(1, D), router, routes
     )
-    along_seq = lax.all_gather(row, "seq").reshape(1, seq_count * TOK, WIDE)
-    rows = lax.all_to_all(
-        jnp.broadcast_to(along_seq, (kv_count, seq_count * TOK, WIDE)), "kv", 0, 0, tiled=True
-    ).reshape(kv_count * seq_count * TOK, WIDE)
-    finished = expert(my_expert.reshape(1), rows, weights)
-    back = lax.all_to_all(finished.reshape(kv_count, seq_count * TOK, D), "kv", 0, 0, tiled=True)
-    back = jnp.sum(back.astype(jnp.float32), axis=0).astype(jnp.bfloat16)
-    back = lax.all_to_all(back.reshape(seq_count, TOK, D), "seq", 0, 0, tiled=True)
-    total = (residual + jnp.sum(back.astype(jnp.float32), axis=0)).astype(jnp.bfloat16)
-    columns = jnp.transpose(total.reshape(TOK, SETS, width), (1, 0, 2))
+    rows = lax.all_gather(row, "seq").reshape(seq_count * TOK, WIDE)
+    ident = my_expert.reshape(1)
+    arrived = {by: shifted(rows, "kv", kv_count, by) for by in range(1, kv_count)}
+    total, kept = own_expert(ident, rows, weights)
+    near = other_expert(ident, kept, arrived[1], arrived[kv_count - 1])
+    returned = [
+        shifted(near[0], "kv", kv_count, -1),
+        shifted(near[1], "kv", kv_count, 1),
+    ]
+    for by in range(2, kv_count - 1):
+        (far,) = other_expert(ident, kept, arrived[by])
+        returned.append(shifted(far, "kv", kv_count, -by))
+    total = total.astype(jnp.float32)
+    for part in returned:
+        total = total + part.astype(jnp.float32)
+    back = total.astype(jnp.bfloat16).reshape(seq_count, TOK, D)
+    back = lax.all_to_all(back, "seq", 0, 0, tiled=True)
+    output = (residual + jnp.sum(back.astype(jnp.float32), axis=0)).astype(jnp.bfloat16)
+    columns = jnp.transpose(output.reshape(TOK, SETS, width), (1, 0, 2))
     return lax.all_to_all(columns, "exp", 0, 0, tiled=True).reshape(1, DRAFT, width)
 
 

time: 206 us -> 191 us (0.927)
  starting transfers between devices: 7.7 us -> 23.7 us
  blocking collectives: 114 us -> 104 us
  Pallas kernels: 27.8 us -> 18.6 us
  waiting for transfers between devices: 30 us -> 24.2 us
  local copies, waits for them, and re-layouts: 7.97 us -> 2.29 us
    all_to_all x1 -> x0, waiting for transfers between devices: 22.6 us -> none  [local(): lax.all_to_all(jnp.broadcast_to(along_seq, (kv_count, seq_count * TOK, WI...]
    ppermute x0 -> x6, starting transfers between devices: none -> 19.8 us  [shifted(): lax.ppermute(value, axis, [(i, (i + by) % count) for i in range(count)])]
    all_to_all x2 -> x1, blocking collectives: 48 us -> 30.6 us  [local(): back = lax.all_to_all(back, 'seq', 0, 0, tiled=True)]
    ppermute x0 -> x6, waiting for transfers between devices: none -> 10.8 us  [shifted(): lax.ppermute(value, axis, [(i, (i + by) % count) for i in range(count)])]
    all_to_all x1, blocking collectives: 18.1 us -> 25.6 us  [local(): lax.all_to_all(columns, 'exp', 0, 0, tiled=True).reshape(1, DRAFT, width)]
    pallas_call x1 -> x3, Pallas kernels: 17.1 us -> 11 us  [the longest x1 5.68 us: own_expert(): pl.pallas_call(own_kernel, out_shape=(jax.ShapeDtypeStruct((count, D), jn...]
    all_to_all x1 -> x0, starting transfers between devices: 4.03 us -> none  [local(): lax.all_to_all(jnp.broadcast_to(along_seq, (kv_count, seq_count * TOK, WI...]
    all_gather x1, waiting for transfers between devices: 0.01 us -> 4.03 us  [local(): weights = lax.all_gather(packed, 'exp')]
  transfers between devices with their start and end apart: 3 -> 8, of which waited for: 2 -> 5; matrix products, arithmetic and copies ran while one was open for 2% -> 0% of each run, Pallas kernels for 5% -> 10%
where the time goes in v2:
time: 191 us; the launch traced here: 190 us
  blocking collectives  104 us (54%)
  waiting for transfers between devices  24.2 us (13%)
  starting transfers between devices  23.7 us (12%)
  Pallas kernels  18.6 us (10%)
  between operations  14.4 us (8%)
  other arithmetic  3.09 us (2%)
  local copies, waits for them, and re-layouts  2.29 us (1%)
    all_gather x1, blocking collectives, local(): rows = lax.all_gather(row, 'seq').reshape(seq_count * TOK, WIDE)  31.2 us
    all_to_all x1, blocking collectives, local(): back = lax.all_to_all(back, 'seq', 0, 0, tiled=True)  30.6 us
    all_to_all x1, blocking collectives, local(): lax.all_to_all(columns, 'exp', 0, 0, tiled=True).reshape(1, DRAFT, width)  25.6 us
    ppermute x6, starting transfers between devices, shifted(): lax.ppermute(value, axis, [(i, (i + by) % count) for i in range(count)])  19.8 us
    all_to_all x1, blocking collectives, local(): parts = lax.all_to_all(partials, 'exp', 0, 0, tiled=True)  16.6 us
    ppermute x6, waiting for transfers between devices, shifted(): lax.ppermute(value, axis, [(i, (i + by) % count) for i in range(count)])  10.8 us
    all_to_all x1, waiting for transfers between devices, local(): lax.all_to_all(projected.reshape(SETS, TOK, D), 'exp', 0, 0, tiled=True)  9.38 us
    pallas_call x1, Pallas kernels, attention(): pl.pallas_call(attention_kernel, out_shape=jax.ShapeDtypeStruct((SETS, ST...  5.87 us
  transfers between devices with their start and end apart: 8, of which 5 were waited for; matrix products, arithmetic and copies ran while one was open for 0% of the time, Pallas kernels for 10%

profile of v2, /device:TPU:1, one launch (start us, length us, event | category | flops | bytes accessed | tf_op | source)
XLA Modules:
  0.0 190.1 jit_solution(2223793430861187701)
XLA Ops:
  6.5 1.1 copy.18
  7.9 2.7 %pad_maximum_fusion = bf16[3072,256]{1,0:T(8,128)(2,1)} fusion(bf16[1024,256]{1,0:T(8,128)(2,1)S(1)} %bitcast.22, bf16[2048,128]{1,0:T(8,128)(2,1)} %bitcast.24, bf16[2048,128]{1,0:T(8,128)(2,1)} %bitcast.25), kind=kLoop, calls=%fused_computation | loop fusion | flops 4718592 | bytes 3145728 | tf_op jit(solution)/shard_map/concatenate | solution.py:312
  11.4 5.9 %attention.1 = bf16[8,72,256]{2,1,0:T(8,128)(2,1)S(1)} custom-call(s32[12]{0:T(128)S(1)} %bitcast.19, s32[1]{0:T(128)S(6)} %copy.20.lens, bf16[1,64,2048]{2,1,0:T(8,128)(2,1)S(1)} %copy-done.2, s32[1,64]{1,0:T(1,128)S(1)} %copy-done.6, bf16[2,1,8,2048]{3,2,1,0:T(8,128)(2,1)S(1)} %copy-done.4, bf16[2,12,16,2048]{3,2,1,0:T(8,128)(2,1)S(1)} %copy-done), custom_call_target="tpu_custom_call" | custom-call | tf_op jit(solution)/shard_map/attention/pallas_call | solution.py:113
  17.2 16.6 %all_to_all.20.parts_ref = bf16[8,72,256]{2,1,0:T(8,128)(2,1)S(1)} all-to-all(bf16[8,72,256]{2,1,0:T(8,128)(2,1)S(1)} %attention.1), channel_id=1, replica_groups=mesh['kv'=4,'seq'=16,'exp'=8] {'exp'}, dimensions={0} | all-to-all | bytes 589824 | tf_op jit(solution)/shard_map/all_to_all | solution.py:323
  33.8 1.3 merge.1
  35.1 3.9 %all-to-all-start.1 = ((bf16[8,8,2048]{2,1,0:T(8,128)(2,1)}), bf16[8,8,2048]{2,1,0:T(8,128)(2,1)S(1)}, u32[]{:S(2)}, u32[]{:S(2)}) async-start(bf16[8,8,2048]{2,1,0:T(8,128)(2,1)} %bitcast.2), calls=%async_computation.1 | async-start | bytes 524288 | tf_op jit(solution)/shard_map/all_to_all | solution.py:325
  39.4 9.4 %all-to-all-done.1.parts_ref = bf16[8,8,2048]{2,1,0:T(8,128)(2,1)S(1)} async-done(((bf16[8,8,2048]{2,1,0:T(8,128)(2,1)}), bf16[8,8,2048]{2,1,0:T(8,128)(2,1)S(1)}, u32[]{:S(2)}, u32[]{:S(2)}) %all-to-all-start.1) | async-done | bytes 262176 | tf_op jit(solution)/shard_map/all_to_all | solution.py:325
  49.2 31.2 %all-gather.rows_ref = bf16[128,2176]{1,0:T(8,128)(2,1)S(1)} all-gather(bf16[8,2176]{1,0:T(8,128)(2,1)S(1)} %get-tuple-element.12), channel_id=2, replica_groups=mesh['kv'=4,'seq'=16,'exp'=8] {'seq'}, dimensions={0}, use_global_device_ids=true | all-gather | bytes 591872 | tf_op jit(solution)/shard_map/all_gather | solution.py:329
  80.3 3.1 %collective-permute-start = (bf16[128,2176]{1,0:T(8,128)(2,1)S(1)}, bf16[128,2176]{1,0:T(8,128)(2,1)S(1)}, u32[]{:S(2)}, u32[]{:S(2)}) collective-permute-start(bf16[128,2176]{1,0:T(8,128)(2,1)S(1)} %all-gather.rows_ref), channel_id=1, source_target_pairs={{0,128},{128,256},{256,384},{384,0},{1,129},{129,257},{257,385},{3... | collective-permute-start | bytes 1671176 | tf_op jit(solution)/shard_map/ppermute | solution.py:288
  83.5 3.4 %collective-permute-start.1 = (bf16[128,2176]{1,0:T(8,128)(2,1)S(1)}, bf16[128,2176]{1,0:T(8,128)(2,1)S(1)}, u32[]{:S(2)}, u32[]{:S(2)}) collective-permute-start(bf16[128,2176]{1,0:T(8,128)(2,1)S(1)} %all-gather.rows_ref), channel_id=1, source_target_pairs={{0,384},{128,0},{256,128},{384,256},{1,385},{129,1},{257,129},{385... | collective-permute-start | bytes 1671176 | tf_op jit(solution)/shard_map/ppermute | solution.py:288
  86.8 3.4 %collective-permute-start.4 = (bf16[128,2176]{1,0:T(8,128)(2,1)S(1)}, bf16[128,2176]{1,0:T(8,128)(2,1)S(1)}, u32[]{:S(2)}, u32[]{:S(2)}) collective-permute-start(bf16[128,2176]{1,0:T(8,128)(2,1)S(1)} %all-gather.rows_ref), channel_id=1, source_target_pairs={{0,256},{128,384},{256,0},{384,128},{1,257},{129,385},{257,1},{385... | collective-permute-start | bytes 1671176 | tf_op jit(solution)/shard_map/ppermute | solution.py:288
  90.3 4.0 %all-gather.4.cloned.1.call-done = bf16[24576,256]{1,0:T(8,128)(2,1)} async-done(((bf16[3072,256]{1,0:T(8,128)(2,1)}), bf16[24576,256]{1,0:T(8,128)(2,1)}) %all-gather.4.cloned.1.call-update) | async-done | bytes 12582928 | tf_op jit(solution)/shard_map/all_gather | solution.py:319
  94.3 5.7 %own_expert.1 = (bf16[128,2048]{1,0:T(8,128)(2,1)S(1)}, bf16[8,3072,256]{2,1,0:T(8,128)(2,1)S(1)}) custom-call(s32[1]{0:T(128)} %bitcast.3.my_expert, bf16[128,2176]{1,0:T(8,128)(2,1)S(1)} %all-gather.rows_ref, bf16[8,3072,256]{2,1,0:T(8,128)(2,1)} %bitcast.20), custom_call_target="tpu_custom_call" | custom-call | tf_op jit(solution)/shard_map/own_expert/pallas_call | solution.py:252
  100.0 3.5 %other_expert.2 = (bf16[128,2048]{1,0:T(8,128)(2,1)S(1)}, bf16[128,2048]{1,0:T(8,128)(2,1)S(1)}) custom-call(s32[1]{0:T(128)} %bitcast.3.my_expert, bf16[128,2176]{1,0:T(8,128)(2,1)S(1)} %collective-permute-done.refs_0_, bf16[128,2176]{1,0:T(8,128)(2,1)S(1)} %collective-permute-done.1.refs_1_, bf16[8,3072,256]{2,1,0:T(8,128)(2,1)S(1)} %get-tuple-element.14.refs_2_.refs_1_), custom_call_target="tpu_custom_call" | custom-call | tf_op jit(solution)/shard_map/other_expert/pallas_call | solution.py:276
  103.5 4.3 %collective-permute-start.2 = (bf16[128,2048]{1,0:T(8,128)(2,1)S(1)}, bf16[128,2048]{1,0:T(8,128)(2,1)S(1)}, u32[]{:S(2)}, u32[]{:S(2)}) collective-permute-start(bf16[128,2048]{1,0:T(8,128)(2,1)S(1)} %get-tuple-element.15), channel_id=1, source_target_pairs={{0,384},{128,0},{256,128},{384,256},{1,385},{129,1},{257,129},{385... | collective-permute-start | bytes 1572872 | tf_op jit(solution)/shard_map/ppermute | solution.py:288
  107.8 1.9 %collective-permute-start.3 = (bf16[128,2048]{1,0:T(8,128)(2,1)S(1)}, bf16[128,2048]{1,0:T(8,128)(2,1)S(1)}, u32[]{:S(2)}, u32[]{:S(2)}) collective-permute-start(bf16[128,2048]{1,0:T(8,128)(2,1)S(1)} %get-tuple-element.16), channel_id=1, source_target_pairs={{0,128},{128,256},{256,384},{384,0},{1,129},{129,257},{257,385},{3... | collective-permute-start | bytes 1572872 | tf_op jit(solution)/shard_map/ppermute | solution.py:288
  109.8 1.8 other_expert.3
  111.6 3.6 %collective-permute-start.5 = (bf16[128,2048]{1,0:T(8,128)(2,1)S(1)}, bf16[128,2048]{1,0:T(8,128)(2,1)S(1)}, u32[]{:S(2)}, u32[]{:S(2)}) collective-permute-start(bf16[128,2048]{1,0:T(8,128)(2,1)S(1)} %other_expert.3), channel_id=1, source_target_pairs={{0,256},{128,384},{256,0},{384,128},{1,257},{129,385},{257,1},{385... | collective-permute-start | bytes 1572872 | tf_op jit(solution)/shard_map/ppermute | solution.py:288
  115.3 4.1 %collective-permute-done.2 = bf16[128,2048]{1,0:T(8,128)(2,1)S(1)} collective-permute-done((bf16[128,2048]{1,0:T(8,128)(2,1)S(1)}, bf16[128,2048]{1,0:T(8,128)(2,1)S(1)}, u32[]{:S(2)}, u32[]{:S(2)}) %collective-permute-start.2) | collective-permute-done | bytes 524320 | tf_op jit(solution)/shard_map/ppermute | solution.py:288
  119.4 3.7 %collective-permute-done.3 = bf16[128,2048]{1,0:T(8,128)(2,1)S(1)} collective-permute-done((bf16[128,2048]{1,0:T(8,128)(2,1)S(1)}, bf16[128,2048]{1,0:T(8,128)(2,1)S(1)}, u32[]{:S(2)}, u32[]{:S(2)}) %collective-permute-start.3) | collective-permute-done | bytes 524320 | tf_op jit(solution)/shard_map/ppermute | solution.py:288
  123.2 2.9 %collective-permute-done.5 = bf16[128,2048]{1,0:T(8,128)(2,1)S(1)} collective-permute-done((bf16[128,2048]{1,0:T(8,128)(2,1)S(1)}, bf16[128,2048]{1,0:T(8,128)(2,1)S(1)}, u32[]{:S(2)}, u32[]{:S(2)}) %collective-permute-start.5) | collective-permute-done | bytes 524320 | tf_op jit(solution)/shard_map/ppermute | solution.py:288
  126.4 30.6 %all_to_all.21 = bf16[16,8,2048]{2,1,0:T(8,128)(2,1)S(1)} all-to-all(bf16[16,8,2048]{2,1,0:T(8,128)(2,1)S(1)} %fusion), channel_id=1, replica_groups=mesh['kv'=4,'seq'=16,'exp'=8] {'seq'}, dimensions={0} | all-to-all | bytes 1048576 | tf_op jit(solution)/shard_map/all_to_all | solution.py:345
  157.1 25.6 %all_to_all.22 = bf16[8,8,256]{2,1,0:T(8,128)(2,1)S(1)} all-to-all(bf16[8,8,256]{2,1,0:T(8,128)(2,1)S(1)} %bitcast.26), channel_id=1, replica_groups=mesh['kv'=4,'seq'=16,'exp'=8] {'exp'}, dimensions={0} | all-to-all | bytes 65536 | tf_op jit(solution)/shard_map/all_to_all | solution.py:348
  182.7 0.6 copy.21
  (33 shorter events, 1.3 us)
Async XLA Ops:
  6.5 87.8 %all-gather.4.cloned.1.call-start = ((), (), s32[]{:S(2)}) async-start(), calls=%async_computation.4 | async-start | bytes 14155776 | tf_op jit(solution)/shard_map/all_gather | solution.py:319
  7.7 3.6 %copy-start = (bf16[2,12,16,2048]{3,2,1,0:T(8,128)(2,1)S(1)}, bf16[2,12,16,2048]{3,2,1,0:T(8,128)(2,1)}, u32[]{:S(2)}) copy-start(bf16[2,12,16,2048]{3,2,1,0:T(8,128)(2,1)} %pool_ref.1) | copy-start | bytes 4718596
  7.7 3.6 %copy-start.2 = (bf16[1,64,2048]{2,1,0:T(8,128)(2,1)S(1)}, bf16[1,64,2048]{2,1,0:T(8,128)(2,1)}, u32[]{:S(2)}) copy-start(bf16[1,64,2048]{2,1,0:T(8,128)(2,1)} %q_ref.1) | copy-start | bytes 786436
  7.7 3.6 %copy-start.4 = (bf16[2,1,8,2048]{3,2,1,0:T(8,128)(2,1)S(1)}, bf16[2,1,8,2048]{3,2,1,0:T(8,128)(2,1)}, u32[]{:S(2)}) copy-start(bf16[2,1,8,2048]{3,2,1,0:T(8,128)(2,1)} %draft_ref.1) | copy-start | bytes 196612
  7.7 3.6 %copy-start.5 = (s32[1,12,1]{1,2,0:T(1,128)S(1)}, s32[1,12,1]{1,2,0:T(1,128)}, u32[]{:S(2)}) copy-start(s32[1,12,1]{1,2,0:T(1,128)} %param.17) | copy-start | bytes 148
  7.7 3.6 %copy-start.6 = (s32[1,64]{1,0:T(1,128)S(1)}, s32[1,64]{1,0:T(1,128)}, u32[]{:S(2)}) copy-start(s32[1,64]{1,0:T(1,128)} %parents_ref.1) | copy-start | bytes 772
  7.9 25.9 %copy-start.1 = (bf16[256,2048]{1,0:T(8,128)(2,1)S(1)}, bf16[256,2048]{1,0:T(8,128)(2,1)}, u32[]{:S(2)}) copy-start(bf16[256,2048]{1,0:T(8,128)(2,1)} %proj_ref.1) | copy-start | bytes 3145732
  10.6 28.5 %copy-start.7 = (bf16[2048,64]{0,1:T(8,128)(2,1)S(1)}, bf16[2048,64]{0,1:T(8,128)(2,1)}, u32[]{:S(2)}) copy-start(bf16[2048,64]{0,1:T(8,128)(2,1)} %param.23) | copy-start | bytes 786436
  10.6 28.7 %copy-start.8 = (s32[1,64,8]{1,2,0:T(8,128)S(1)}, s32[1,64,8]{1,2,0:T(8,128)}, u32[]{:S(2)}) copy-start(s32[1,64,8]{1,2,0:T(8,128)} %param.24) | copy-start | bytes 6148
  10.6 28.8 %copy-start.9 = (bf16[2048]{0:T(1024)(128)(2,1)S(1)}, bf16[2048]{0:T(1024)(128)(2,1)}, u32[]{:S(2)}) copy-start(bf16[2048]{0:T(1024)(128)(2,1)} %param.21) | copy-start | bytes 12292
  10.6 38.2 %copy-start.3 = (bf16[1,64,2048]{2,1,0:T(8,128)(2,1)S(1)}, bf16[1,64,2048]{2,1,0:T(8,128)(2,1)}, u32[]{:S(2)}) copy-start(bf16[1,64,2048]{2,1,0:T(8,128)(2,1)} %hidden_ref.1) | copy-start | bytes 786436
  35.1 13.7 %all-to-all-start.1 = ((bf16[8,8,2048]{2,1,0:T(8,128)(2,1)}), bf16[8,8,2048]{2,1,0:T(8,128)(2,1)S(1)}, u32[]{:S(2)}, u32[]{:S(2)}) async-start(bf16[8,8,2048]{2,1,0:T(8,128)(2,1)} %bitcast.2), calls=%async_computation.1 | async-start | bytes 524288 | tf_op jit(solution)/shard_map/all_to_all | solution.py:325
  80.3 19.7 %collective-permute-start = (bf16[128,2176]{1,0:T(8,128)(2,1)S(1)}, bf16[128,2176]{1,0:T(8,128)(2,1)S(1)}, u32[]{:S(2)}, u32[]{:S(2)}) collective-permute-start(bf16[128,2176]{1,0:T(8,128)(2,1)S(1)} %all-gather.rows_ref), channel_id=1, source_target_pairs={{0,128},{128,256},{256,384},{384,0},{1,129},{129,257},{257,385},{3... | collective-permute-start | bytes 1671176 | tf_op jit(solution)/shard_map/ppermute | solution.py:288
  83.5 16.6 %collective-permute-start.1 = (bf16[128,2176]{1,0:T(8,128)(2,1)S(1)}, bf16[128,2176]{1,0:T(8,128)(2,1)S(1)}, u32[]{:S(2)}, u32[]{:S(2)}) collective-permute-start(bf16[128,2176]{1,0:T(8,128)(2,1)S(1)} %all-gather.rows_ref), channel_id=1, source_target_pairs={{0,384},{128,0},{256,128},{384,256},{1,385},{129,1},{257,129},{385... | collective-permute-start | bytes 1671176 | tf_op jit(solution)/shard_map/ppermute | solution.py:288
  86.8 22.9 %collective-permute-start.4 = (bf16[128,2176]{1,0:T(8,128)(2,1)S(1)}, bf16[128,2176]{1,0:T(8,128)(2,1)S(1)}, u32[]{:S(2)}, u32[]{:S(2)}) collective-permute-start(bf16[128,2176]{1,0:T(8,128)(2,1)S(1)} %all-gather.rows_ref), channel_id=1, source_target_pairs={{0,256},{128,384},{256,0},{384,128},{1,257},{129,385},{257,1},{385... | collective-permute-start | bytes 1671176 | tf_op jit(solution)/shard_map/ppermute | solution.py:288
  103.5 15.9 %collective-permute-start.2 = (bf16[128,2048]{1,0:T(8,128)(2,1)S(1)}, bf16[128,2048]{1,0:T(8,128)(2,1)S(1)}, u32[]{:S(2)}, u32[]{:S(2)}) collective-permute-start(bf16[128,2048]{1,0:T(8,128)(2,1)S(1)} %get-tuple-element.15), channel_id=1, source_target_pairs={{0,384},{128,0},{256,128},{384,256},{1,385},{129,1},{257,129},{385... | collective-permute-start | bytes 1572872 | tf_op jit(solution)/shard_map/ppermute | solution.py:288
  107.8 15.3 %collective-permute-start.3 = (bf16[128,2048]{1,0:T(8,128)(2,1)S(1)}, bf16[128,2048]{1,0:T(8,128)(2,1)S(1)}, u32[]{:S(2)}, u32[]{:S(2)}) collective-permute-start(bf16[128,2048]{1,0:T(8,128)(2,1)S(1)} %get-tuple-element.16), channel_id=1, source_target_pairs={{0,128},{128,256},{256,384},{384,0},{1,129},{129,257},{257,385},{3... | collective-permute-start | bytes 1572872 | tf_op jit(solution)/shard_map/ppermute | solution.py:288
  111.6 14.4 %collective-permute-start.5 = (bf16[128,2048]{1,0:T(8,128)(2,1)S(1)}, bf16[128,2048]{1,0:T(8,128)(2,1)S(1)}, u32[]{:S(2)}, u32[]{:S(2)}) collective-permute-start(bf16[128,2048]{1,0:T(8,128)(2,1)S(1)} %other_expert.3), channel_id=1, source_target_pairs={{0,256},{128,384},{256,0},{384,128},{1,257},{129,385},{257,1},{385... | collective-permute-start | bytes 1572872 | tf_op jit(solution)/shard_map/ppermute | solution.py:288
Sparse Core Ops, SparseCore 0:
  10.7 83.5 all-gather.3

commit v3 on v2

--- a/solution.py
+++ b/solution.py
@@ -206,7 +206,76 @@
     )(my_set, parts, hidden, norm_gain, router, routes)
 
 
-def expert_rows(my_expert, rows_ref, weights_ref, out_ref, act_ref, before_block):
+def pack_kernel(gate_ref, up_ref, down_ref, out_ref, buf, in_sems, out_sems):
+    width = D // SETS
+    pieces = []
+    part = D // 4
+    for piece in range(4):
+        rows = pl.ds(piece * part, part)
+        pieces.append(
+            (
+                [
+                    (gate_ref.at[0, rows], buf.at[rows, pl.ds(0, BLK)]),
+                    (up_ref.at[0, rows], buf.at[rows, pl.ds(BLK, BLK)]),
+                ],
+                rows,
+            )
+        )
+    for half in range(2):
+        blocks = range(half * SETS // 2, (half + 1) * SETS // 2)
+        pieces.append(
+            (
+                [
+                    (
+                        down_ref.at[0, :, pl.ds(block * width, width)],
+                        buf.at[pl.ds(D + block * BLK, BLK)],
+                    )
+                    for block in blocks
+                ],
+                pl.ds(D + half * FF // 2, FF // 2),
+            )
+        )
+    loads = []
+    count = 0
+    for moves, rows in pieces:
+        group = []
+        for source, target in moves:
+            group.append(pltpu.make_async_copy(source, target, in_sems.at[count]))
+            count += 1
+        loads.append((group, rows))
+    for group, rows in loads:
+        for copy in group:
+            copy.start()
+    stores = []
+    for index, (group, rows) in enumerate(loads):
+        for copy in group:
+            copy.wait()
+        store = pltpu.make_async_copy(buf.at[rows], out_ref.at[rows], out_sems.at[index])
+        store.start()
+        stores.append(store)
+    for store in stores:
+        store.wait()
+
+
+def pack(gate_w, up_w, down_w):
+    hbm = pl.BlockSpec(memory_space=pltpu.HBM)
+    width = D // SETS
+    return pl.pallas_call(
+        pack_kernel,
+        out_shape=jax.ShapeDtypeStruct((D + FF, width), gate_w.dtype),
+        in_specs=[hbm] * 3,
+        out_specs=hbm,
+        scratch_shapes=[
+            pltpu.VMEM((D + FF, width), jnp.bfloat16),
+            pltpu.SemaphoreType.DMA((16,)),
+            pltpu.SemaphoreType.DMA((6,)),
+        ],
+        compiler_params=pltpu.CompilerParams(vmem_limit_bytes=VMEM_LIMIT),
+        name="pack",
+    )(*(pltpu.with_memory_space_constraint(x, pltpu.HBM) for x in (gate_w, up_w, down_w)))
+
+
+def expert_rows(my_expert, rows_ref, weights_ref, store, act_ref, before_block):
     gates = rows_ref[:, D:WIDE].astype(jnp.float32)
     lane = lax.broadcasted_iota(jnp.int32, gates.shape, 1) % EXPERTS
     scale = jnp.sum(jnp.where(lane == my_expert, gates, 0.0), axis=1, keepdims=True)
@@ -219,44 +288,61 @@
     width = D // SETS
     for block in range(SETS):
         down = weights_ref[:, D + block * BLK : D + (block + 1) * BLK, :].reshape(FF, width)
-        out = nn(act_ref[...], down) * scale
-        out_ref[:, block * width : (block + 1) * width] = out.astype(jnp.bfloat16)
-
-
-def own_kernel(my_expert, rows_ref, weights_ref, out_ref, kept_ref, act_ref, sems):
+        store(block, (nn(act_ref[...], down) * scale).astype(jnp.bfloat16))
+
+
+def own_kernel(place, rows_ref, residual_ref, weights_ref, out_ref, kept_ref, act_ref, sems):
     copies = [
         pltpu.make_async_copy(weights_ref.at[block], kept_ref.at[block], sems.at[block])
         for block in range(SETS)
     ]
     for copy in copies:
         copy.start()
+    width = D // SETS
+    mine = pl.ds(pl.multiple_of(place[2] * TOK, TOK), TOK)
+
+    def store(block, value):
+        out_ref[block] = value
+
     expert_rows(
-        my_expert[0], rows_ref, kept_ref, out_ref, act_ref, lambda block: copies[block].wait()
-    )
-
-
-def other_kernel(count, my_expert, *refs):
-    rows_refs, weights_ref, out_refs, act_ref = (
+        place[0], rows_ref, kept_ref, store, act_ref, lambda block: copies[block].wait()
+    )
+    for block in range(SETS):
+        own = out_ref[block, mine, :].astype(jnp.float32)
+        own = own + residual_ref[:, block * width : (block + 1) * width]
+        out_ref[block, mine, :] = own.astype(jnp.bfloat16)
+
+
+def other_kernel(count, place, *refs):
+    rows_refs, own_ref, weights_ref, out_ref, act_ref = (
         refs[:count],
         refs[count],
-        refs[count + 1 : 2 * count + 1],
-        refs[2 * count + 1],
-    )
-    for rows_ref, out_ref in zip(rows_refs, out_refs):
-        expert_rows(my_expert[0], rows_ref, weights_ref, out_ref, act_ref, lambda block: None)
-
-
-def own_expert(my_expert, rows, weights):
+        refs[count + 1],
+        refs[count + 2],
+        refs[count + 3],
+    )
+    out_ref[place[1]] = own_ref[...]
+    for by, rows_ref in enumerate(rows_refs, 1):
+        target = lax.rem(place[1] + (count + 1 - by), count + 1)
+
+        def store(block, value, target=target):
+            out_ref[target, block] = value
+
+        expert_rows(place[0], rows_ref, weights_ref, store, act_ref, lambda block: None)
+
+
+def own_expert(place, rows, residual, weights):
     count = rows.shape[0]
     vmem = pl.BlockSpec(memory_space=pltpu.VMEM)
     return pl.pallas_call(
         own_kernel,
         out_shape=(
-            jax.ShapeDtypeStruct((count, D), jnp.bfloat16),
+            pltpu.VMEM((SETS, count, D // SETS), jnp.bfloat16),
             pltpu.VMEM(weights.shape, weights.dtype),
         ),
         in_specs=[
             pl.BlockSpec(memory_space=pltpu.SMEM),
+            vmem,
             vmem,
             pl.BlockSpec(memory_space=pl.ANY),
         ],
@@ -267,21 +353,64 @@
         ],
         compiler_params=pltpu.CompilerParams(vmem_limit_bytes=EXPERT_VMEM),
         name="own_expert",
-    )(my_expert, rows, pltpu.with_memory_space_constraint(weights, pltpu.HBM))
-
-
-def other_expert(my_expert, weights, *blocks):
+    )(place, rows, residual, pltpu.with_memory_space_constraint(weights, pltpu.HBM))
+
+
+def other_expert(place, own, weights, blocks):
     rows = blocks[0].shape[0]
     vmem = pl.BlockSpec(memory_space=pltpu.VMEM)
+    held = [pltpu.with_memory_space_constraint(x, pltpu.VMEM) for x in (*blocks, own, weights)]
     return pl.pallas_call(
         functools.partial(other_kernel, len(blocks)),
-        out_shape=tuple(jax.ShapeDtypeStruct((rows, D), jnp.bfloat16) for block in blocks),
-        in_specs=[pl.BlockSpec(memory_space=pltpu.SMEM)] + [vmem] * (len(blocks) + 1),
-        out_specs=(vmem,) * len(blocks),
+        out_shape=jax.ShapeDtypeStruct((len(blocks) + 1, SETS, rows, D // SETS), jnp.bfloat16),
+        in_specs=[pl.BlockSpec(memory_space=pltpu.SMEM)] + [vmem] * len(held),
+        out_specs=vmem,
         scratch_shapes=[pltpu.VMEM((rows, FF), jnp.bfloat16)],
         compiler_params=pltpu.CompilerParams(vmem_limit_bytes=EXPERT_VMEM),
         name="other_expert",
-    )(my_expert, *blocks, pltpu.with_memory_space_constraint(weights, pltpu.VMEM))
+    )(place, *held)
+
+
+def fold_kernel(parts_ref, out_ref):
+    seq_count = out_ref.shape[0]
+    width = out_ref.shape[2]
+    for source in range(SETS):
+        total = parts_ref[source].astype(jnp.float32)
+        for block in range(1, parts_ref.shape[0] // SETS):
+            total = total + parts_ref[block * SETS + source].astype(jnp.float32)
+        total = total.astype(jnp.bfloat16).reshape(seq_count, TOK, width)
+        out_ref[:, source * TOK : (source + 1) * TOK, :] = total
+
+
+def fold(parts, seq_count):
+    vmem = pl.BlockSpec(memory_space=pltpu.VMEM)
+    return pl.pallas_call(
+        fold_kernel,
+        out_shape=pltpu.VMEM((seq_count, DRAFT, parts.shape[2]), parts.dtype),
+        in_specs=[vmem],
+        out_specs=vmem,
+        compiler_params=pltpu.CompilerParams(vmem_limit_bytes=VMEM_LIMIT),
+        name="fold",
+    )(pltpu.with_memory_space_constraint(parts, pltpu.VMEM))
+
+
+def total_kernel(parts_ref, out_ref):
+    total = parts_ref[0].astype(jnp.float32)
+    for source in range(1, parts_ref.shape[0]):
+        total = total + parts_ref[source].astype(jnp.float32)
+    out_ref[0] = total.astype(jnp.bfloat16)
+
+
+def total(parts):
+    vmem = pl.BlockSpec(memory_space=pltpu.VMEM)
+    return pl.pallas_call(
+        total_kernel,
+        out_shape=jax.ShapeDtypeStruct((1,) + parts.shape[1:], parts.dtype),
+        in_specs=[vmem],
+        out_specs=vmem,
+        compiler_params=pltpu.CompilerParams(vmem_limit_bytes=VMEM_LIMIT),
+        name="total",
+    )(pltpu.with_memory_space_constraint(parts, pltpu.VMEM))
 
 
 def shifted(value, axis, count, by):
@@ -305,18 +434,12 @@
     down_w,
 ):
     my_set = lax.axis_index("exp").astype(jnp.int32)
+    my_kv = lax.axis_index("kv").astype(jnp.int32)
+    my_seq = lax.axis_index("seq").astype(jnp.int32)
     kv_count = lax.axis_size("kv")
     seq_count = lax.axis_size("seq")
-    my_expert = (lax.axis_index("kv") * seq_count + lax.axis_index("seq")).astype(jnp.int32)
     width = D // SETS
-    packed = jnp.concatenate(
-        [
-            jnp.concatenate([gate_w[0], up_w[0]], axis=1),
-            jnp.transpose(down_w[0].reshape(BLK, SETS, width), (1, 0, 2)).reshape(SETS * BLK, width),
-        ],
-        axis=0,
-    )
-    weights = lax.all_gather(packed, "exp")
+    weights = lax.all_gather(pack(gate_w, up_w, down_w), "exp")
     partials = attention(
         page_table.reshape(PPD), cache_lens, queries, parents, draft_kv, kv_pool
     )
@@ -327,25 +450,14 @@
         my_set.reshape(1), shares, hidden, norm_gain.reshape(1, D), router, routes
     )
     rows = lax.all_gather(row, "seq").reshape(seq_count * TOK, WIDE)
-    ident = my_expert.reshape(1)
-    arrived = {by: shifted(rows, "kv", kv_count, by) for by in range(1, kv_count)}
-    total, kept = own_expert(ident, rows, weights)
-    near = other_expert(ident, kept, arrived[1], arrived[kv_count - 1])
-    returned = [
-        shifted(near[0], "kv", kv_count, -1),
-        shifted(near[1], "kv", kv_count, 1),
-    ]
-    for by in range(2, kv_count - 1):
-        (far,) = other_expert(ident, kept, arrived[by])
-        returned.append(shifted(far, "kv", kv_count, -by))
-    total = total.astype(jnp.float32)
-    for part in returned:
-        total = total + part.astype(jnp.float32)
-    back = total.astype(jnp.bfloat16).reshape(seq_count, TOK, D)
-    back = lax.all_to_all(back, "seq", 0, 0, tiled=True)
-    output = (residual + jnp.sum(back.astype(jnp.float32), axis=0)).astype(jnp.bfloat16)
-    columns = jnp.transpose(output.reshape(TOK, SETS, width), (1, 0, 2))
-    return lax.all_to_all(columns, "exp", 0, 0, tiled=True).reshape(1, DRAFT, width)
+    place = jnp.stack([my_kv * seq_count + my_seq, my_kv, my_seq])
+    arrived = [shifted(rows, "kv", kv_count, by) for by in range(1, kv_count)]
+    own, kept = own_expert(place, rows, residual, weights)
+    finished = other_expert(place, own, kept, arrived)
+    back = finished.reshape(kv_count * SETS, seq_count * TOK, width)
+    back = lax.all_to_all(back, ("kv", "exp"), 0, 0, tiled=True)
+    back = lax.all_to_all(fold(back, seq_count), "seq", 0, 0, tiled=True)
+    return total(back)
 
 
 def solution(mesh):

time: 191 us -> 194 us (1.016)
  the two profiles are of different devices: /device:TPU:1 before, /device:TPU:32 now
where the time goes in v3:
time: 194 us; the launch traced here: 193 us
  blocking collectives  121 us (62%)
  Pallas kernels  23.2 us (12%)
  waiting for transfers between devices  20 us (10%)
  starting transfers between devices  14.8 us (8%)
  between operations  14.3 us (7%)
    all_to_all x1, blocking collectives, local(): back = lax.all_to_all(fold(back, seq_count), 'seq', 0, 0, tiled=True)  38.5 us
    all_gather x1, blocking collectives, local(): rows = lax.all_gather(row, 'seq').reshape(seq_count * TOK, WIDE)  36.7 us
    all_to_all x1, blocking collectives, local(): back = lax.all_to_all(back, ('kv', 'exp'), 0, 0, tiled=True)  33 us
    all_to_all x1, blocking collectives, local(): parts = lax.all_to_all(partials, 'exp', 0, 0, tiled=True)  12.3 us
    ppermute x3, starting transfers between devices, shifted(): lax.ppermute(value, axis, [(i, (i + by) % count) for i in range(count)])  11.4 us
    all_to_all x1, waiting for transfers between devices, local(): lax.all_to_all(projected.reshape(SETS, TOK, D), 'exp', 0, 0, tiled=True)  10 us
    ppermute x3, waiting for transfers between devices, shifted(): lax.ppermute(value, axis, [(i, (i + by) % count) for i in range(count)])  9.97 us
    pallas_call x1, Pallas kernels, own_expert(): pl.pallas_call(own_kernel, out_shape=(pltpu.VMEM((SETS, count, D // SETS)...  6.26 us
  transfers between devices with their start and end apart: 5, of which 4 were waited for; matrix products, arithmetic and copies ran while one was open for 0% of the time, Pallas kernels for 7%

profile of v3, /device:TPU:32, one launch (start us, length us, event | category | flops | bytes accessed | tf_op | source)
XLA Modules:
  0.0 193.4 jit_solution(3119322129946835239)
XLA Ops:
  6.5 0.0 all-gather.4.cloned.1.call-start
  6.6 2.5 %pack.1 = bf16[3072,256]{1,0:T(8,128)(2,1)} custom-call(bf16[1,2048,128]{2,1,0:T(8,128)(2,1)} %gate_ref.1, bf16[1,2048,128]{2,1,0:T(8,128)(2,1)} %up_ref.1, bf16[1,128,2048]{2,1,0:T(8,128)(2,1)} %down_ref.1), custom_call_target="tpu_custom_call" | custom-call | tf_op jit(solution)/shard_map/pack/pallas_call | solution.py:263
  9.9 5.9 %attention.1 = bf16[8,72,256]{2,1,0:T(8,128)(2,1)S(1)} custom-call(s32[12]{0:T(128)S(1)} %bitcast.9, s32[1]{0:T(128)S(6)} %copy.17.lens, bf16[1,64,2048]{2,1,0:T(8,128)(2,1)S(1)} %copy-done.2, s32[1,64]{1,0:T(1,128)S(1)} %copy-done.6, bf16[2,1,8,2048]{3,2,1,0:T(8,128)(2,1)S(1)} %copy-done.4, bf16[2,12,16,2048]{3,2,1,0:T(8,128)(2,1)S(1)} %copy-done), custom_call_target="tpu_custom_call" | custom-call | tf_op jit(solution)/shard_map/attention/pallas_call | solution.py:113
  15.8 12.3 %all_to_all.20.parts_ref = bf16[8,72,256]{2,1,0:T(8,128)(2,1)S(1)} all-to-all(bf16[8,72,256]{2,1,0:T(8,128)(2,1)S(1)} %attention.1), channel_id=1, replica_groups=mesh['kv'=4,'seq'=16,'exp'=8] {'exp'}, dimensions={0} | all-to-all | bytes 589824 | tf_op jit(solution)/shard_map/all_to_all | solution.py:446
  28.1 1.3 merge.1
  29.5 3.4 %all-to-all-start.1 = ((bf16[8,8,2048]{2,1,0:T(8,128)(2,1)}), bf16[8,8,2048]{2,1,0:T(8,128)(2,1)S(1)}, u32[]{:S(2)}, u32[]{:S(2)}) async-start(bf16[8,8,2048]{2,1,0:T(8,128)(2,1)} %bitcast.5), calls=%async_computation.1 | async-start | bytes 524288 | tf_op jit(solution)/shard_map/all_to_all | solution.py:448
  32.9 0.3 copy.15.router_ref
  33.2 0.1 copy.16.routes_ref
  33.3 10.0 %all-to-all-done.1.parts_ref = bf16[8,8,2048]{2,1,0:T(8,128)(2,1)S(1)} async-done(((bf16[8,8,2048]{2,1,0:T(8,128)(2,1)}), bf16[8,8,2048]{2,1,0:T(8,128)(2,1)S(1)}, u32[]{:S(2)}, u32[]{:S(2)}) %all-to-all-start.1) | async-done | bytes 262176 | tf_op jit(solution)/shard_map/all_to_all | solution.py:448
  43.3 0.4 norm.1
  43.7 36.7 %all-gather.rows_ref = bf16[128,2176]{1,0:T(8,128)(2,1)S(1)} all-gather(bf16[8,2176]{1,0:T(8,128)(2,1)S(1)} %get-tuple-element.9), channel_id=2, replica_groups=mesh['kv'=4,'seq'=16,'exp'=8] {'seq'}, dimensions={0}, use_global_device_ids=true | all-gather | bytes 591872 | tf_op jit(solution)/shard_map/all_gather | solution.py:452
  80.4 3.4 %collective-permute-start = (bf16[128,2176]{1,0:T(8,128)(2,1)S(1)}, bf16[128,2176]{1,0:T(8,128)(2,1)S(1)}, u32[]{:S(2)}, u32[]{:S(2)}) collective-permute-start(bf16[128,2176]{1,0:T(8,128)(2,1)S(1)} %all-gather.rows_ref), channel_id=1, source_target_pairs={{0,128},{128,256},{256,384},{384,0},{1,129},{129,257},{257,385},{3... | collective-permute-start | bytes 1671176 | tf_op jit(solution)/shard_map/ppermute | solution.py:417
  83.8 4.6 %collective-permute-start.1 = (bf16[128,2176]{1,0:T(8,128)(2,1)S(1)}, bf16[128,2176]{1,0:T(8,128)(2,1)S(1)}, u32[]{:S(2)}, u32[]{:S(2)}) collective-permute-start(bf16[128,2176]{1,0:T(8,128)(2,1)S(1)} %all-gather.rows_ref), channel_id=1, source_target_pairs={{0,256},{128,384},{256,0},{384,128},{1,257},{129,385},{257,1},{385... | collective-permute-start | bytes 1671176 | tf_op jit(solution)/shard_map/ppermute | solution.py:417
  88.5 3.3 %collective-permute-start.2 = (bf16[128,2176]{1,0:T(8,128)(2,1)S(1)}, bf16[128,2176]{1,0:T(8,128)(2,1)S(1)}, u32[]{:S(2)}, u32[]{:S(2)}) collective-permute-start(bf16[128,2176]{1,0:T(8,128)(2,1)S(1)} %all-gather.rows_ref), channel_id=1, source_target_pairs={{0,384},{128,0},{256,128},{384,256},{1,385},{129,1},{257,129},{385... | collective-permute-start | bytes 1671176 | tf_op jit(solution)/shard_map/ppermute | solution.py:417
  91.8 0.1 pad_add_fusion.place
  91.9 6.3 %own_expert.1 = (bf16[8,128,256]{2,1,0:T(8,128)(2,1)S(1)}, bf16[8,3072,256]{2,1,0:T(8,128)(2,1)S(1)}) custom-call(s32[3]{0:T(128)S(1)} %pad_add_fusion.place, bf16[128,2176]{1,0:T(8,128)(2,1)S(1)} %all-gather.rows_ref, f32[8,2048]{1,0:T(8,128)S(1)} %get-tuple-element.10.residual_ref, bf16[8,3072,256]{2,1,0:T(8,128)(2,1)} %bitcast.10), custom_call_target="tpu_custom_call" | custom-call | tf_op jit(solution)/shard_map/own_expert/pallas_call | solution.py:337
  98.1 0.1 collective-permute-done.refs_0_
  98.3 8.2 %collective-permute-done.1.refs_1_ = bf16[128,2176]{1,0:T(8,128)(2,1)S(1)} collective-permute-done((bf16[128,2176]{1,0:T(8,128)(2,1)S(1)}, bf16[128,2176]{1,0:T(8,128)(2,1)S(1)}, u32[]{:S(2)}, u32[]{:S(2)}) %collective-permute-start.1) | collective-permute-done | bytes 557088 | tf_op jit(solution)/shard_map/ppermute | solution.py:417
  106.5 1.6 collective-permute-done.2.refs_2_
  108.1 5.9 %other_expert.1 = bf16[4,8,128,256]{3,2,1,0:T(8,128)(2,1)S(1)} custom-call(s32[3]{0:T(128)S(1)} %pad_add_fusion.place, bf16[128,2176]{1,0:T(8,128)(2,1)S(1)} %collective-permute-done.refs_0_, bf16[128,2176]{1,0:T(8,128)(2,1)S(1)} %collective-permute-done.1.refs_1_, bf16[128,2176]{1,0:T(8,128)(2,1)S(1)} %collective-permute-done.2.refs_2_, ...), custom_call_target="tpu_custom_call" | custom-call | tf_op jit(solution)/shard_map/other_expert/pallas_call | solution.py:363
  114.1 33.0 %all_to_all.21.parts_ref = bf16[32,128,256]{2,1,0:T(8,128)(2,1)S(1)} all-to-all(bf16[32,128,256]{2,1,0:T(8,128)(2,1)S(1)} %bitcast.8), channel_id=1, replica_groups=mesh['kv'=4,'seq'=16,'exp'=8] {'kv','exp'}, dimensions={0} | all-to-all | bytes 4194304 | tf_op jit(solution)/shard_map/all_to_all | solution.py:458
  147.1 0.3 fold.1
  147.4 38.5 %all_to_all.22.parts_ref = bf16[16,64,256]{2,1,0:T(8,128)(2,1)S(1)} all-to-all(bf16[16,64,256]{2,1,0:T(8,128)(2,1)S(1)} %fold.1), channel_id=1, replica_groups=mesh['kv'=4,'seq'=16,'exp'=8] {'seq'}, dimensions={0} | all-to-all | bytes 1048576 | tf_op jit(solution)/shard_map/all_to_all | solution.py:459
  185.8 0.7 total.1
  (23 shorter events, 0.1 us)
Async XLA Ops:
  6.5 3.3 %copy-start.5 = (s32[1,12,1]{1,2,0:T(1,128)S(1)}, s32[1,12,1]{1,2,0:T(1,128)}, u32[]{:S(2)}) copy-start(s32[1,12,1]{1,2,0:T(1,128)} %param.17) | copy-start | bytes 148
  6.5 3.3 %copy-start.2 = (bf16[1,64,2048]{2,1,0:T(8,128)(2,1)S(1)}, bf16[1,64,2048]{2,1,0:T(8,128)(2,1)}, u32[]{:S(2)}) copy-start(bf16[1,64,2048]{2,1,0:T(8,128)(2,1)} %q_ref.1) | copy-start | bytes 786436
  6.5 3.4 %copy-start.4 = (bf16[2,1,8,2048]{3,2,1,0:T(8,128)(2,1)S(1)}, bf16[2,1,8,2048]{3,2,1,0:T(8,128)(2,1)}, u32[]{:S(2)}) copy-start(bf16[2,1,8,2048]{3,2,1,0:T(8,128)(2,1)} %draft_ref.1) | copy-start | bytes 196612
  6.5 3.4 %copy-start = (bf16[2,12,16,2048]{3,2,1,0:T(8,128)(2,1)S(1)}, bf16[2,12,16,2048]{3,2,1,0:T(8,128)(2,1)}, u32[]{:S(2)}) copy-start(bf16[2,12,16,2048]{3,2,1,0:T(8,128)(2,1)} %pool_ref.1) | copy-start | bytes 4718596
  6.5 3.4 %copy-start.6 = (s32[1,64]{1,0:T(1,128)S(1)}, s32[1,64]{1,0:T(1,128)}, u32[]{:S(2)}) copy-start(s32[1,64]{1,0:T(1,128)} %parents_ref.1) | copy-start | bytes 772
  6.5 85.3 %all-gather.4.cloned.1.call-start = ((), (), s32[]{:S(2)}) async-start(), calls=%async_computation.4 | async-start | bytes 14155776 | tf_op jit(solution)/shard_map/all_gather | solution.py:442
  9.1 19.0 %copy-start.1 = (bf16[256,2048]{1,0:T(8,128)(2,1)S(1)}, bf16[256,2048]{1,0:T(8,128)(2,1)}, u32[]{:S(2)}) copy-start(bf16[256,2048]{1,0:T(8,128)(2,1)} %proj_ref.1) | copy-start | bytes 3145732
  9.9 23.0 %copy-start.7 = (bf16[2048,64]{0,1:T(8,128)(2,1)S(1)}, bf16[2048,64]{0,1:T(8,128)(2,1)}, u32[]{:S(2)}) copy-start(bf16[2048,64]{0,1:T(8,128)(2,1)} %param.23) | copy-start | bytes 786436
  15.8 17.4 %copy-start.8 = (s32[1,64,8]{1,2,0:T(8,128)S(1)}, s32[1,64,8]{1,2,0:T(8,128)}, u32[]{:S(2)}) copy-start(s32[1,64,8]{1,2,0:T(8,128)} %param.24) | copy-start | bytes 6148
  15.8 17.4 %copy-start.9 = (bf16[2048]{0:T(1024)(128)(2,1)S(1)}, bf16[2048]{0:T(1024)(128)(2,1)}, u32[]{:S(2)}) copy-start(bf16[2048]{0:T(1024)(128)(2,1)} %param.21) | copy-start | bytes 12292
  15.8 27.5 %copy-start.3 = (bf16[1,64,2048]{2,1,0:T(8,128)(2,1)S(1)}, bf16[1,64,2048]{2,1,0:T(8,128)(2,1)}, u32[]{:S(2)}) copy-start(bf16[1,64,2048]{2,1,0:T(8,128)(2,1)} %hidden_ref.1) | copy-start | bytes 786436
  29.5 13.8 %all-to-all-start.1 = ((bf16[8,8,2048]{2,1,0:T(8,128)(2,1)}), bf16[8,8,2048]{2,1,0:T(8,128)(2,1)S(1)}, u32[]{:S(2)}, u32[]{:S(2)}) async-start(bf16[8,8,2048]{2,1,0:T(8,128)(2,1)} %bitcast.5), calls=%async_computation.1 | async-start | bytes 524288 | tf_op jit(solution)/shard_map/all_to_all | solution.py:448
  80.4 17.8 %collective-permute-start = (bf16[128,2176]{1,0:T(8,128)(2,1)S(1)}, bf16[128,2176]{1,0:T(8,128)(2,1)S(1)}, u32[]{:S(2)}, u32[]{:S(2)}) collective-permute-start(bf16[128,2176]{1,0:T(8,128)(2,1)S(1)} %all-gather.rows_ref), channel_id=1, source_target_pairs={{0,128},{128,256},{256,384},{384,0},{1,129},{129,257},{257,385},{3... | collective-permute-start | bytes 1671176 | tf_op jit(solution)/shard_map/ppermute | solution.py:417
  83.8 22.7 %collective-permute-start.1 = (bf16[128,2176]{1,0:T(8,128)(2,1)S(1)}, bf16[128,2176]{1,0:T(8,128)(2,1)S(1)}, u32[]{:S(2)}, u32[]{:S(2)}) collective-permute-start(bf16[128,2176]{1,0:T(8,128)(2,1)S(1)} %all-gather.rows_ref), channel_id=1, source_target_pairs={{0,256},{128,384},{256,0},{384,128},{1,257},{129,385},{257,1},{385... | collective-permute-start | bytes 1671176 | tf_op jit(solution)/shard_map/ppermute | solution.py:417
  88.5 19.7 %collective-permute-start.2 = (bf16[128,2176]{1,0:T(8,128)(2,1)S(1)}, bf16[128,2176]{1,0:T(8,128)(2,1)S(1)}, u32[]{:S(2)}, u32[]{:S(2)}) collective-permute-start(bf16[128,2176]{1,0:T(8,128)(2,1)S(1)} %all-gather.rows_ref), channel_id=1, source_target_pairs={{0,384},{128,0},{256,128},{384,256},{1,385},{129,1},{257,129},{385... | collective-permute-start | bytes 1671176 | tf_op jit(solution)/shard_map/ppermute | solution.py:417
Sparse Core Ops, SparseCore 0:
  9.5 81.9 all-gather.3

commit v4 on v3

--- a/solution.py
+++ b/solution.py
@@ -291,58 +291,56 @@
         store(block, (nn(act_ref[...], down) * scale).astype(jnp.bfloat16))
 
 
-def own_kernel(place, rows_ref, residual_ref, weights_ref, out_ref, kept_ref, act_ref, sems):
+def columns_of(out_ref):
+    width = D // SETS
+
+    def store(block, value):
+        out_ref[:, block * width : (block + 1) * width] = value
+
+    return store
+
+
+def own_kernel(place, rows_ref, weights_ref, out_ref, kept_ref, act_ref, sems):
     copies = [
         pltpu.make_async_copy(weights_ref.at[block], kept_ref.at[block], sems.at[block])
         for block in range(SETS)
     ]
     for copy in copies:
         copy.start()
-    width = D // SETS
-    mine = pl.ds(pl.multiple_of(place[2] * TOK, TOK), TOK)
-
-    def store(block, value):
-        out_ref[block] = value
-
     expert_rows(
-        place[0], rows_ref, kept_ref, store, act_ref, lambda block: copies[block].wait()
-    )
-    for block in range(SETS):
-        own = out_ref[block, mine, :].astype(jnp.float32)
-        own = own + residual_ref[:, block * width : (block + 1) * width]
-        out_ref[block, mine, :] = own.astype(jnp.bfloat16)
+        place[0],
+        rows_ref,
+        kept_ref,
+        columns_of(out_ref),
+        act_ref,
+        lambda block: copies[block].wait(),
+    )
 
 
 def other_kernel(count, place, *refs):
-    rows_refs, own_ref, weights_ref, out_ref, act_ref = (
+    rows_refs, weights_ref, out_refs, act_ref = (
         refs[:count],
         refs[count],
-        refs[count + 1],
-        refs[count + 2],
-        refs[count + 3],
-    )
-    out_ref[place[1]] = own_ref[...]
-    for by, rows_ref in enumerate(rows_refs, 1):
-        target = lax.rem(place[1] + (count + 1 - by), count + 1)
-
-        def store(block, value, target=target):
-            out_ref[target, block] = value
-
-        expert_rows(place[0], rows_ref, weights_ref, store, act_ref, lambda block: None)
-
-
-def own_expert(place, rows, residual, weights):
+        refs[count + 1 : 2 * count + 1],
+        refs[2 * count + 1],
+    )
+    for rows_ref, out_ref in zip(rows_refs, out_refs):
+        expert_rows(
+            place[0], rows_ref, weights_ref, columns_of(out_ref), act_ref, lambda block: None
+        )
+
+
+def own_expert(place, rows, weights):
     count = rows.shape[0]
     vmem = pl.BlockSpec(memory_space=pltpu.VMEM)
     return pl.pallas_call(
         own_kernel,
         out_shape=(
-            pltpu.VMEM((SETS, count, D // SETS), jnp.bfloat16),
+            pltpu.VMEM((count, D), jnp.bfloat16),
             pltpu.VMEM(weights.shape, weights.dtype),
         ),
         in_specs=[
             pl.BlockSpec(memory_space=pltpu.SMEM),
-            vmem,
             vmem,
             pl.BlockSpec(memory_space=pl.ANY),
         ],
@@ -353,64 +351,108 @@
         ],
         compiler_params=pltpu.CompilerParams(vmem_limit_bytes=EXPERT_VMEM),
         name="own_expert",
-    )(place, rows, residual, pltpu.with_memory_space_constraint(weights, pltpu.HBM))
-
-
-def other_expert(place, own, weights, blocks):
+    )(place, rows, pltpu.with_memory_space_constraint(weights, pltpu.HBM))
+
+
+def in_vmem(*arrays):
+    return [pltpu.with_memory_space_constraint(x, pltpu.VMEM) for x in arrays]
+
+
+def other_expert(place, weights, *blocks):
     rows = blocks[0].shape[0]
     vmem = pl.BlockSpec(memory_space=pltpu.VMEM)
-    held = [pltpu.with_memory_space_constraint(x, pltpu.VMEM) for x in (*blocks, own, weights)]
     return pl.pallas_call(
         functools.partial(other_kernel, len(blocks)),
-        out_shape=jax.ShapeDtypeStruct((len(blocks) + 1, SETS, rows, D // SETS), jnp.bfloat16),
-        in_specs=[pl.BlockSpec(memory_space=pltpu.SMEM)] + [vmem] * len(held),
-        out_specs=vmem,
+        out_shape=tuple(jax.ShapeDtypeStruct((rows, D), jnp.bfloat16) for block in blocks),
+        in_specs=[pl.BlockSpec(memory_space=pltpu.SMEM)] + [vmem] * (len(blocks) + 1),
+        out_specs=(vmem,) * len(blocks),
         scratch_shapes=[pltpu.VMEM((rows, FF), jnp.bfloat16)],
         compiler_params=pltpu.CompilerParams(vmem_limit_bytes=EXPERT_VMEM),
         name="other_expert",
-    )(place, *held)
+    )(place, *in_vmem(*blocks, weights))
+
+
+def summed(refs, rows):
+    total = refs[0][rows].astype(jnp.float32)
+    for ref in refs[1:]:
+        total = total + ref[rows].astype(jnp.float32)
+    return total
+
+
+def join_kernel(place, residual_ref, *refs):
+    parts_refs, out_ref, work_ref = refs[:-2], refs[-2], refs[-1]
+    near = out_ref.shape[0]
+    rows = work_ref.shape[0]
+    step = 2 * TOK
+    for start in range(0, rows, step):
+        work_ref[start : start + step, :] = summed(parts_refs, slice(start, start + step))
+    mine = pl.ds(pl.multiple_of(place[2] * TOK, TOK), TOK)
+    work_ref[mine, :] = work_ref[mine, :] + residual_ref[...]
+    for seq in range(rows // TOK):
+        far = seq // near
+        out_ref[seq % near, far * TOK : (far + 1) * TOK, :] = work_ref[
+            seq * TOK : (seq + 1) * TOK, :
+        ].astype(jnp.bfloat16)
+
+
+def join(place, residual, parts, near):
+    rows = parts[0].shape[0]
+    vmem = pl.BlockSpec(memory_space=pltpu.VMEM)
+    return pl.pallas_call(
+        join_kernel,
+        out_shape=pltpu.VMEM((near, rows // near, D), jnp.bfloat16),
+        in_specs=[pl.BlockSpec(memory_space=pltpu.SMEM)] + [vmem] * (len(parts) + 1),
+        out_specs=vmem,
+        scratch_shapes=[pltpu.VMEM((rows, D), jnp.float32)],
+        compiler_params=pltpu.CompilerParams(vmem_limit_bytes=VMEM_LIMIT),
+        name="join",
+    )(place, *in_vmem(residual, *parts))
 
 
 def fold_kernel(parts_ref, out_ref):
-    seq_count = out_ref.shape[0]
-    width = out_ref.shape[2]
+    width = D // SETS
+    for far in range(parts_ref.shape[1] // TOK):
+        for block in range(SETS):
+            cols = slice(block * width, (block + 1) * width)
+            total = parts_ref[0, far * TOK : (far + 1) * TOK, cols].astype(jnp.float32)
+            for source in range(1, parts_ref.shape[0]):
+                total = total + parts_ref[
+                    source, far * TOK : (far + 1) * TOK, cols
+                ].astype(jnp.float32)
+            out_ref[far * SETS + block] = total.astype(jnp.bfloat16)
+
+
+def fold(parts):
+    far = parts.shape[1] // TOK
+    vmem = pl.BlockSpec(memory_space=pltpu.VMEM)
+    return pl.pallas_call(
+        fold_kernel,
+        out_shape=pltpu.VMEM((far * SETS, TOK, D // SETS), parts.dtype),
+        in_specs=[vmem],
+        out_specs=vmem,
+        compiler_params=pltpu.CompilerParams(vmem_limit_bytes=VMEM_LIMIT),
+        name="fold",
+    )(*in_vmem(parts))
+
+
+def total_kernel(parts_ref, out_ref):
     for source in range(SETS):
         total = parts_ref[source].astype(jnp.float32)
-        for block in range(1, parts_ref.shape[0] // SETS):
-            total = total + parts_ref[block * SETS + source].astype(jnp.float32)
-        total = total.astype(jnp.bfloat16).reshape(seq_count, TOK, width)
-        out_ref[:, source * TOK : (source + 1) * TOK, :] = total
-
-
-def fold(parts, seq_count):
+        for far in range(1, parts_ref.shape[0] // SETS):
+            total = total + parts_ref[far * SETS + source].astype(jnp.float32)
+        out_ref[0, source * TOK : (source + 1) * TOK, :] = total.astype(jnp.bfloat16)
+
+
+def total(parts):
     vmem = pl.BlockSpec(memory_space=pltpu.VMEM)
     return pl.pallas_call(
-        fold_kernel,
-        out_shape=pltpu.VMEM((seq_count, DRAFT, parts.shape[2]), parts.dtype),
+        total_kernel,
+        out_shape=jax.ShapeDtypeStruct((1, DRAFT, parts.shape[2]), parts.dtype),
         in_specs=[vmem],
         out_specs=vmem,
         compiler_params=pltpu.CompilerParams(vmem_limit_bytes=VMEM_LIMIT),
-        name="fold",
-    )(pltpu.with_memory_space_constraint(parts, pltpu.VMEM))
-
-
-def total_kernel(parts_ref, out_ref):
-    total = parts_ref[0].astype(jnp.float32)
-    for source in range(1, parts_ref.shape[0]):
-        total = total + parts_ref[source].astype(jnp.float32)
-    out_ref[0] = total.astype(jnp.bfloat16)
-
-
-def total(parts):
-    vmem = pl.BlockSpec(memory_space=pltpu.VMEM)
-    return pl.pallas_call(
-        total_kernel,
-        out_shape=jax.ShapeDtypeStruct((1,) + parts.shape[1:], parts.dtype),
-        in_specs=[vmem],
-        out_specs=vmem,
-        compiler_params=pltpu.CompilerParams(vmem_limit_bytes=VMEM_LIMIT),
         name="total",
-    )(pltpu.with_memory_space_constraint(parts, pltpu.VMEM))
+    )(*in_vmem(parts))
 
 
 def shifted(value, axis, count, by):
@@ -451,12 +493,33 @@
     )
     rows = lax.all_gather(row, "seq").reshape(seq_count * TOK, WIDE)
     place = jnp.stack([my_kv * seq_count + my_seq, my_kv, my_seq])
-    arrived = [shifted(rows, "kv", kv_count, by) for by in range(1, kv_count)]
-    own, kept = own_expert(place, rows, residual, weights)
-    finished = other_expert(place, own, kept, arrived)
-    back = finished.reshape(kv_count * SETS, seq_count * TOK, width)
-    back = lax.all_to_all(back, ("kv", "exp"), 0, 0, tiled=True)
-    back = lax.all_to_all(fold(back, seq_count), "seq", 0, 0, tiled=True)
+    arrived = {by: shifted(rows, "kv", kv_count, by) for by in range(1, kv_count)}
+    own, kept = own_expert(place, rows, weights)
+    near = other_expert(place, kept, arrived[1], arrived[kv_count - 1])
+    parts = [
+        own,
+        shifted(near[0], "kv", kv_count, -1),
+        shifted(near[1], "kv", kv_count, 1),
+    ]
+    for by in range(2, kv_count - 1):
+        (far,) = other_expert(place, kept, arrived[by])
+        parts.append(shifted(far, "kv", kv_count, -by))
+    run = 4
+    far_count = seq_count // run
+    runs = [[far * run + near for near in range(run)] for far in range(far_count)]
+    strides = [
+        [
+            (far * run + near) * SETS + block
+            for far in range(far_count)
+            for block in range(SETS)
+        ]
+        for near in range(run)
+    ]
+    back = join(place, residual, parts, run)
+    back = lax.all_to_all(back, "seq", 0, 0, tiled=True, axis_index_groups=runs)
+    back = lax.all_to_all(
+        fold(back), ("seq", "exp"), 0, 0, tiled=True, axis_index_groups=strides
+    )
     return total(back)
 
 

time: 194 us -> 188 us (0.969)
  the two profiles are of different devices: /device:TPU:32 before, /device:TPU:1 now
where the time goes in v4:
time: 188 us; the launch traced here: 187 us
  blocking collectives  98.6 us (52%)
  Pallas kernels  24.4 us (13%)
  starting transfers between devices  22.5 us (12%)
  waiting for transfers between devices  18 us (10%)
  between operations  14.2 us (8%)
  local copies, waits for them, and re-layouts  9.48 us (5%)
    all_to_all x1, blocking collectives, local(): lax.all_to_all(fold(back), ('seq', 'exp'), 0, 0, tiled=True, axis_index_g...  38.3 us
    all_gather x1, blocking collectives, local(): rows = lax.all_gather(row, 'seq').reshape(seq_count * TOK, WIDE)  32.2 us
    ppermute x6, starting transfers between devices, shifted(): lax.ppermute(value, axis, [(i, (i + by) % count) for i in range(count)])  18.5 us
    all_to_all x1, blocking collectives, local(): parts = lax.all_to_all(partials, 'exp', 0, 0, tiled=True)  16.6 us
    all_to_all x1, blocking collectives, local(): back = lax.all_to_all(back, 'seq', 0, 0, tiled=True, axis_index_groups=runs)  11.5 us
    ppermute x6, waiting for transfers between devices, shifted(): lax.ppermute(value, axis, [(i, (i + by) % count) for i in range(count)])  10.9 us
    unnamed x16, local copies, waits for them, and re-layouts  8.79 us
    all_to_all x1, waiting for transfers between devices, local(): lax.all_to_all(projected.reshape(SETS, TOK, D), 'exp', 0, 0, tiled=True)  7.07 us
  transfers between devices with their start and end apart: 8, of which 4 were waited for; matrix products, arithmetic and copies ran while one was open for 1% of the time, Pallas kernels for 11%

profile of v4, /device:TPU:1, one launch (start us, length us, event | category | flops | bytes accessed | tf_op | source)
XLA Modules:
  0.0 187.4 jit_solution(11559990471217420785)
XLA Ops:
  6.5 2.4 %pack.1 = bf16[3072,256]{1,0:T(8,128)(2,1)} custom-call(bf16[1,2048,128]{2,1,0:T(8,128)(2,1)} %gate_ref.1, bf16[1,2048,128]{2,1,0:T(8,128)(2,1)} %up_ref.1, bf16[1,128,2048]{2,1,0:T(8,128)(2,1)} %down_ref.1), custom_call_target="tpu_custom_call" | custom-call | tf_op jit(solution)/shard_map/pack/pallas_call | solution.py:263
  9.6 1.4 copy-done
  14.1 5.9 %attention.1 = bf16[8,72,256]{2,1,0:T(8,128)(2,1)S(1)} custom-call(s32[12]{0:T(128)S(1)} %bitcast.7, s32[1]{0:T(128)S(6)} %copy.17.lens, bf16[1,64,2048]{2,1,0:T(8,128)(2,1)S(1)} %copy-done.2, s32[1,64]{1,0:T(1,128)S(1)} %copy-done.6, bf16[2,1,8,2048]{3,2,1,0:T(8,128)(2,1)S(1)} %copy-done.4, bf16[2,12,16,2048]{3,2,1,0:T(8,128)(2,1)S(1)} %copy-done), custom_call_target="tpu_custom_call" | custom-call | tf_op jit(solution)/shard_map/attention/pallas_call | solution.py:113
  20.0 16.6 %all_to_all.20.parts_ref = bf16[8,72,256]{2,1,0:T(8,128)(2,1)S(1)} all-to-all(bf16[8,72,256]{2,1,0:T(8,128)(2,1)S(1)} %attention.1), channel_id=1, replica_groups=mesh['kv'=4,'seq'=16,'exp'=8] {'exp'}, dimensions={0} | all-to-all | bytes 589824 | tf_op jit(solution)/shard_map/all_to_all | solution.py:488
  36.5 1.3 copy-done.1
  37.8 1.3 merge.1
  39.1 3.9 %all-to-all-start.1 = ((bf16[8,8,2048]{2,1,0:T(8,128)(2,1)}), bf16[8,8,2048]{2,1,0:T(8,128)(2,1)S(1)}, u32[]{:S(2)}, u32[]{:S(2)}) async-start(bf16[8,8,2048]{2,1,0:T(8,128)(2,1)} %bitcast.5), calls=%async_computation.1 | async-start | bytes 524288 | tf_op jit(solution)/shard_map/all_to_all | solution.py:490
  43.8 1.2 copy.15.router_ref
  45.8 7.1 %all-to-all-done.1.parts_ref = bf16[8,8,2048]{2,1,0:T(8,128)(2,1)S(1)} async-done(((bf16[8,8,2048]{2,1,0:T(8,128)(2,1)}), bf16[8,8,2048]{2,1,0:T(8,128)(2,1)S(1)}, u32[]{:S(2)}, u32[]{:S(2)}) %all-to-all-start.1) | async-done | bytes 262176 | tf_op jit(solution)/shard_map/all_to_all | solution.py:490
  54.2 32.2 %all-gather.rows_ref = bf16[128,2176]{1,0:T(8,128)(2,1)S(1)} all-gather(bf16[8,2176]{1,0:T(8,128)(2,1)S(1)} %get-tuple-element.12), channel_id=2, replica_groups=mesh['kv'=4,'seq'=16,'exp'=8] {'seq'}, dimensions={0}, use_global_device_ids=true | all-gather | bytes 591872 | tf_op jit(solution)/shard_map/all_gather | solution.py:494
  86.4 3.1 %collective-permute-start = (bf16[128,2176]{1,0:T(8,128)(2,1)S(1)}, bf16[128,2176]{1,0:T(8,128)(2,1)S(1)}, u32[]{:S(2)}, u32[]{:S(2)}) collective-permute-start(bf16[128,2176]{1,0:T(8,128)(2,1)S(1)} %all-gather.rows_ref), channel_id=1, source_target_pairs={{0,128},{128,256},{256,384},{384,0},{1,129},{129,257},{257,385},{3... | collective-permute-start | bytes 1671176 | tf_op jit(solution)/shard_map/ppermute | solution.py:459
  89.6 3.4 %collective-permute-start.1 = (bf16[128,2176]{1,0:T(8,128)(2,1)S(1)}, bf16[128,2176]{1,0:T(8,128)(2,1)S(1)}, u32[]{:S(2)}, u32[]{:S(2)}) collective-permute-start(bf16[128,2176]{1,0:T(8,128)(2,1)S(1)} %all-gather.rows_ref), channel_id=1, source_target_pairs={{0,384},{128,0},{256,128},{384,256},{1,385},{129,1},{257,129},{385... | collective-permute-start | bytes 1671176 | tf_op jit(solution)/shard_map/ppermute | solution.py:459
  92.9 3.5 %collective-permute-start.4 = (bf16[128,2176]{1,0:T(8,128)(2,1)S(1)}, bf16[128,2176]{1,0:T(8,128)(2,1)S(1)}, u32[]{:S(2)}, u32[]{:S(2)}) collective-permute-start(bf16[128,2176]{1,0:T(8,128)(2,1)S(1)} %all-gather.rows_ref), channel_id=1, source_target_pairs={{0,256},{128,384},{256,0},{384,128},{1,257},{129,385},{257,1},{385... | collective-permute-start | bytes 1671176 | tf_op jit(solution)/shard_map/ppermute | solution.py:459
  96.5 6.3 %own_expert.1 = (bf16[128,2048]{1,0:T(8,128)(2,1)S(1)}, bf16[8,3072,256]{2,1,0:T(8,128)(2,1)S(1)}) custom-call(s32[3]{0:T(128)S(1)} %pad_add_fusion.place, bf16[128,2176]{1,0:T(8,128)(2,1)S(1)} %all-gather.rows_ref, bf16[8,3072,256]{2,1,0:T(8,128)(2,1)} %bitcast.8), custom_call_target="tpu_custom_call" | custom-call | tf_op jit(solution)/shard_map/own_expert/pallas_call | solution.py:336
  102.8 4.2 %other_expert.2 = (bf16[128,2048]{1,0:T(8,128)(2,1)S(1)}, bf16[128,2048]{1,0:T(8,128)(2,1)S(1)}) custom-call(s32[3]{0:T(128)S(1)} %pad_add_fusion.place, bf16[128,2176]{1,0:T(8,128)(2,1)S(1)} %collective-permute-done.refs_0_, bf16[128,2176]{1,0:T(8,128)(2,1)S(1)} %collective-permute-done.1.refs_1_, bf16[8,3072,256]{2,1,0:T(8,128)(2,1)S(1)} %get-tuple-element.14.refs_2_.refs_1_), custom_call_target="tpu_custom_call" | custom-call | tf_op jit(solution)/shard_map/other_expert/pallas_call | solution.py:364
  107.0 2.7 %collective-permute-start.2 = (bf16[128,2048]{1,0:T(8,128)(2,1)S(1)}, bf16[128,2048]{1,0:T(8,128)(2,1)S(1)}, u32[]{:S(2)}, u32[]{:S(2)}) collective-permute-start(bf16[128,2048]{1,0:T(8,128)(2,1)S(1)} %get-tuple-element.15), channel_id=1, source_target_pairs={{0,384},{128,0},{256,128},{384,256},{1,385},{129,1},{257,129},{385... | collective-permute-start | bytes 1572872 | tf_op jit(solution)/shard_map/ppermute | solution.py:459
  109.8 2.5 %collective-permute-start.3 = (bf16[128,2048]{1,0:T(8,128)(2,1)S(1)}, bf16[128,2048]{1,0:T(8,128)(2,1)S(1)}, u32[]{:S(2)}, u32[]{:S(2)}) collective-permute-start(bf16[128,2048]{1,0:T(8,128)(2,1)S(1)} %get-tuple-element.16), channel_id=1, source_target_pairs={{0,128},{128,256},{256,384},{384,0},{1,129},{129,257},{257,385},{3... | collective-permute-start | bytes 1572872 | tf_op jit(solution)/shard_map/ppermute | solution.py:459
  112.3 2.5 %other_expert.3 = bf16[128,2048]{1,0:T(8,128)(2,1)S(1)} custom-call(s32[3]{0:T(128)S(1)} %pad_add_fusion.place, bf16[128,2176]{1,0:T(8,128)(2,1)S(1)} %collective-permute-done.4.refs_0_, bf16[8,3072,256]{2,1,0:T(8,128)(2,1)S(1)} %get-tuple-element.14.refs_2_.refs_1_), custom_call_target="tpu_custom_call" | custom-call | tf_op jit(solution)/shard_map/other_expert/pallas_call | solution.py:364
  114.8 3.3 %collective-permute-start.5 = (bf16[128,2048]{1,0:T(8,128)(2,1)S(1)}, bf16[128,2048]{1,0:T(8,128)(2,1)S(1)}, u32[]{:S(2)}, u32[]{:S(2)}) collective-permute-start(bf16[128,2048]{1,0:T(8,128)(2,1)S(1)} %other_expert.3), channel_id=1, source_target_pairs={{0,256},{128,384},{256,0},{384,128},{1,257},{129,385},{257,1},{385... | collective-permute-start | bytes 1572872 | tf_op jit(solution)/shard_map/ppermute | solution.py:459
  118.1 5.1 %collective-permute-done.2.refs_1_ = bf16[128,2048]{1,0:T(8,128)(2,1)S(1)} collective-permute-done((bf16[128,2048]{1,0:T(8,128)(2,1)S(1)}, bf16[128,2048]{1,0:T(8,128)(2,1)S(1)}, u32[]{:S(2)}, u32[]{:S(2)}) %collective-permute-start.2) | collective-permute-done | bytes 524320 | tf_op jit(solution)/shard_map/ppermute | solution.py:459
  123.2 4.6 %collective-permute-done.3.refs_2_ = bf16[128,2048]{1,0:T(8,128)(2,1)S(1)} collective-permute-done((bf16[128,2048]{1,0:T(8,128)(2,1)S(1)}, bf16[128,2048]{1,0:T(8,128)(2,1)S(1)}, u32[]{:S(2)}, u32[]{:S(2)}) %collective-permute-start.3) | collective-permute-done | bytes 524320 | tf_op jit(solution)/shard_map/ppermute | solution.py:459
  127.8 1.2 collective-permute-done.5.refs_3_
  129.9 11.5 %all_to_all.21.parts_ref = bf16[4,32,2048]{2,1,0:T(8,128)(2,1)S(1)} all-to-all(bf16[4,32,2048]{2,1,0:T(8,128)(2,1)S(1)} %join.1), channel_id=1, replica_groups={{0,8,16,24},{32,40,48,56},{64,72,80,88},{96,104,112,120},{1,9,17,25},{3..., dimensions={0} | all-to-all | bytes 1048576 | tf_op jit(solution)/shard_map/all_to_all | solution.py:519
  141.5 38.3 %all_to_all.22.parts_ref = bf16[32,8,256]{2,1,0:T(8,128)(2,1)S(1)} all-to-all(bf16[32,8,256]{2,1,0:T(8,128)(2,1)S(1)} %fold.1), channel_id=1, replica_groups={{0,1,2,3,4,5,6,7,32,33,34,35,36,37,38,39,64,65,66,67,68,69,70,71,96,97,..., dimensions={0} | all-to-all | bytes 262144 | tf_op jit(solution)/shard_map/all_to_all | solution.py:520
  (25 shorter events, 7.7 us)
Async XLA Ops:
  6.5 90.0 %all-gather.4.cloned.1.call-start = ((), (), s32[]{:S(2)}) async-start(), calls=%async_computation.4 | async-start | bytes 14155776 | tf_op jit(solution)/shard_map/all_gather | solution.py:484
  9.6 1.4 copy-start
  11.0 0.9 copy-start.2
  11.9 0.8 copy-start.4
  12.8 0.7 copy-start.5
  13.4 0.7 copy-start.6
  36.5 1.3 copy-start.1
  39.1 13.7 %all-to-all-start.1 = ((bf16[8,8,2048]{2,1,0:T(8,128)(2,1)}), bf16[8,8,2048]{2,1,0:T(8,128)(2,1)S(1)}, u32[]{:S(2)}, u32[]{:S(2)}) async-start(bf16[8,8,2048]{2,1,0:T(8,128)(2,1)} %bitcast.5), calls=%async_computation.1 | async-start | bytes 524288 | tf_op jit(solution)/shard_map/all_to_all | solution.py:490
  52.8 1.0 copy-start.3
  86.4 16.3 %collective-permute-start = (bf16[128,2176]{1,0:T(8,128)(2,1)S(1)}, bf16[128,2176]{1,0:T(8,128)(2,1)S(1)}, u32[]{:S(2)}, u32[]{:S(2)}) collective-permute-start(bf16[128,2176]{1,0:T(8,128)(2,1)S(1)} %all-gather.rows_ref), channel_id=1, source_target_pairs={{0,128},{128,256},{256,384},{384,0},{1,129},{129,257},{257,385},{3... | collective-permute-start | bytes 1671176 | tf_op jit(solution)/shard_map/ppermute | solution.py:459
  89.6 13.2 %collective-permute-start.1 = (bf16[128,2176]{1,0:T(8,128)(2,1)S(1)}, bf16[128,2176]{1,0:T(8,128)(2,1)S(1)}, u32[]{:S(2)}, u32[]{:S(2)}) collective-permute-start(bf16[128,2176]{1,0:T(8,128)(2,1)S(1)} %all-gather.rows_ref), channel_id=1, source_target_pairs={{0,384},{128,0},{256,128},{384,256},{1,385},{129,1},{257,129},{385... | collective-permute-start | bytes 1671176 | tf_op jit(solution)/shard_map/ppermute | solution.py:459
  92.9 19.4 %collective-permute-start.4 = (bf16[128,2176]{1,0:T(8,128)(2,1)S(1)}, bf16[128,2176]{1,0:T(8,128)(2,1)S(1)}, u32[]{:S(2)}, u32[]{:S(2)}) collective-permute-start(bf16[128,2176]{1,0:T(8,128)(2,1)S(1)} %all-gather.rows_ref), channel_id=1, source_target_pairs={{0,256},{128,384},{256,0},{384,128},{1,257},{129,385},{257,1},{385... | collective-permute-start | bytes 1671176 | tf_op jit(solution)/shard_map/ppermute | solution.py:459
  107.0 16.2 %collective-permute-start.2 = (bf16[128,2048]{1,0:T(8,128)(2,1)S(1)}, bf16[128,2048]{1,0:T(8,128)(2,1)S(1)}, u32[]{:S(2)}, u32[]{:S(2)}) collective-permute-start(bf16[128,2048]{1,0:T(8,128)(2,1)S(1)} %get-tuple-element.15), channel_id=1, source_target_pairs={{0,384},{128,0},{256,128},{384,256},{1,385},{129,1},{257,129},{385... | collective-permute-start | bytes 1572872 | tf_op jit(solution)/shard_map/ppermute | solution.py:459
  109.8 18.0 %collective-permute-start.3 = (bf16[128,2048]{1,0:T(8,128)(2,1)S(1)}, bf16[128,2048]{1,0:T(8,128)(2,1)S(1)}, u32[]{:S(2)}, u32[]{:S(2)}) collective-permute-start(bf16[128,2048]{1,0:T(8,128)(2,1)S(1)} %get-tuple-element.16), channel_id=1, source_target_pairs={{0,128},{128,256},{256,384},{384,0},{1,129},{129,257},{257,385},{3... | collective-permute-start | bytes 1572872 | tf_op jit(solution)/shard_map/ppermute | solution.py:459
  114.8 14.2 %collective-permute-start.5 = (bf16[128,2048]{1,0:T(8,128)(2,1)S(1)}, bf16[128,2048]{1,0:T(8,128)(2,1)S(1)}, u32[]{:S(2)}, u32[]{:S(2)}) collective-permute-start(bf16[128,2048]{1,0:T(8,128)(2,1)S(1)} %other_expert.3), channel_id=1, source_target_pairs={{0,256},{128,384},{256,0},{384,128},{1,257},{129,385},{257,1},{385... | collective-permute-start | bytes 1572872 | tf_op jit(solution)/shard_map/ppermute | solution.py:459
Sparse Core Ops, SparseCore 0:
  9.5 83.5 all-gather.3

commit v5 on v4

--- a/solution.py
+++ b/solution.py
@@ -42,95 +42,138 @@
     return lax.dot_general(a, b, (((1,), (0,)), ((), ())), preferred_element_type=jnp.float32)
 
 
+def in_vmem(*arrays):
+    return [pltpu.with_memory_space_constraint(x, pltpu.VMEM) for x in arrays]
+
+
+def expert_index():
+    return lax.axis_index("kv") * lax.axis_size("seq") + lax.axis_index("seq")
+
+
 def attention_kernel(
-    table, lens, q_ref, parents_ref, draft_ref, pool_ref, out_ref, kbuf, vbuf, seen_ref, sems
+    table,
+    lens,
+    q_hbm,
+    parents_hbm,
+    draft_hbm,
+    pool_ref,
+    proj_ref,
+    out_ref,
+    kept_ref,
+    kbuf,
+    vbuf,
+    q_ref,
+    draft_ref,
+    parents_ref,
+    seen_ref,
+    score_ref,
+    weight_ref,
+    sems,
+    more_sems,
 ):
-    copies = []
+    keys, values = [], []
     for page in range(PPD):
         slot = table[page]
         rows = pl.ds(page * PAGE, PAGE)
-        copies.append(pltpu.make_async_copy(pool_ref.at[0, slot], kbuf.at[rows], sems.at[0, page]))
-        copies.append(pltpu.make_async_copy(pool_ref.at[1, slot], vbuf.at[rows], sems.at[1, page]))
-    for copy in copies:
+        keys.append(pltpu.make_async_copy(pool_ref.at[0, slot], kbuf.at[rows], sems.at[0, page]))
+        values.append(pltpu.make_async_copy(pool_ref.at[1, slot], vbuf.at[rows], sems.at[1, page]))
+    query_copy = pltpu.make_async_copy(q_hbm.at[0], q_ref, more_sems.at[0])
+    draft_copy = pltpu.make_async_copy(draft_hbm.at[:, 0], draft_ref, more_sems.at[1])
+    proj_copy = pltpu.make_async_copy(proj_ref, kept_ref, more_sems.at[2])
+    parents_copy = pltpu.make_async_copy(parents_hbm, parents_ref, more_sems.at[3])
+    for copy in [parents_copy, draft_copy, query_copy] + keys + values + [proj_copy]:
         copy.start()
     length = lens[0]
     my_set = lax.axis_index("exp")
-    pad = jnp.zeros((8, D), jnp.float32)
-    kbuf[KEYS:ROWS, :] = jnp.concatenate([draft_ref[0, 0].astype(jnp.float32), pad], axis=0).astype(
-        jnp.bfloat16
-    )
-    vbuf[KEYS:ROWS, :] = jnp.concatenate([draft_ref[1, 0].astype(jnp.float32), pad], axis=0).astype(
-        jnp.bfloat16
-    )
     ancestor = lax.broadcasted_iota(jnp.int32, (DRAFT, 2 * DRAFT), 0)
     token = lax.broadcasted_iota(jnp.int32, (DRAFT, 2 * DRAFT), 1) % DRAFT
+    parents_copy.wait()
     parents = jnp.concatenate([parents_ref[...], parents_ref[...]], axis=1)
     linked = jnp.where((parents == ancestor) | (ancestor == token), 1.0, 0.0)
     for doubling in range((DRAFT - 1).bit_length()):
         narrow = linked.astype(jnp.bfloat16)
         linked = jnp.minimum(nn(narrow[:, :DRAFT], narrow), 1.0)
-    seen_ref[...] = linked
+    seen_ref[0:DRAFT, :] = linked
     draft_seen = seen_ref[pl.ds(pl.multiple_of(my_set * TOK, TOK), TOK), :]
     key_row = lax.broadcasted_iota(jnp.int32, (KEYS, 2 * DRAFT), 0)
     position = ((key_row // PAGE) * SETS + my_set) * PAGE + key_row % PAGE
     cache_seen = jnp.where(position < length, 1.0, 0.0)
-    seen = (
-        jnp.concatenate(
-            [cache_seen, draft_seen, jnp.zeros((8, 2 * DRAFT), jnp.float32)], axis=0
-        )
-        > 0.5
+    seen_ref[0:ROWS, :] = jnp.concatenate(
+        [cache_seen, draft_seen, jnp.zeros((8, 2 * DRAFT), jnp.float32)], axis=0
     )
     own = (lax.broadcasted_iota(jnp.int32, (2 * DRAFT, 2 * HD), 0) < DRAFT) == (
         lax.broadcasted_iota(jnp.int32, (2 * DRAFT, 2 * HD), 1) < HD
     )
     stat_row = lax.broadcasted_iota(jnp.int32, (8, 2 * DRAFT), 0)
-    for copy in copies:
+    pad = jnp.zeros((8, D), jnp.float32)
+    draft_copy.wait()
+    for place, buf in ((0, kbuf), (1, vbuf)):
+        rows = jnp.concatenate([draft_ref[place].astype(jnp.float32), pad], axis=0)
+        buf[KEYS:ROWS, :] = rows.astype(jnp.bfloat16)
+    query_copy.wait()
+    for copy in keys:
         copy.wait()
     for pair in range(H // 2):
         cols = slice(pair * 2 * HD, (pair + 1) * 2 * HD)
-        query = q_ref[0, :, cols]
+        query = q_ref[:, cols]
         query = jnp.where(own, jnp.concatenate([query, query], axis=0), jnp.zeros((), jnp.bfloat16))
-        scores = nt(kbuf[:, cols], query) * (HD**-0.5)
-        scores = jnp.where(seen, scores, NEG_FILL)
+        score_ref[pair] = nt(kbuf[:, cols], query) * (HD**-0.5)
+    for pair in range(H // 2):
+        seen = seen_ref[0:ROWS, :] > 0.5
+        scores = jnp.where(seen, score_ref[pair], NEG_FILL)
         top = jnp.max(scores, axis=0, keepdims=True).astype(jnp.bfloat16).astype(jnp.float32)
         weights = jnp.where(seen, jnp.exp(scores - top), 0.0)
         total = jnp.sum(weights, axis=0, keepdims=True)
-        acc = tn(weights.astype(jnp.bfloat16), vbuf[:, cols])
+        weight_ref[pair] = weights.astype(jnp.bfloat16)
         total_high = total.astype(jnp.bfloat16).astype(jnp.float32)
         stats = jnp.where(
             stat_row == 0,
             top,
             jnp.where(stat_row == 1, total_high, jnp.where(stat_row == 2, total - total_high, 0.0)),
         )
+        out_ref[pair, DRAFT:STAT, 0:HD] = stats.astype(jnp.bfloat16)
+        out_ref[pair, DRAFT:STAT, HD : 2 * HD] = jnp.zeros((8, HD), jnp.bfloat16)
+    for copy in values:
+        copy.wait()
+    for pair in range(H // 2):
+        cols = slice(pair * 2 * HD, (pair + 1) * 2 * HD)
+        acc = tn(weight_ref[pair], vbuf[:, cols])
         out_ref[pair, 0:DRAFT, 0:HD] = acc[:DRAFT, :HD].astype(jnp.bfloat16)
         out_ref[pair, 0:DRAFT, HD : 2 * HD] = acc[DRAFT:, HD:].astype(jnp.bfloat16)
-        out_ref[pair, DRAFT:STAT, 0:HD] = stats.astype(jnp.bfloat16)
-        out_ref[pair, DRAFT:STAT, HD : 2 * HD] = jnp.zeros((8, HD), jnp.bfloat16)
-
-
-def attention(table, lens, queries, parents, draft_kv, kv_pool):
-    vmem = pl.BlockSpec(memory_space=pltpu.VMEM)
+    proj_copy.wait()
+
+
+def attention(table, lens, queries, parents, draft_kv, kv_pool, out_proj):
+    smem = pl.BlockSpec(memory_space=pltpu.SMEM)
+    vmem = pl.BlockSpec(memory_space=pltpu.VMEM)
+    hbm = pl.BlockSpec(memory_space=pltpu.HBM)
+    queries, parents, draft_kv, kv_pool, out_proj = (
+        pltpu.with_memory_space_constraint(x, pltpu.HBM)
+        for x in (queries, parents, draft_kv, kv_pool, out_proj)
+    )
     return pl.pallas_call(
         attention_kernel,
-        out_shape=jax.ShapeDtypeStruct((SETS, STAT, 2 * HD), jnp.bfloat16),
-        in_specs=[
-            pl.BlockSpec(memory_space=pltpu.SMEM),
-            pl.BlockSpec(memory_space=pltpu.SMEM),
-            vmem,
-            vmem,
-            vmem,
-            pl.BlockSpec(memory_space=pl.ANY),
-        ],
-        out_specs=vmem,
+        out_shape=(
+            jax.ShapeDtypeStruct((SETS, STAT, 2 * HD), jnp.bfloat16),
+            pltpu.VMEM(out_proj.shape, out_proj.dtype),
+        ),
+        in_specs=[smem, smem, hbm, hbm, hbm, hbm, hbm],
+        out_specs=(vmem, vmem),
         scratch_shapes=[
             pltpu.VMEM((ROWS, D), jnp.bfloat16),
             pltpu.VMEM((ROWS, D), jnp.bfloat16),
-            pltpu.VMEM((DRAFT, 2 * DRAFT), jnp.float32),
+            pltpu.VMEM((DRAFT, D), jnp.bfloat16),
+            pltpu.VMEM((2, TOK, D), jnp.bfloat16),
+            pltpu.VMEM((1, DRAFT), jnp.int32),
+            pltpu.VMEM((ROWS, 2 * DRAFT), jnp.float32),
+            pltpu.VMEM((H // 2, ROWS, 2 * DRAFT), jnp.float32),
+            pltpu.VMEM((H // 2, ROWS, 2 * DRAFT), jnp.bfloat16),
             pltpu.SemaphoreType.DMA((2, PPD)),
+            pltpu.SemaphoreType.DMA((4,)),
         ],
         compiler_params=pltpu.CompilerParams(vmem_limit_bytes=VMEM_LIMIT),
         name="attention",
-    )(table, lens, queries, parents, draft_kv, kv_pool)
+    )(table, lens, queries, parents, draft_kv, kv_pool, out_proj)
 
 
 def merge_kernel(parts_ref, proj_ref, out_ref):
@@ -156,54 +199,55 @@
         out_shape=jax.ShapeDtypeStruct((DRAFT, D), jnp.bfloat16),
         compiler_params=pltpu.CompilerParams(vmem_limit_bytes=VMEM_LIMIT),
         name="merge",
-    )(parts, out_proj)
-
-
-def norm_kernel(my_set, parts_ref, hidden_ref, gain_ref, router_ref, routes_ref, residual_ref, row_ref):
-    residual = hidden_ref[0].astype(jnp.float32)
-    for source in range(SETS):
+    )(parts, *in_vmem(out_proj))
+
+
+def norm_kernel(
+    parts_ref, hidden_ref, gain_ref, router_ref, routes_ref, residual_ref, row_ref, own_ref, sem
+):
+    mine = pl.ds(pl.multiple_of(lax.axis_index("exp") * TOK, TOK), TOK)
+    copy = pltpu.make_async_copy(hidden_ref.at[0, mine], own_ref, sem)
+    copy.start()
+    residual = parts_ref[0].astype(jnp.float32)
+    for source in range(1, SETS):
         residual = residual + parts_ref[source].astype(jnp.float32)
+    expert = lax.broadcasted_iota(jnp.int32, (TOK, EXPERTS), 1)
+    routes = routes_ref[0, mine, :]
+    chosen = routes[:, 0:1] == expert
+    for pick in range(1, TOPK):
+        chosen = chosen | (routes[:, pick : pick + 1] == expert)
+    copy.wait()
+    residual = own_ref[...].astype(jnp.float32) + residual
     residual_ref[...] = residual
     mean_sq = jnp.mean(residual * residual, axis=1, keepdims=True)
     normed = (residual * lax.rsqrt(mean_sq + EPS_NORM) * gain_ref[...].astype(jnp.float32)).astype(
         jnp.bfloat16
     )
     logits = nn(normed, router_ref[...])
-    gates = 1.0 / (1.0 + jnp.exp(-logits))
-    expert = lax.broadcasted_iota(jnp.int32, (TOK, EXPERTS), 1)
-    routes = routes_ref[0]
-    chosen = routes[:, 0:1] == expert
-    for pick in range(1, TOPK):
-        chosen = chosen | (routes[:, pick : pick + 1] == expert)
-    gates = jnp.where(chosen, gates, 0.0)
+    gates = jnp.where(chosen, 1.0 / (1.0 + jnp.exp(-logits)), 0.0)
     high = gates.astype(jnp.bfloat16).astype(jnp.float32)
     row_ref[:, 0:D] = normed
     row_ref[:, D:WIDE] = jnp.concatenate([high, gates - high], axis=1).astype(jnp.bfloat16)
 
 
-def norm(my_set, parts, hidden, norm_gain, router, routes):
-    whole = lambda *shape: pl.BlockSpec(shape, lambda i, s: (0,) * len(shape))
+def norm(parts, hidden, norm_gain, router, routes):
+    vmem = pl.BlockSpec(memory_space=pltpu.VMEM)
     return pl.pallas_call(
         norm_kernel,
         out_shape=(
-            jax.ShapeDtypeStruct((TOK, D), jnp.float32),
+            pltpu.VMEM((TOK, D), jnp.float32),
             jax.ShapeDtypeStruct((TOK, WIDE), jnp.bfloat16),
         ),
-        grid_spec=pltpu.PrefetchScalarGridSpec(
-            num_scalar_prefetch=1,
-            grid=(1,),
-            in_specs=[
-                whole(SETS, TOK, D),
-                pl.BlockSpec((1, TOK, D), lambda i, s: (0, s[0], 0)),
-                whole(1, D),
-                whole(D, EXPERTS),
-                pl.BlockSpec((1, TOK, TOPK), lambda i, s: (0, s[0], 0)),
-            ],
-            out_specs=(whole(TOK, D), whole(TOK, WIDE)),
-        ),
+        in_specs=[vmem, pl.BlockSpec(memory_space=pltpu.HBM), vmem, vmem, vmem],
+        out_specs=(vmem, vmem),
+        scratch_shapes=[pltpu.VMEM((TOK, D), jnp.bfloat16), pltpu.SemaphoreType.DMA],
         compiler_params=pltpu.CompilerParams(vmem_limit_bytes=VMEM_LIMIT),
         name="norm",
-    )(my_set, parts, hidden, norm_gain, router, routes)
+    )(
+        *in_vmem(parts),
+        pltpu.with_memory_space_constraint(hidden, pltpu.HBM),
+        *in_vmem(norm_gain, router, routes),
+    )
 
 
 def pack_kernel(gate_ref, up_ref, down_ref, out_ref, buf, in_sems, out_sems):
@@ -300,7 +344,7 @@
     return store
 
 
-def own_kernel(place, rows_ref, weights_ref, out_ref, kept_ref, act_ref, sems):
+def own_kernel(rows_ref, weights_ref, out_ref, kept_ref, act_ref, sems):
     copies = [
         pltpu.make_async_copy(weights_ref.at[block], kept_ref.at[block], sems.at[block])
         for block in range(SETS)
@@ -308,7 +352,7 @@
     for copy in copies:
         copy.start()
     expert_rows(
-        place[0],
+        expert_index(),
         rows_ref,
         kept_ref,
         columns_of(out_ref),
@@ -317,7 +361,7 @@
     )
 
 
-def other_kernel(count, place, *refs):
+def other_kernel(count, *refs):
     rows_refs, weights_ref, out_refs, act_ref = (
         refs[:count],
         refs[count],
@@ -326,11 +370,11 @@
     )
     for rows_ref, out_ref in zip(rows_refs, out_refs):
         expert_rows(
-            place[0], rows_ref, weights_ref, columns_of(out_ref), act_ref, lambda block: None
+            expert_index(), rows_ref, weights_ref, columns_of(out_ref), act_ref, lambda block: None
         )
 
 
-def own_expert(place, rows, weights):
+def own_expert(rows, weights):
     count = rows.shape[0]
     vmem = pl.BlockSpec(memory_space=pltpu.VMEM)
     return pl.pallas_call(
@@ -339,11 +383,7 @@
             pltpu.VMEM((count, D), jnp.bfloat16),
             pltpu.VMEM(weights.shape, weights.dtype),
         ),
-        in_specs=[
-            pl.BlockSpec(memory_space=pltpu.SMEM),
-            vmem,
-            pl.BlockSpec(memory_space=pl.ANY),
-        ],
+        in_specs=[vmem, pl.BlockSpec(memory_space=pltpu.HBM)],
         out_specs=(vmem, vmem),
         scratch_shapes=[
             pltpu.VMEM((count, FF), jnp.bfloat16),
@@ -351,25 +391,21 @@
         ],
         compiler_params=pltpu.CompilerParams(vmem_limit_bytes=EXPERT_VMEM),
         name="own_expert",
-    )(place, rows, pltpu.with_memory_space_constraint(weights, pltpu.HBM))
-
-
-def in_vmem(*arrays):
-    return [pltpu.with_memory_space_constraint(x, pltpu.VMEM) for x in arrays]
-
-
-def other_expert(place, weights, *blocks):
+    )(*in_vmem(rows), pltpu.with_memory_space_constraint(weights, pltpu.HBM))
+
+
+def other_expert(weights, *blocks):
     rows = blocks[0].shape[0]
     vmem = pl.BlockSpec(memory_space=pltpu.VMEM)
     return pl.pallas_call(
         functools.partial(other_kernel, len(blocks)),
         out_shape=tuple(jax.ShapeDtypeStruct((rows, D), jnp.bfloat16) for block in blocks),
-        in_specs=[pl.BlockSpec(memory_space=pltpu.SMEM)] + [vmem] * (len(blocks) + 1),
+        in_specs=[vmem] * (len(blocks) + 1),
         out_specs=(vmem,) * len(blocks),
         scratch_shapes=[pltpu.VMEM((rows, FF), jnp.bfloat16)],
         compiler_params=pltpu.CompilerParams(vmem_limit_bytes=EXPERT_VMEM),
         name="other_expert",
-    )(place, *in_vmem(*blocks, weights))
+    )(*in_vmem(*blocks, weights))
 
 
 def summed(refs, rows):
@@ -379,14 +415,14 @@
     return total
 
 
-def join_kernel(place, residual_ref, *refs):
+def join_kernel(residual_ref, *refs):
     parts_refs, out_ref, work_ref = refs[:-2], refs[-2], refs[-1]
     near = out_ref.shape[0]
     rows = work_ref.shape[0]
     step = 2 * TOK
     for start in range(0, rows, step):
         work_ref[start : start + step, :] = summed(parts_refs, slice(start, start + step))
-    mine = pl.ds(pl.multiple_of(place[2] * TOK, TOK), TOK)
+    mine = pl.ds(pl.multiple_of(lax.axis_index("seq") * TOK, TOK), TOK)
     work_ref[mine, :] = work_ref[mine, :] + residual_ref[...]
     for seq in range(rows // TOK):
         far = seq // near
@@ -395,18 +431,18 @@
         ].astype(jnp.bfloat16)
 
 
-def join(place, residual, parts, near):
+def join(residual, parts, near):
     rows = parts[0].shape[0]
     vmem = pl.BlockSpec(memory_space=pltpu.VMEM)
     return pl.pallas_call(
         join_kernel,
         out_shape=pltpu.VMEM((near, rows // near, D), jnp.bfloat16),
-        in_specs=[pl.BlockSpec(memory_space=pltpu.SMEM)] + [vmem] * (len(parts) + 1),
+        in_specs=[vmem] * (len(parts) + 1),
         out_specs=vmem,
         scratch_shapes=[pltpu.VMEM((rows, D), jnp.float32)],
         compiler_params=pltpu.CompilerParams(vmem_limit_bytes=VMEM_LIMIT),
         name="join",
-    )(place, *in_vmem(residual, *parts))
+    )(*in_vmem(residual, *parts))
 
 
 def fold_kernel(parts_ref, out_ref):
@@ -475,34 +511,27 @@
     up_w,
     down_w,
 ):
-    my_set = lax.axis_index("exp").astype(jnp.int32)
-    my_kv = lax.axis_index("kv").astype(jnp.int32)
-    my_seq = lax.axis_index("seq").astype(jnp.int32)
     kv_count = lax.axis_size("kv")
     seq_count = lax.axis_size("seq")
-    width = D // SETS
     weights = lax.all_gather(pack(gate_w, up_w, down_w), "exp")
-    partials = attention(
-        page_table.reshape(PPD), cache_lens, queries, parents, draft_kv, kv_pool
+    partials, out_proj = attention(
+        page_table.reshape(PPD), cache_lens, queries, parents, draft_kv, kv_pool, out_proj
     )
     parts = lax.all_to_all(partials, "exp", 0, 0, tiled=True)
     projected = merge(parts, out_proj)
     shares = lax.all_to_all(projected.reshape(SETS, TOK, D), "exp", 0, 0, tiled=True)
-    residual, row = norm(
-        my_set.reshape(1), shares, hidden, norm_gain.reshape(1, D), router, routes
-    )
+    residual, row = norm(shares, hidden, norm_gain.reshape(1, D), router, routes)
     rows = lax.all_gather(row, "seq").reshape(seq_count * TOK, WIDE)
-    place = jnp.stack([my_kv * seq_count + my_seq, my_kv, my_seq])
     arrived = {by: shifted(rows, "kv", kv_count, by) for by in range(1, kv_count)}
-    own, kept = own_expert(place, rows, weights)
-    near = other_expert(place, kept, arrived[1], arrived[kv_count - 1])
+    own, kept = own_expert(rows, weights)
+    near = other_expert(kept, arrived[1], arrived[kv_count - 1])
     parts = [
         own,
         shifted(near[0], "kv", kv_count, -1),
         shifted(near[1], "kv", kv_count, 1),
     ]
     for by in range(2, kv_count - 1):
-        (far,) = other_expert(place, kept, arrived[by])
+        (far,) = other_expert(kept, arrived[by])
         parts.append(shifted(far, "kv", kv_count, -by))
     run = 4
     far_count = seq_count // run
@@ -515,7 +544,7 @@
         ]
         for near in range(run)
     ]
-    back = join(place, residual, parts, run)
+    back = join(residual, parts, run)
     back = lax.all_to_all(back, "seq", 0, 0, tiled=True, axis_index_groups=runs)
     back = lax.all_to_all(
         fold(back), ("seq", "exp"), 0, 0, tiled=True, axis_index_groups=strides

time: 188 us -> 189 us (level)
  blocking collectives: 98.6 us -> 106 us
  local copies, waits for them, and re-layouts: 9.48 us -> 3.36 us
  Pallas kernels: 24.4 us -> 20.6 us
  waiting for transfers between devices: 18 us -> 21.7 us
    unnamed x16 -> x4, local copies, waits for them, and re-layouts: 8.79 us -> 2.67 us
    all_to_all x1, blocking collectives: 11.5 us -> 17.6 us  [local(): back = lax.all_to_all(back, 'seq', 0, 0, tiled=True, axis_index_groups=runs)]
    all_gather x1, waiting for transfers between devices: 0.01 us -> 5.31 us  [local(): weights = lax.all_gather(pack(gate_w, up_w, down_w), 'exp')]
    all_to_all x1, blocking collectives: 38.3 us -> 40.6 us  [local(): lax.all_to_all(fold(back), ('seq', 'exp'), 0, 0, tiled=True, axis_index_g...]
  transfers between devices with their start and end apart: 8 -> 8, of which waited for: 4 -> 4; matrix products, arithmetic and copies ran while one was open for 1% -> 1% of each run, Pallas kernels for 11% -> 9%
where the time goes in v5:
time: 189 us; the launch traced here: 188 us
  blocking collectives  106 us (56%)
  starting transfers between devices  22.6 us (12%)
  waiting for transfers between devices  21.7 us (11%)
  Pallas kernels  20.6 us (11%)
  between operations  14.2 us (8%)
  local copies, waits for them, and re-layouts  3.36 us (2%)
    all_to_all x1, blocking collectives, local(): lax.all_to_all(fold(back), ('seq', 'exp'), 0, 0, tiled=True, axis_index_g...  40.6 us
    all_gather x1, blocking collectives, local(): rows = lax.all_gather(row, 'seq').reshape(seq_count * TOK, WIDE)  31.2 us
    ppermute x6, starting transfers between devices, shifted(): lax.ppermute(value, axis, [(i, (i + by) % count) for i in range(count)])  18.7 us
    all_to_all x1, blocking collectives, local(): back = lax.all_to_all(back, 'seq', 0, 0, tiled=True, axis_index_groups=runs)  17.6 us
    all_to_all x1, blocking collectives, local(): parts = lax.all_to_all(partials, 'exp', 0, 0, tiled=True)  16.6 us
    ppermute x6, waiting for transfers between devices, shifted(): lax.ppermute(value, axis, [(i, (i + by) % count) for i in range(count)])  9.36 us
    all_to_all x1, waiting for transfers between devices, local(): lax.all_to_all(projected.reshape(SETS, TOK, D), 'exp', 0, 0, tiled=True)  7.04 us
    pallas_call x1, Pallas kernels, own_expert(): pl.pallas_call(own_kernel, out_shape=(pltpu.VMEM((count, D), jnp.bfloat16...  5.68 us
  transfers between devices with their start and end apart: 8, of which 4 were waited for; matrix products, arithmetic and copies ran while one was open for 1% of the time, Pallas kernels for 9%

profile of v5, /device:TPU:1, one launch (start us, length us, event | category | flops | bytes accessed | tf_op | source)
XLA Modules:
  0.0 188.4 jit_solution(14032236972313803611)
XLA Ops:
  6.5 2.4 %pack.1 = bf16[3072,256]{1,0:T(8,128)(2,1)} custom-call(bf16[1,2048,128]{2,1,0:T(8,128)(2,1)} %gate_ref.1, bf16[1,2048,128]{2,1,0:T(8,128)(2,1)} %up_ref.1, bf16[1,128,2048]{2,1,0:T(8,128)(2,1)} %down_ref.1), custom_call_target="tpu_custom_call" | custom-call | tf_op jit(solution)/shard_map/pack/pallas_call | solution.py:307
  10.2 3.7 %attention.1 = (bf16[8,72,256]{2,1,0:T(8,128)(2,1)S(1)}, bf16[256,2048]{1,0:T(8,128)(2,1)S(1)}) custom-call(s32[12]{0:T(128)S(1)} %bitcast.3, s32[1]{0:T(128)S(6)} %copy.17.lens, bf16[1,64,2048]{2,1,0:T(8,128)(2,1)} %q_hbm.1, s32[1,64]{1,0:T(1,128)} %parents_hbm.1, bf16[2,1,8,2048]{3,2,1,0:T(8,128)(2,1)} %draft_hbm.1, bf16[2,12,16,2048]{3,2,1,0:T(8,128)(2,1)} %pool_ref.1, ...), custom_call_target="tpu_custom_call" | custom-call | tf_op jit(solution)/shard_map/attention/pallas_call | solution.py:154
  14.0 16.6 %all_to_all.20.parts_ref = bf16[8,72,256]{2,1,0:T(8,128)(2,1)S(1)} all-to-all(bf16[8,72,256]{2,1,0:T(8,128)(2,1)S(1)} %get-tuple-element.13), channel_id=1, replica_groups=mesh['kv'=4,'seq'=16,'exp'=8] {'exp'}, dimensions={0} | all-to-all | bytes 589824 | tf_op jit(solution)/shard_map/all_to_all | solution.py:520
  30.5 1.3 merge.1
  31.9 3.9 %all-to-all-start.1 = ((bf16[8,8,2048]{2,1,0:T(8,128)(2,1)}), bf16[8,8,2048]{2,1,0:T(8,128)(2,1)S(1)}, u32[]{:S(2)}, u32[]{:S(2)}) async-start(bf16[8,8,2048]{2,1,0:T(8,128)(2,1)} %bitcast.1), calls=%async_computation.1 | async-start | bytes 524288 | tf_op jit(solution)/shard_map/all_to_all | solution.py:522
  36.4 1.2 copy.15.router_ref
  37.7 0.8 copy.16.routes_ref
  38.5 7.0 %all-to-all-done.1.parts_ref = bf16[8,8,2048]{2,1,0:T(8,128)(2,1)S(1)} async-done(((bf16[8,8,2048]{2,1,0:T(8,128)(2,1)}), bf16[8,8,2048]{2,1,0:T(8,128)(2,1)S(1)}, u32[]{:S(2)}, u32[]{:S(2)}) %all-to-all-start.1) | async-done | bytes 262176 | tf_op jit(solution)/shard_map/all_to_all | solution.py:522
  45.5 1.1 norm.1
  46.7 31.2 %all-gather.rows_ref = bf16[128,2176]{1,0:T(8,128)(2,1)S(1)} all-gather(bf16[8,2176]{1,0:T(8,128)(2,1)S(1)} %get-tuple-element.16), channel_id=2, replica_groups=mesh['kv'=4,'seq'=16,'exp'=8] {'seq'}, dimensions={0}, use_global_device_ids=true | all-gather | bytes 591872 | tf_op jit(solution)/shard_map/all_gather | solution.py:524
  77.8 3.1 %collective-permute-start = (bf16[128,2176]{1,0:T(8,128)(2,1)S(1)}, bf16[128,2176]{1,0:T(8,128)(2,1)S(1)}, u32[]{:S(2)}, u32[]{:S(2)}) collective-permute-start(bf16[128,2176]{1,0:T(8,128)(2,1)S(1)} %all-gather.rows_ref), channel_id=1, source_target_pairs={{0,128},{128,256},{256,384},{384,0},{1,129},{129,257},{257,385},{3... | collective-permute-start | bytes 1671176 | tf_op jit(solution)/shard_map/ppermute | solution.py:495
  80.9 3.4 %collective-permute-start.1 = (bf16[128,2176]{1,0:T(8,128)(2,1)S(1)}, bf16[128,2176]{1,0:T(8,128)(2,1)S(1)}, u32[]{:S(2)}, u32[]{:S(2)}) collective-permute-start(bf16[128,2176]{1,0:T(8,128)(2,1)S(1)} %all-gather.rows_ref), channel_id=1, source_target_pairs={{0,384},{128,0},{256,128},{384,256},{1,385},{129,1},{257,129},{385... | collective-permute-start | bytes 1671176 | tf_op jit(solution)/shard_map/ppermute | solution.py:495
  84.3 3.4 %collective-permute-start.4 = (bf16[128,2176]{1,0:T(8,128)(2,1)S(1)}, bf16[128,2176]{1,0:T(8,128)(2,1)S(1)}, u32[]{:S(2)}, u32[]{:S(2)}) collective-permute-start(bf16[128,2176]{1,0:T(8,128)(2,1)S(1)} %all-gather.rows_ref), channel_id=1, source_target_pairs={{0,256},{128,384},{256,0},{384,128},{1,257},{129,385},{257,1},{385... | collective-permute-start | bytes 1671176 | tf_op jit(solution)/shard_map/ppermute | solution.py:495
  87.8 5.3 %all-gather.4.cloned.1.call-done = bf16[24576,256]{1,0:T(8,128)(2,1)} async-done(((bf16[3072,256]{1,0:T(8,128)(2,1)}), bf16[24576,256]{1,0:T(8,128)(2,1)}) %all-gather.4.cloned.1.call-update) | async-done | bytes 12582928 | tf_op jit(solution)/shard_map/all_gather | solution.py:516
  93.1 5.7 %own_expert.1 = (bf16[128,2048]{1,0:T(8,128)(2,1)S(1)}, bf16[8,3072,256]{2,1,0:T(8,128)(2,1)S(1)}) custom-call(bf16[128,2176]{1,0:T(8,128)(2,1)S(1)} %all-gather.rows_ref, bf16[8,3072,256]{2,1,0:T(8,128)(2,1)} %bitcast.4), custom_call_target="tpu_custom_call" | custom-call | tf_op jit(solution)/shard_map/own_expert/pallas_call | solution.py:380
  98.8 3.5 %other_expert.2 = (bf16[128,2048]{1,0:T(8,128)(2,1)S(1)}, bf16[128,2048]{1,0:T(8,128)(2,1)S(1)}) custom-call(bf16[128,2176]{1,0:T(8,128)(2,1)S(1)} %collective-permute-done.refs_0_, bf16[128,2176]{1,0:T(8,128)(2,1)S(1)} %collective-permute-done.1.refs_1_, bf16[8,3072,256]{2,1,0:T(8,128)(2,1)S(1)} %get-tuple-element.18.refs_2_.refs_1_), custom_call_target="tpu_custom_call" | custom-call | tf_op jit(solution)/shard_map/other_expert/pallas_call | solution.py:400
  102.3 3.2 %collective-permute-start.2 = (bf16[128,2048]{1,0:T(8,128)(2,1)S(1)}, bf16[128,2048]{1,0:T(8,128)(2,1)S(1)}, u32[]{:S(2)}, u32[]{:S(2)}) collective-permute-start(bf16[128,2048]{1,0:T(8,128)(2,1)S(1)} %get-tuple-element.19), channel_id=1, source_target_pairs={{0,384},{128,0},{256,128},{384,256},{1,385},{129,1},{257,129},{385... | collective-permute-start | bytes 1572872 | tf_op jit(solution)/shard_map/ppermute | solution.py:495
  105.5 2.1 %collective-permute-start.3 = (bf16[128,2048]{1,0:T(8,128)(2,1)S(1)}, bf16[128,2048]{1,0:T(8,128)(2,1)S(1)}, u32[]{:S(2)}, u32[]{:S(2)}) collective-permute-start(bf16[128,2048]{1,0:T(8,128)(2,1)S(1)} %get-tuple-element.20), channel_id=1, source_target_pairs={{0,128},{128,256},{256,384},{384,0},{1,129},{129,257},{257,385},{3... | collective-permute-start | bytes 1572872 | tf_op jit(solution)/shard_map/ppermute | solution.py:495
  107.6 1.8 other_expert.3
  109.4 3.5 %collective-permute-start.5 = (bf16[128,2048]{1,0:T(8,128)(2,1)S(1)}, bf16[128,2048]{1,0:T(8,128)(2,1)S(1)}, u32[]{:S(2)}, u32[]{:S(2)}) collective-permute-start(bf16[128,2048]{1,0:T(8,128)(2,1)S(1)} %other_expert.3), channel_id=1, source_target_pairs={{0,256},{128,384},{256,0},{384,128},{1,257},{129,385},{257,1},{385... | collective-permute-start | bytes 1572872 | tf_op jit(solution)/shard_map/ppermute | solution.py:495
  112.9 1.9 collective-permute-done.2.refs_1_
  114.8 7.5 %collective-permute-done.3.refs_2_ = bf16[128,2048]{1,0:T(8,128)(2,1)S(1)} collective-permute-done((bf16[128,2048]{1,0:T(8,128)(2,1)S(1)}, bf16[128,2048]{1,0:T(8,128)(2,1)S(1)}, u32[]{:S(2)}, u32[]{:S(2)}) %collective-permute-start.3) | collective-permute-done | bytes 524320 | tf_op jit(solution)/shard_map/ppermute | solution.py:495
  122.6 17.6 %all_to_all.21.parts_ref = bf16[4,32,2048]{2,1,0:T(8,128)(2,1)S(1)} all-to-all(bf16[4,32,2048]{2,1,0:T(8,128)(2,1)S(1)} %join.1), channel_id=1, replica_groups={{0,8,16,24},{32,40,48,56},{64,72,80,88},{96,104,112,120},{1,9,17,25},{3..., dimensions={0} | all-to-all | bytes 1048576 | tf_op jit(solution)/shard_map/all_to_all | solution.py:548
  140.3 40.6 %all_to_all.22.parts_ref = bf16[32,8,256]{2,1,0:T(8,128)(2,1)S(1)} all-to-all(bf16[32,8,256]{2,1,0:T(8,128)(2,1)S(1)} %fold.1), channel_id=1, replica_groups={{0,1,2,3,4,5,6,7,32,33,34,35,36,37,38,39,64,65,66,67,68,69,70,71,96,97,..., dimensions={0} | all-to-all | bytes 262144 | tf_op jit(solution)/shard_map/all_to_all | solution.py:549
  (12 shorter events, 2.4 us)
Async XLA Ops:
  6.5 86.6 %all-gather.4.cloned.1.call-start = ((), (), s32[]{:S(2)}) async-start(), calls=%async_computation.4 | async-start | bytes 14155776 | tf_op jit(solution)/shard_map/all_gather | solution.py:516
  9.6 0.7 copy-start
  31.9 13.7 %all-to-all-start.1 = ((bf16[8,8,2048]{2,1,0:T(8,128)(2,1)}), bf16[8,8,2048]{2,1,0:T(8,128)(2,1)S(1)}, u32[]{:S(2)}, u32[]{:S(2)}) async-start(bf16[8,8,2048]{2,1,0:T(8,128)(2,1)} %bitcast.1), calls=%async_computation.1 | async-start | bytes 524288 | tf_op jit(solution)/shard_map/all_to_all | solution.py:522
  77.8 21.0 %collective-permute-start = (bf16[128,2176]{1,0:T(8,128)(2,1)S(1)}, bf16[128,2176]{1,0:T(8,128)(2,1)S(1)}, u32[]{:S(2)}, u32[]{:S(2)}) collective-permute-start(bf16[128,2176]{1,0:T(8,128)(2,1)S(1)} %all-gather.rows_ref), channel_id=1, source_target_pairs={{0,128},{128,256},{256,384},{384,0},{1,129},{129,257},{257,385},{3... | collective-permute-start | bytes 1671176 | tf_op jit(solution)/shard_map/ppermute | solution.py:495
  80.9 17.9 %collective-permute-start.1 = (bf16[128,2176]{1,0:T(8,128)(2,1)S(1)}, bf16[128,2176]{1,0:T(8,128)(2,1)S(1)}, u32[]{:S(2)}, u32[]{:S(2)}) collective-permute-start(bf16[128,2176]{1,0:T(8,128)(2,1)S(1)} %all-gather.rows_ref), channel_id=1, source_target_pairs={{0,384},{128,0},{256,128},{384,256},{1,385},{129,1},{257,129},{385... | collective-permute-start | bytes 1671176 | tf_op jit(solution)/shard_map/ppermute | solution.py:495
  84.3 23.3 %collective-permute-start.4 = (bf16[128,2176]{1,0:T(8,128)(2,1)S(1)}, bf16[128,2176]{1,0:T(8,128)(2,1)S(1)}, u32[]{:S(2)}, u32[]{:S(2)}) collective-permute-start(bf16[128,2176]{1,0:T(8,128)(2,1)S(1)} %all-gather.rows_ref), channel_id=1, source_target_pairs={{0,256},{128,384},{256,0},{384,128},{1,257},{129,385},{257,1},{385... | collective-permute-start | bytes 1671176 | tf_op jit(solution)/shard_map/ppermute | solution.py:495
  102.3 12.5 %collective-permute-start.2 = (bf16[128,2048]{1,0:T(8,128)(2,1)S(1)}, bf16[128,2048]{1,0:T(8,128)(2,1)S(1)}, u32[]{:S(2)}, u32[]{:S(2)}) collective-permute-start(bf16[128,2048]{1,0:T(8,128)(2,1)S(1)} %get-tuple-element.19), channel_id=1, source_target_pairs={{0,384},{128,0},{256,128},{384,256},{1,385},{129,1},{257,129},{385... | collective-permute-start | bytes 1572872 | tf_op jit(solution)/shard_map/ppermute | solution.py:495
  105.5 16.8 %collective-permute-start.3 = (bf16[128,2048]{1,0:T(8,128)(2,1)S(1)}, bf16[128,2048]{1,0:T(8,128)(2,1)S(1)}, u32[]{:S(2)}, u32[]{:S(2)}) collective-permute-start(bf16[128,2048]{1,0:T(8,128)(2,1)S(1)} %get-tuple-element.20), channel_id=1, source_target_pairs={{0,128},{128,256},{256,384},{384,0},{1,129},{129,257},{257,385},{3... | collective-permute-start | bytes 1572872 | tf_op jit(solution)/shard_map/ppermute | solution.py:495
  109.4 12.8 %collective-permute-start.5 = (bf16[128,2048]{1,0:T(8,128)(2,1)S(1)}, bf16[128,2048]{1,0:T(8,128)(2,1)S(1)}, u32[]{:S(2)}, u32[]{:S(2)}) collective-permute-start(bf16[128,2048]{1,0:T(8,128)(2,1)S(1)} %other_expert.3), channel_id=1, source_target_pairs={{0,256},{128,384},{256,0},{384,128},{1,257},{129,385},{257,1},{385... | collective-permute-start | bytes 1572872 | tf_op jit(solution)/shard_map/ppermute | solution.py:495
Sparse Core Ops, SparseCore 0:
  9.5 83.5 all-gather.3

commit v6 on v5

--- a/solution.py
+++ b/solution.py
@@ -58,13 +58,17 @@
     draft_hbm,
     pool_ref,
     proj_ref,
+    routes_hbm,
     out_ref,
     kept_ref,
+    chosen_ref,
     kbuf,
     vbuf,
     q_ref,
     draft_ref,
     parents_ref,
+    routes_ref,
+    mask_ref,
     seen_ref,
     score_ref,
     weight_ref,
@@ -81,7 +85,8 @@
     draft_copy = pltpu.make_async_copy(draft_hbm.at[:, 0], draft_ref, more_sems.at[1])
     proj_copy = pltpu.make_async_copy(proj_ref, kept_ref, more_sems.at[2])
     parents_copy = pltpu.make_async_copy(parents_hbm, parents_ref, more_sems.at[3])
-    for copy in [parents_copy, draft_copy, query_copy] + keys + values + [proj_copy]:
+    routes_copy = pltpu.make_async_copy(routes_hbm.at[0], routes_ref, more_sems.at[4])
+    for copy in [parents_copy, routes_copy, draft_copy, query_copy] + keys + values + [proj_copy]:
         copy.start()
     length = lens[0]
     my_set = lax.axis_index("exp")
@@ -105,6 +110,13 @@
         lax.broadcasted_iota(jnp.int32, (2 * DRAFT, 2 * HD), 1) < HD
     )
     stat_row = lax.broadcasted_iota(jnp.int32, (8, 2 * DRAFT), 0)
+    routes_copy.wait()
+    expert = lax.broadcasted_iota(jnp.int32, (EXPERTS, DRAFT), 0)
+    chosen = routes_ref[0:1, :] == expert
+    for pick in range(1, TOPK):
+        chosen = chosen | (routes_ref[pick : pick + 1, :] == expert)
+    mask_ref[...] = jnp.transpose(jnp.where(chosen, 1.0, 0.0))
+    chosen_ref[...] = mask_ref[pl.ds(pl.multiple_of(my_set * TOK, TOK), TOK), :]
     pad = jnp.zeros((8, D), jnp.float32)
     draft_copy.wait()
     for place, buf in ((0, kbuf), (1, vbuf)):
@@ -143,37 +155,40 @@
     proj_copy.wait()
 
 
-def attention(table, lens, queries, parents, draft_kv, kv_pool, out_proj):
+def attention(table, lens, queries, parents, draft_kv, kv_pool, out_proj, routes):
     smem = pl.BlockSpec(memory_space=pltpu.SMEM)
     vmem = pl.BlockSpec(memory_space=pltpu.VMEM)
     hbm = pl.BlockSpec(memory_space=pltpu.HBM)
-    queries, parents, draft_kv, kv_pool, out_proj = (
+    queries, parents, draft_kv, kv_pool, out_proj, routes = (
         pltpu.with_memory_space_constraint(x, pltpu.HBM)
-        for x in (queries, parents, draft_kv, kv_pool, out_proj)
+        for x in (queries, parents, draft_kv, kv_pool, out_proj, routes)
     )
     return pl.pallas_call(
         attention_kernel,
         out_shape=(
             jax.ShapeDtypeStruct((SETS, STAT, 2 * HD), jnp.bfloat16),
             pltpu.VMEM(out_proj.shape, out_proj.dtype),
+            pltpu.VMEM((TOK, EXPERTS), jnp.float32),
         ),
-        in_specs=[smem, smem, hbm, hbm, hbm, hbm, hbm],
-        out_specs=(vmem, vmem),
+        in_specs=[smem, smem, hbm, hbm, hbm, hbm, hbm, hbm],
+        out_specs=(vmem, vmem, vmem),
         scratch_shapes=[
             pltpu.VMEM((ROWS, D), jnp.bfloat16),
             pltpu.VMEM((ROWS, D), jnp.bfloat16),
             pltpu.VMEM((DRAFT, D), jnp.bfloat16),
             pltpu.VMEM((2, TOK, D), jnp.bfloat16),
             pltpu.VMEM((1, DRAFT), jnp.int32),
+            pltpu.VMEM((TOPK, DRAFT), jnp.int32),
+            pltpu.VMEM((DRAFT, EXPERTS), jnp.float32),
             pltpu.VMEM((ROWS, 2 * DRAFT), jnp.float32),
             pltpu.VMEM((H // 2, ROWS, 2 * DRAFT), jnp.float32),
             pltpu.VMEM((H // 2, ROWS, 2 * DRAFT), jnp.bfloat16),
             pltpu.SemaphoreType.DMA((2, PPD)),
-            pltpu.SemaphoreType.DMA((4,)),
+            pltpu.SemaphoreType.DMA((5,)),
         ],
         compiler_params=pltpu.CompilerParams(vmem_limit_bytes=VMEM_LIMIT),
         name="attention",
-    )(table, lens, queries, parents, draft_kv, kv_pool, out_proj)
+    )(table, lens, queries, parents, draft_kv, kv_pool, out_proj, routes)
 
 
 def merge_kernel(parts_ref, proj_ref, out_ref):
@@ -203,51 +218,66 @@
 
 
 def norm_kernel(
-    parts_ref, hidden_ref, gain_ref, router_ref, routes_ref, residual_ref, row_ref, own_ref, sem
+    parts_ref,
+    hidden_ref,
+    gain_hbm,
+    router_hbm,
+    chosen_ref,
+    residual_ref,
+    row_ref,
+    own_ref,
+    gain_ref,
+    router_ref,
+    sems,
 ):
     mine = pl.ds(pl.multiple_of(lax.axis_index("exp") * TOK, TOK), TOK)
-    copy = pltpu.make_async_copy(hidden_ref.at[0, mine], own_ref, sem)
-    copy.start()
+    copies = [
+        pltpu.make_async_copy(hidden_ref.at[0, mine], own_ref, sems.at[0]),
+        pltpu.make_async_copy(gain_hbm, gain_ref, sems.at[1]),
+        pltpu.make_async_copy(router_hbm, router_ref, sems.at[2]),
+    ]
+    for copy in copies:
+        copy.start()
     residual = parts_ref[0].astype(jnp.float32)
     for source in range(1, SETS):
         residual = residual + parts_ref[source].astype(jnp.float32)
-    expert = lax.broadcasted_iota(jnp.int32, (TOK, EXPERTS), 1)
-    routes = routes_ref[0, mine, :]
-    chosen = routes[:, 0:1] == expert
-    for pick in range(1, TOPK):
-        chosen = chosen | (routes[:, pick : pick + 1] == expert)
-    copy.wait()
+    for copy in copies:
+        copy.wait()
     residual = own_ref[...].astype(jnp.float32) + residual
     residual_ref[...] = residual
     mean_sq = jnp.mean(residual * residual, axis=1, keepdims=True)
-    normed = (residual * lax.rsqrt(mean_sq + EPS_NORM) * gain_ref[...].astype(jnp.float32)).astype(
-        jnp.bfloat16
-    )
-    logits = nn(normed, router_ref[...])
-    gates = jnp.where(chosen, 1.0 / (1.0 + jnp.exp(-logits)), 0.0)
+    gain = gain_ref[...].astype(jnp.float32).reshape(1, D)
+    normed = (residual * lax.rsqrt(mean_sq + EPS_NORM) * gain).astype(jnp.bfloat16)
+    logits = nt(normed, router_ref[...])
+    gates = jnp.where(chosen_ref[...] > 0.5, 1.0 / (1.0 + jnp.exp(-logits)), 0.0)
     high = gates.astype(jnp.bfloat16).astype(jnp.float32)
     row_ref[:, 0:D] = normed
     row_ref[:, D:WIDE] = jnp.concatenate([high, gates - high], axis=1).astype(jnp.bfloat16)
 
 
-def norm(parts, hidden, norm_gain, router, routes):
-    vmem = pl.BlockSpec(memory_space=pltpu.VMEM)
+def norm(parts, hidden, norm_gain, router, chosen):
+    vmem = pl.BlockSpec(memory_space=pltpu.VMEM)
+    hbm = pl.BlockSpec(memory_space=pltpu.HBM)
+    held = [
+        pltpu.with_memory_space_constraint(x, pltpu.HBM) for x in (hidden, norm_gain, router)
+    ]
     return pl.pallas_call(
         norm_kernel,
         out_shape=(
             pltpu.VMEM((TOK, D), jnp.float32),
             jax.ShapeDtypeStruct((TOK, WIDE), jnp.bfloat16),
         ),
-        in_specs=[vmem, pl.BlockSpec(memory_space=pltpu.HBM), vmem, vmem, vmem],
+        in_specs=[vmem, hbm, hbm, hbm, vmem],
         out_specs=(vmem, vmem),
-        scratch_shapes=[pltpu.VMEM((TOK, D), jnp.bfloat16), pltpu.SemaphoreType.DMA],
+        scratch_shapes=[
+            pltpu.VMEM((TOK, D), jnp.bfloat16),
+            pltpu.VMEM(norm_gain.shape, jnp.bfloat16),
+            pltpu.VMEM((EXPERTS, D), jnp.bfloat16),
+            pltpu.SemaphoreType.DMA((3,)),
+        ],
         compiler_params=pltpu.CompilerParams(vmem_limit_bytes=VMEM_LIMIT),
         name="norm",
-    )(
-        *in_vmem(parts),
-        pltpu.with_memory_space_constraint(hidden, pltpu.HBM),
-        *in_vmem(norm_gain, router, routes),
-    )
+    )(*in_vmem(parts), *held, *in_vmem(chosen))
 
 
 def pack_kernel(gate_ref, up_ref, down_ref, out_ref, buf, in_sems, out_sems):
@@ -417,7 +447,8 @@
 
 def join_kernel(residual_ref, *refs):
     parts_refs, out_ref, work_ref = refs[:-2], refs[-2], refs[-1]
-    near = out_ref.shape[0]
+    near = out_ref.shape[0] // SETS
+    width = out_ref.shape[2]
     rows = work_ref.shape[0]
     step = 2 * TOK
     for start in range(0, rows, step):
@@ -426,9 +457,10 @@
     work_ref[mine, :] = work_ref[mine, :] + residual_ref[...]
     for seq in range(rows // TOK):
         far = seq // near
-        out_ref[seq % near, far * TOK : (far + 1) * TOK, :] = work_ref[
-            seq * TOK : (seq + 1) * TOK, :
-        ].astype(jnp.bfloat16)
+        for block in range(SETS):
+            out_ref[(seq % near) * SETS + block, far * TOK : (far + 1) * TOK, :] = work_ref[
+                seq * TOK : (seq + 1) * TOK, block * width : (block + 1) * width
+            ].astype(jnp.bfloat16)
 
 
 def join(residual, parts, near):
@@ -436,7 +468,7 @@
     vmem = pl.BlockSpec(memory_space=pltpu.VMEM)
     return pl.pallas_call(
         join_kernel,
-        out_shape=pltpu.VMEM((near, rows // near, D), jnp.bfloat16),
+        out_shape=pltpu.VMEM((near * SETS, rows // near, D // SETS), jnp.bfloat16),
         in_specs=[vmem] * (len(parts) + 1),
         out_specs=vmem,
         scratch_shapes=[pltpu.VMEM((rows, D), jnp.float32)],
@@ -446,24 +478,20 @@
 
 
 def fold_kernel(parts_ref, out_ref):
-    width = D // SETS
-    for far in range(parts_ref.shape[1] // TOK):
-        for block in range(SETS):
-            cols = slice(block * width, (block + 1) * width)
-            total = parts_ref[0, far * TOK : (far + 1) * TOK, cols].astype(jnp.float32)
-            for source in range(1, parts_ref.shape[0]):
-                total = total + parts_ref[
-                    source, far * TOK : (far + 1) * TOK, cols
-                ].astype(jnp.float32)
-            out_ref[far * SETS + block] = total.astype(jnp.bfloat16)
+    for source in range(SETS):
+        total = summed([parts_ref.at[near * SETS + source] for near in range(parts_ref.shape[0] // SETS)], ...)
+        total = total.astype(jnp.bfloat16)
+        for far in range(out_ref.shape[0]):
+            out_ref[far, source * TOK : (source + 1) * TOK, :] = total[
+                far * TOK : (far + 1) * TOK, :
+            ]
 
 
 def fold(parts):
-    far = parts.shape[1] // TOK
     vmem = pl.BlockSpec(memory_space=pltpu.VMEM)
     return pl.pallas_call(
         fold_kernel,
-        out_shape=pltpu.VMEM((far * SETS, TOK, D // SETS), parts.dtype),
+        out_shape=pltpu.VMEM((parts.shape[1] // TOK, DRAFT, parts.shape[2]), parts.dtype),
         in_specs=[vmem],
         out_specs=vmem,
         compiler_params=pltpu.CompilerParams(vmem_limit_bytes=VMEM_LIMIT),
@@ -472,18 +500,15 @@
 
 
 def total_kernel(parts_ref, out_ref):
-    for source in range(SETS):
-        total = parts_ref[source].astype(jnp.float32)
-        for far in range(1, parts_ref.shape[0] // SETS):
-            total = total + parts_ref[far * SETS + source].astype(jnp.float32)
-        out_ref[0, source * TOK : (source + 1) * TOK, :] = total.astype(jnp.bfloat16)
+    total = summed([parts_ref.at[far] for far in range(parts_ref.shape[0])], ...)
+    out_ref[0] = total.astype(jnp.bfloat16)
 
 
 def total(parts):
     vmem = pl.BlockSpec(memory_space=pltpu.VMEM)
     return pl.pallas_call(
         total_kernel,
-        out_shape=jax.ShapeDtypeStruct((1, DRAFT, parts.shape[2]), parts.dtype),
+        out_shape=jax.ShapeDtypeStruct((1,) + parts.shape[1:], parts.dtype),
         in_specs=[vmem],
         out_specs=vmem,
         compiler_params=pltpu.CompilerParams(vmem_limit_bytes=VMEM_LIMIT),
@@ -514,13 +539,20 @@
     kv_count = lax.axis_size("kv")
     seq_count = lax.axis_size("seq")
     weights = lax.all_gather(pack(gate_w, up_w, down_w), "exp")
-    partials, out_proj = attention(
-        page_table.reshape(PPD), cache_lens, queries, parents, draft_kv, kv_pool, out_proj
+    partials, out_proj, chosen = attention(
+        page_table.reshape(PPD),
+        cache_lens,
+        queries,
+        parents,
+        draft_kv,
+        kv_pool,
+        out_proj,
+        jnp.transpose(routes, (0, 2, 1)),
     )
     parts = lax.all_to_all(partials, "exp", 0, 0, tiled=True)
     projected = merge(parts, out_proj)
     shares = lax.all_to_all(projected.reshape(SETS, TOK, D), "exp", 0, 0, tiled=True)
-    residual, row = norm(shares, hidden, norm_gain.reshape(1, D), router, routes)
+    residual, row = norm(shares, hidden, norm_gain, jnp.transpose(router), chosen)
     rows = lax.all_gather(row, "seq").reshape(seq_count * TOK, WIDE)
     arrived = {by: shifted(rows, "kv", kv_count, by) for by in range(1, kv_count)}
     own, kept = own_expert(rows, weights)
@@ -535,20 +567,14 @@
         parts.append(shifted(far, "kv", kv_count, -by))
     run = 4
     far_count = seq_count // run
-    runs = [[far * run + near for near in range(run)] for far in range(far_count)]
-    strides = [
-        [
-            (far * run + near) * SETS + block
-            for far in range(far_count)
-            for block in range(SETS)
-        ]
-        for near in range(run)
+    runs = [
+        [(far * run + near) * SETS + block for near in range(run) for block in range(SETS)]
+        for far in range(far_count)
     ]
+    strides = [[far * run + near for far in range(far_count)] for near in range(run)]
     back = join(residual, parts, run)
-    back = lax.all_to_all(back, "seq", 0, 0, tiled=True, axis_index_groups=runs)
-    back = lax.all_to_all(
-        fold(back), ("seq", "exp"), 0, 0, tiled=True, axis_index_groups=strides
-    )
+    back = lax.all_to_all(back, ("seq", "exp"), 0, 0, tiled=True, axis_index_groups=runs)
+    back = lax.all_to_all(fold(back), "seq", 0, 0, tiled=True, axis_index_groups=strides)
     return total(back)
 
 

time: 189 us -> 189 us (level)
  blocking collectives: 106 us -> 119 us
  waiting for transfers between devices: 21.7 us -> 16.4 us
  starting transfers between devices: 22.6 us -> 17.4 us
  local copies, waits for them, and re-layouts: 3.36 us -> 0.65 us
    all_to_all x2 -> x3, blocking collectives: 58.2 us -> 70.9 us  [the longest x1 34.1 us: local(): lax.all_to_all(back, ('seq', 'exp'), 0, 0, tiled=True, axis_index_groups=...]
    all_to_all x1 -> x0, waiting for transfers between devices: 7.04 us -> none  [local(): lax.all_to_all(projected.reshape(SETS, TOK, D), 'exp', 0, 0, tiled=True)]
    all_to_all x1 -> x0, starting transfers between devices: 3.89 us -> none  [local(): lax.all_to_all(projected.reshape(SETS, TOK, D), 'exp', 0, 0, tiled=True)]
    unnamed x4 -> x2, local copies, waits for them, and re-layouts: 2.67 us -> 0.65 us
  transfers between devices with their start and end apart: 8 -> 7, of which waited for: 4 -> 4; matrix products, arithmetic and copies ran while one was open for 1% -> 0% of each run, Pallas kernels for 9% -> 9%
where the time goes in v6:
time: 189 us; the launch traced here: 188 us
  blocking collectives  119 us (63%)
  Pallas kernels  20.2 us (11%)
  starting transfers between devices  17.4 us (9%)
  waiting for transfers between devices  16.4 us (9%)
  between operations  14.2 us (8%)
    all_to_all x1, blocking collectives, local(): lax.all_to_all(back, ('seq', 'exp'), 0, 0, tiled=True, axis_index_groups=...  34.1 us
    all_gather x1, blocking collectives, local(): rows = lax.all_gather(row, 'seq').reshape(seq_count * TOK, WIDE)  31.5 us
    all_to_all x1, blocking collectives, local(): lax.all_to_all(fold(back), 'seq', 0, 0, tiled=True, axis_index_groups=str...  24.4 us
    ppermute x6, starting transfers between devices, shifted(): lax.ppermute(value, axis, [(i, (i + by) % count) for i in range(count)])  17.4 us
    all_to_all x1, blocking collectives, local(): parts = lax.all_to_all(partials, 'exp', 0, 0, tiled=True)  16.6 us
    all_to_all x1, blocking collectives, local(): lax.all_to_all(projected.reshape(SETS, TOK, D), 'exp', 0, 0, tiled=True)  12.3 us
    ppermute x6, waiting for transfers between devices, shifted(): lax.ppermute(value, axis, [(i, (i + by) % count) for i in range(count)])  9.75 us
    all_gather x1, waiting for transfers between devices, local(): weights = lax.all_gather(pack(gate_w, up_w, down_w), 'exp')  6.63 us
  transfers between devices with their start and end apart: 7, of which 4 were waited for; matrix products, arithmetic and copies ran while one was open for 0% of the time, Pallas kernels for 9%

profile of v6, /device:TPU:1, one launch (start us, length us, event | category | flops | bytes accessed | tf_op | source)
XLA Modules:
  0.0 187.9 jit_solution(9026322353919226521)
XLA Ops:
  6.5 2.4 %pack.1 = bf16[3072,256]{1,0:T(8,128)(2,1)} custom-call(bf16[1,2048,128]{2,1,0:T(8,128)(2,1)} %gate_ref.1, bf16[1,2048,128]{2,1,0:T(8,128)(2,1)} %up_ref.1, bf16[1,128,2048]{2,1,0:T(8,128)(2,1)} %down_ref.1), custom_call_target="tpu_custom_call" | custom-call | tf_op jit(solution)/shard_map/pack/pallas_call | solution.py:337
  9.6 0.6 copy-done
  10.2 3.8 %attention.1 = (bf16[8,72,256]{2,1,0:T(8,128)(2,1)S(1)}, bf16[256,2048]{1,0:T(8,128)(2,1)S(1)}, f32[8,64]{1,0:T(8,128)S(1)}) custom-call(s32[12]{0:T(128)S(1)} %bitcast.6, s32[1]{0:T(128)S(6)} %copy.15.lens, bf16[1,64,2048]{2,1,0:T(8,128)(2,1)} %q_hbm.1, s32[1,64]{1,0:T(1,128)} %parents_hbm.1, bf16[2,1,8,2048]{3,2,1,0:T(8,128)(2,1)} %draft_hbm.1, ...), custom_call_target="tpu_custom_call" | custom-call | tf_op jit(solution)/shard_map/attention/pallas_call | solution.py:166
  14.1 16.6 %all_to_all.20.parts_ref = bf16[8,72,256]{2,1,0:T(8,128)(2,1)S(1)} all-to-all(bf16[8,72,256]{2,1,0:T(8,128)(2,1)S(1)} %get-tuple-element.14), channel_id=1, replica_groups=mesh['kv'=4,'seq'=16,'exp'=8] {'exp'}, dimensions={0} | all-to-all | bytes 589824 | tf_op jit(solution)/shard_map/all_to_all | solution.py:552
  30.6 0.6 merge.1
  31.3 12.3 %all_to_all.21.parts_ref = bf16[8,8,2048]{2,1,0:T(8,128)(2,1)S(1)} all-to-all(bf16[8,8,2048]{2,1,0:T(8,128)(2,1)S(1)} %bitcast.5), channel_id=1, replica_groups=mesh['kv'=4,'seq'=16,'exp'=8] {'exp'}, dimensions={0} | all-to-all | bytes 524288 | tf_op jit(solution)/shard_map/all_to_all | solution.py:554
  43.6 1.4 norm.1
  45.0 31.5 %all-gather.rows_ref = bf16[128,2176]{1,0:T(8,128)(2,1)S(1)} all-gather(bf16[8,2176]{1,0:T(8,128)(2,1)S(1)} %get-tuple-element.18), channel_id=2, replica_groups=mesh['kv'=4,'seq'=16,'exp'=8] {'seq'}, dimensions={0}, use_global_device_ids=true | all-gather | bytes 591872 | tf_op jit(solution)/shard_map/all_gather | solution.py:556
  76.5 3.1 %collective-permute-start = (bf16[128,2176]{1,0:T(8,128)(2,1)S(1)}, bf16[128,2176]{1,0:T(8,128)(2,1)S(1)}, u32[]{:S(2)}, u32[]{:S(2)}) collective-permute-start(bf16[128,2176]{1,0:T(8,128)(2,1)S(1)} %all-gather.rows_ref), channel_id=1, source_target_pairs={{0,128},{128,256},{256,384},{384,0},{1,129},{129,257},{257,385},{3... | collective-permute-start | bytes 1671176 | tf_op jit(solution)/shard_map/ppermute | solution.py:520
  79.6 3.4 %collective-permute-start.1 = (bf16[128,2176]{1,0:T(8,128)(2,1)S(1)}, bf16[128,2176]{1,0:T(8,128)(2,1)S(1)}, u32[]{:S(2)}, u32[]{:S(2)}) collective-permute-start(bf16[128,2176]{1,0:T(8,128)(2,1)S(1)} %all-gather.rows_ref), channel_id=1, source_target_pairs={{0,384},{128,0},{256,128},{384,256},{1,385},{129,1},{257,129},{385... | collective-permute-start | bytes 1671176 | tf_op jit(solution)/shard_map/ppermute | solution.py:520
  83.0 3.4 %collective-permute-start.4 = (bf16[128,2176]{1,0:T(8,128)(2,1)S(1)}, bf16[128,2176]{1,0:T(8,128)(2,1)S(1)}, u32[]{:S(2)}, u32[]{:S(2)}) collective-permute-start(bf16[128,2176]{1,0:T(8,128)(2,1)S(1)} %all-gather.rows_ref), channel_id=1, source_target_pairs={{0,256},{128,384},{256,0},{384,128},{1,257},{129,385},{257,1},{385... | collective-permute-start | bytes 1671176 | tf_op jit(solution)/shard_map/ppermute | solution.py:520
  86.5 6.6 %all-gather.4.cloned.1.call-done = bf16[24576,256]{1,0:T(8,128)(2,1)} async-done(((bf16[3072,256]{1,0:T(8,128)(2,1)}), bf16[24576,256]{1,0:T(8,128)(2,1)}) %all-gather.4.cloned.1.call-update) | async-done | bytes 12582928 | tf_op jit(solution)/shard_map/all_gather | solution.py:541
  93.1 5.7 %own_expert.1 = (bf16[128,2048]{1,0:T(8,128)(2,1)S(1)}, bf16[8,3072,256]{2,1,0:T(8,128)(2,1)S(1)}) custom-call(bf16[128,2176]{1,0:T(8,128)(2,1)S(1)} %all-gather.rows_ref, bf16[8,3072,256]{2,1,0:T(8,128)(2,1)} %bitcast.7), custom_call_target="tpu_custom_call" | custom-call | tf_op jit(solution)/shard_map/own_expert/pallas_call | solution.py:410
  98.8 3.5 %other_expert.2 = (bf16[128,2048]{1,0:T(8,128)(2,1)S(1)}, bf16[128,2048]{1,0:T(8,128)(2,1)S(1)}) custom-call(bf16[128,2176]{1,0:T(8,128)(2,1)S(1)} %collective-permute-done.refs_0_, bf16[128,2176]{1,0:T(8,128)(2,1)S(1)} %collective-permute-done.1.refs_1_, bf16[8,3072,256]{2,1,0:T(8,128)(2,1)S(1)} %get-tuple-element.20.refs_2_.refs_1_), custom_call_target="tpu_custom_call" | custom-call | tf_op jit(solution)/shard_map/other_expert/pallas_call | solution.py:430
  102.3 1.9 %collective-permute-start.2 = (bf16[128,2048]{1,0:T(8,128)(2,1)S(1)}, bf16[128,2048]{1,0:T(8,128)(2,1)S(1)}, u32[]{:S(2)}, u32[]{:S(2)}) collective-permute-start(bf16[128,2048]{1,0:T(8,128)(2,1)S(1)} %get-tuple-element.21), channel_id=1, source_target_pairs={{0,384},{128,0},{256,128},{384,256},{1,385},{129,1},{257,129},{385... | collective-permute-start | bytes 1572872 | tf_op jit(solution)/shard_map/ppermute | solution.py:520
  104.2 3.4 %collective-permute-start.3 = (bf16[128,2048]{1,0:T(8,128)(2,1)S(1)}, bf16[128,2048]{1,0:T(8,128)(2,1)S(1)}, u32[]{:S(2)}, u32[]{:S(2)}) collective-permute-start(bf16[128,2048]{1,0:T(8,128)(2,1)S(1)} %get-tuple-element.22), channel_id=1, source_target_pairs={{0,128},{128,256},{256,384},{384,0},{1,129},{129,257},{257,385},{3... | collective-permute-start | bytes 1572872 | tf_op jit(solution)/shard_map/ppermute | solution.py:520
  107.6 1.8 other_expert.3
  109.4 2.2 %collective-permute-start.5 = (bf16[128,2048]{1,0:T(8,128)(2,1)S(1)}, bf16[128,2048]{1,0:T(8,128)(2,1)S(1)}, u32[]{:S(2)}, u32[]{:S(2)}) collective-permute-start(bf16[128,2048]{1,0:T(8,128)(2,1)S(1)} %other_expert.3), channel_id=1, source_target_pairs={{0,256},{128,384},{256,0},{384,128},{1,257},{129,385},{257,1},{385... | collective-permute-start | bytes 1572872 | tf_op jit(solution)/shard_map/ppermute | solution.py:520
  111.6 1.8 collective-permute-done.2.refs_1_
  113.5 7.1 %collective-permute-done.3.refs_2_ = bf16[128,2048]{1,0:T(8,128)(2,1)S(1)} collective-permute-done((bf16[128,2048]{1,0:T(8,128)(2,1)S(1)}, bf16[128,2048]{1,0:T(8,128)(2,1)S(1)}, u32[]{:S(2)}, u32[]{:S(2)}) %collective-permute-start.3) | collective-permute-done | bytes 524320 | tf_op jit(solution)/shard_map/ppermute | solution.py:520
  120.6 0.8 collective-permute-done.5.refs_3_
  121.8 34.1 %all_to_all.22.parts_ref = bf16[32,32,256]{2,1,0:T(8,128)(2,1)S(1)} all-to-all(bf16[32,32,256]{2,1,0:T(8,128)(2,1)S(1)} %join.1), channel_id=1, replica_groups={{0,1,2,3,4,5,6,7,8,9,10,11,12,13,14,15,16,17,18,19,20,21,22,23,24,25,26..., dimensions={0} | all-to-all | bytes 1048576 | tf_op jit(solution)/shard_map/all_to_all | solution.py:576
  155.9 24.4 %all_to_all.23.parts_ref = bf16[4,64,256]{2,1,0:T(8,128)(2,1)S(1)} all-to-all(bf16[4,64,256]{2,1,0:T(8,128)(2,1)S(1)} %fold.1), channel_id=1, replica_groups={{0,32,64,96},{8,40,72,104},{16,48,80,112},{24,56,88,120},{1,33,65,97},{..., dimensions={0} | all-to-all | bytes 262144 | tf_op jit(solution)/shard_map/all_to_all | solution.py:577
  180.4 0.6 total.1
  (8 shorter events, 0.5 us)
Async XLA Ops:
  6.5 86.6 %all-gather.4.cloned.1.call-start = ((), (), s32[]{:S(2)}) async-start(), calls=%async_computation.4 | async-start | bytes 14155776 | tf_op jit(solution)/shard_map/all_gather | solution.py:541
  9.6 0.7 copy-start
  76.5 22.3 %collective-permute-start = (bf16[128,2176]{1,0:T(8,128)(2,1)S(1)}, bf16[128,2176]{1,0:T(8,128)(2,1)S(1)}, u32[]{:S(2)}, u32[]{:S(2)}) collective-permute-start(bf16[128,2176]{1,0:T(8,128)(2,1)S(1)} %all-gather.rows_ref), channel_id=1, source_target_pairs={{0,128},{128,256},{256,384},{384,0},{1,129},{129,257},{257,385},{3... | collective-permute-start | bytes 1671176 | tf_op jit(solution)/shard_map/ppermute | solution.py:520
  79.6 19.2 %collective-permute-start.1 = (bf16[128,2176]{1,0:T(8,128)(2,1)S(1)}, bf16[128,2176]{1,0:T(8,128)(2,1)S(1)}, u32[]{:S(2)}, u32[]{:S(2)}) collective-permute-start(bf16[128,2176]{1,0:T(8,128)(2,1)S(1)} %all-gather.rows_ref), channel_id=1, source_target_pairs={{0,384},{128,0},{256,128},{384,256},{1,385},{129,1},{257,129},{385... | collective-permute-start | bytes 1671176 | tf_op jit(solution)/shard_map/ppermute | solution.py:520
  83.0 24.6 %collective-permute-start.4 = (bf16[128,2176]{1,0:T(8,128)(2,1)S(1)}, bf16[128,2176]{1,0:T(8,128)(2,1)S(1)}, u32[]{:S(2)}, u32[]{:S(2)}) collective-permute-start(bf16[128,2176]{1,0:T(8,128)(2,1)S(1)} %all-gather.rows_ref), channel_id=1, source_target_pairs={{0,256},{128,384},{256,0},{384,128},{1,257},{129,385},{257,1},{385... | collective-permute-start | bytes 1671176 | tf_op jit(solution)/shard_map/ppermute | solution.py:520
  102.3 11.2 %collective-permute-start.2 = (bf16[128,2048]{1,0:T(8,128)(2,1)S(1)}, bf16[128,2048]{1,0:T(8,128)(2,1)S(1)}, u32[]{:S(2)}, u32[]{:S(2)}) collective-permute-start(bf16[128,2048]{1,0:T(8,128)(2,1)S(1)} %get-tuple-element.21), channel_id=1, source_target_pairs={{0,384},{128,0},{256,128},{384,256},{1,385},{129,1},{257,129},{385... | collective-permute-start | bytes 1572872 | tf_op jit(solution)/shard_map/ppermute | solution.py:520
  104.2 16.3 %collective-permute-start.3 = (bf16[128,2048]{1,0:T(8,128)(2,1)S(1)}, bf16[128,2048]{1,0:T(8,128)(2,1)S(1)}, u32[]{:S(2)}, u32[]{:S(2)}) collective-permute-start(bf16[128,2048]{1,0:T(8,128)(2,1)S(1)} %get-tuple-element.22), channel_id=1, source_target_pairs={{0,128},{128,256},{256,384},{384,0},{1,129},{129,257},{257,385},{3... | collective-permute-start | bytes 1572872 | tf_op jit(solution)/shard_map/ppermute | solution.py:520
  109.4 11.9 %collective-permute-start.5 = (bf16[128,2048]{1,0:T(8,128)(2,1)S(1)}, bf16[128,2048]{1,0:T(8,128)(2,1)S(1)}, u32[]{:S(2)}, u32[]{:S(2)}) collective-permute-start(bf16[128,2048]{1,0:T(8,128)(2,1)S(1)} %other_expert.3), channel_id=1, source_target_pairs={{0,256},{128,384},{256,0},{384,128},{1,257},{129,385},{257,1},{385... | collective-permute-start | bytes 1572872 | tf_op jit(solution)/shard_map/ppermute | solution.py:520
Sparse Core Ops, SparseCore 0:
  9.5 83.5 all-gather.3

commit v7 on v6

--- a/solution.py
+++ b/solution.py
@@ -447,8 +447,7 @@
 
 def join_kernel(residual_ref, *refs):
     parts_refs, out_ref, work_ref = refs[:-2], refs[-2], refs[-1]
-    near = out_ref.shape[0] // SETS
-    width = out_ref.shape[2]
+    near = out_ref.shape[0]
     rows = work_ref.shape[0]
     step = 2 * TOK
     for start in range(0, rows, step):
@@ -457,10 +456,9 @@
     work_ref[mine, :] = work_ref[mine, :] + residual_ref[...]
     for seq in range(rows // TOK):
         far = seq // near
-        for block in range(SETS):
-            out_ref[(seq % near) * SETS + block, far * TOK : (far + 1) * TOK, :] = work_ref[
-                seq * TOK : (seq + 1) * TOK, block * width : (block + 1) * width
-            ].astype(jnp.bfloat16)
+        out_ref[seq % near, far * TOK : (far + 1) * TOK, :] = work_ref[
+            seq * TOK : (seq + 1) * TOK, :
+        ].astype(jnp.bfloat16)
 
 
 def join(residual, parts, near):
@@ -468,7 +466,7 @@
     vmem = pl.BlockSpec(memory_space=pltpu.VMEM)
     return pl.pallas_call(
         join_kernel,
-        out_shape=pltpu.VMEM((near * SETS, rows // near, D // SETS), jnp.bfloat16),
+        out_shape=pltpu.VMEM((near, rows // near, D), jnp.bfloat16),
         in_specs=[vmem] * (len(parts) + 1),
         out_specs=vmem,
         scratch_shapes=[pltpu.VMEM((rows, D), jnp.float32)],
@@ -478,20 +476,24 @@
 
 
 def fold_kernel(parts_ref, out_ref):
-    for source in range(SETS):
-        total = summed([parts_ref.at[near * SETS + source] for near in range(parts_ref.shape[0] // SETS)], ...)
-        total = total.astype(jnp.bfloat16)
-        for far in range(out_ref.shape[0]):
-            out_ref[far, source * TOK : (source + 1) * TOK, :] = total[
-                far * TOK : (far + 1) * TOK, :
-            ]
+    width = D // SETS
+    for far in range(parts_ref.shape[1] // TOK):
+        for block in range(SETS):
+            cols = slice(block * width, (block + 1) * width)
+            total = parts_ref[0, far * TOK : (far + 1) * TOK, cols].astype(jnp.float32)
+            for source in range(1, parts_ref.shape[0]):
+                total = total + parts_ref[
+                    source, far * TOK : (far + 1) * TOK, cols
+                ].astype(jnp.float32)
+            out_ref[far * SETS + block] = total.astype(jnp.bfloat16)
 
 
 def fold(parts):
+    far = parts.shape[1] // TOK
     vmem = pl.BlockSpec(memory_space=pltpu.VMEM)
     return pl.pallas_call(
         fold_kernel,
-        out_shape=pltpu.VMEM((parts.shape[1] // TOK, DRAFT, parts.shape[2]), parts.dtype),
+        out_shape=pltpu.VMEM((far * SETS, TOK, D // SETS), parts.dtype),
         in_specs=[vmem],
         out_specs=vmem,
         compiler_params=pltpu.CompilerParams(vmem_limit_bytes=VMEM_LIMIT),
@@ -500,15 +502,18 @@
 
 
 def total_kernel(parts_ref, out_ref):
-    total = summed([parts_ref.at[far] for far in range(parts_ref.shape[0])], ...)
-    out_ref[0] = total.astype(jnp.bfloat16)
+    for source in range(SETS):
+        total = parts_ref[source].astype(jnp.float32)
+        for far in range(1, parts_ref.shape[0] // SETS):
+            total = total + parts_ref[far * SETS + source].astype(jnp.float32)
+        out_ref[0, source * TOK : (source + 1) * TOK, :] = total.astype(jnp.bfloat16)
 
 
 def total(parts):
     vmem = pl.BlockSpec(memory_space=pltpu.VMEM)
     return pl.pallas_call(
         total_kernel,
-        out_shape=jax.ShapeDtypeStruct((1,) + parts.shape[1:], parts.dtype),
+        out_shape=jax.ShapeDtypeStruct((1, DRAFT, parts.shape[2]), parts.dtype),
         in_specs=[vmem],
         out_specs=vmem,
         compiler_params=pltpu.CompilerParams(vmem_limit_bytes=VMEM_LIMIT),
@@ -567,14 +572,20 @@
         parts.append(shifted(far, "kv", kv_count, -by))
     run = 4
     far_count = seq_count // run
-    runs = [
-        [(far * run + near) * SETS + block for near in range(run) for block in range(SETS)]
-        for far in range(far_count)
+    runs = [[far * run + near for near in range(run)] for far in range(far_count)]
+    strides = [
+        [
+            (far * run + near) * SETS + block
+            for far in range(far_count)
+            for block in range(SETS)
+        ]
+        for near in range(run)
     ]
-    strides = [[far * run + near for far in range(far_count)] for near in range(run)]
     back = join(residual, parts, run)
-    back = lax.all_to_all(back, ("seq", "exp"), 0, 0, tiled=True, axis_index_groups=runs)
-    back = lax.all_to_all(fold(back), "seq", 0, 0, tiled=True, axis_index_groups=strides)
+    back = lax.all_to_all(back, "seq", 0, 0, tiled=True, axis_index_groups=runs)
+    back = lax.all_to_all(
+        fold(back), ("seq", "exp"), 0, 0, tiled=True, axis_index_groups=strides
+    )
     return total(back)
 
 

time: 189 us -> 189 us (level)
  no operation moved by 1% of the time
where the time goes in v7:
time: 189 us; the launch traced here: 188 us
  blocking collectives  119 us (63%)
  Pallas kernels  20.2 us (11%)
  starting transfers between devices  17.4 us (9%)
  waiting for transfers between devices  16.4 us (9%)
  between operations  14.2 us (8%)
    all_to_all x1, blocking collectives, local(): lax.all_to_all(fold(back), ('seq', 'exp'), 0, 0, tiled=True, axis_index_g...  41.9 us
    all_gather x1, blocking collectives, local(): rows = lax.all_gather(row, 'seq').reshape(seq_count * TOK, WIDE)  31.5 us
    ppermute x6, starting transfers between devices, shifted(): lax.ppermute(value, axis, [(i, (i + by) % count) for i in range(count)])  17.4 us
    all_to_all x1, blocking collectives, local(): back = lax.all_to_all(back, 'seq', 0, 0, tiled=True, axis_index_groups=runs)  16.7 us
    all_to_all x1, blocking collectives, local(): parts = lax.all_to_all(partials, 'exp', 0, 0, tiled=True)  16.6 us
    all_to_all x1, blocking collectives, local(): lax.all_to_all(projected.reshape(SETS, TOK, D), 'exp', 0, 0, tiled=True)  12.3 us
    ppermute x6, waiting for transfers between devices, shifted(): lax.ppermute(value, axis, [(i, (i + by) % count) for i in range(count)])  9.75 us
    all_gather x1, waiting for transfers between devices, local(): weights = lax.all_gather(pack(gate_w, up_w, down_w), 'exp')  6.63 us
  transfers between devices with their start and end apart: 7, of which 4 were waited for; matrix products, arithmetic and copies ran while one was open for 0% of the time, Pallas kernels for 9%

profile of v7, /device:TPU:1, one launch (start us, length us, event | category | flops | bytes accessed | tf_op | source)
XLA Modules:
  0.0 187.8 jit_solution(1178080586649167661)
XLA Ops:
  6.5 2.4 %pack.1 = bf16[3072,256]{1,0:T(8,128)(2,1)} custom-call(bf16[1,2048,128]{2,1,0:T(8,128)(2,1)} %gate_ref.1, bf16[1,2048,128]{2,1,0:T(8,128)(2,1)} %up_ref.1, bf16[1,128,2048]{2,1,0:T(8,128)(2,1)} %down_ref.1), custom_call_target="tpu_custom_call" | custom-call | tf_op jit(solution)/shard_map/pack/pallas_call | solution.py:337
  9.6 0.6 copy-done
  10.2 3.8 %attention.1 = (bf16[8,72,256]{2,1,0:T(8,128)(2,1)S(1)}, bf16[256,2048]{1,0:T(8,128)(2,1)S(1)}, f32[8,64]{1,0:T(8,128)S(1)}) custom-call(s32[12]{0:T(128)S(1)} %bitcast.6, s32[1]{0:T(128)S(6)} %copy.15.lens, bf16[1,64,2048]{2,1,0:T(8,128)(2,1)} %q_hbm.1, s32[1,64]{1,0:T(1,128)} %parents_hbm.1, bf16[2,1,8,2048]{3,2,1,0:T(8,128)(2,1)} %draft_hbm.1, ...), custom_call_target="tpu_custom_call" | custom-call | tf_op jit(solution)/shard_map/attention/pallas_call | solution.py:166
  14.1 16.6 %all_to_all.20.parts_ref = bf16[8,72,256]{2,1,0:T(8,128)(2,1)S(1)} all-to-all(bf16[8,72,256]{2,1,0:T(8,128)(2,1)S(1)} %get-tuple-element.14), channel_id=1, replica_groups=mesh['kv'=4,'seq'=16,'exp'=8] {'exp'}, dimensions={0} | all-to-all | bytes 589824 | tf_op jit(solution)/shard_map/all_to_all | solution.py:557
  30.6 0.6 merge.1
  31.3 12.3 %all_to_all.21.parts_ref = bf16[8,8,2048]{2,1,0:T(8,128)(2,1)S(1)} all-to-all(bf16[8,8,2048]{2,1,0:T(8,128)(2,1)S(1)} %bitcast.5), channel_id=1, replica_groups=mesh['kv'=4,'seq'=16,'exp'=8] {'exp'}, dimensions={0} | all-to-all | bytes 524288 | tf_op jit(solution)/shard_map/all_to_all | solution.py:559
  43.6 1.4 norm.1
  45.0 31.5 %all-gather.rows_ref = bf16[128,2176]{1,0:T(8,128)(2,1)S(1)} all-gather(bf16[8,2176]{1,0:T(8,128)(2,1)S(1)} %get-tuple-element.18), channel_id=2, replica_groups=mesh['kv'=4,'seq'=16,'exp'=8] {'seq'}, dimensions={0}, use_global_device_ids=true | all-gather | bytes 591872 | tf_op jit(solution)/shard_map/all_gather | solution.py:561
  76.5 3.1 %collective-permute-start = (bf16[128,2176]{1,0:T(8,128)(2,1)S(1)}, bf16[128,2176]{1,0:T(8,128)(2,1)S(1)}, u32[]{:S(2)}, u32[]{:S(2)}) collective-permute-start(bf16[128,2176]{1,0:T(8,128)(2,1)S(1)} %all-gather.rows_ref), channel_id=1, source_target_pairs={{0,128},{128,256},{256,384},{384,0},{1,129},{129,257},{257,385},{3... | collective-permute-start | bytes 1671176 | tf_op jit(solution)/shard_map/ppermute | solution.py:525
  79.6 3.4 %collective-permute-start.1 = (bf16[128,2176]{1,0:T(8,128)(2,1)S(1)}, bf16[128,2176]{1,0:T(8,128)(2,1)S(1)}, u32[]{:S(2)}, u32[]{:S(2)}) collective-permute-start(bf16[128,2176]{1,0:T(8,128)(2,1)S(1)} %all-gather.rows_ref), channel_id=1, source_target_pairs={{0,384},{128,0},{256,128},{384,256},{1,385},{129,1},{257,129},{385... | collective-permute-start | bytes 1671176 | tf_op jit(solution)/shard_map/ppermute | solution.py:525
  83.0 3.4 %collective-permute-start.4 = (bf16[128,2176]{1,0:T(8,128)(2,1)S(1)}, bf16[128,2176]{1,0:T(8,128)(2,1)S(1)}, u32[]{:S(2)}, u32[]{:S(2)}) collective-permute-start(bf16[128,2176]{1,0:T(8,128)(2,1)S(1)} %all-gather.rows_ref), channel_id=1, source_target_pairs={{0,256},{128,384},{256,0},{384,128},{1,257},{129,385},{257,1},{385... | collective-permute-start | bytes 1671176 | tf_op jit(solution)/shard_map/ppermute | solution.py:525
  86.5 6.6 %all-gather.4.cloned.1.call-done = bf16[24576,256]{1,0:T(8,128)(2,1)} async-done(((bf16[3072,256]{1,0:T(8,128)(2,1)}), bf16[24576,256]{1,0:T(8,128)(2,1)}) %all-gather.4.cloned.1.call-update) | async-done | bytes 12582928 | tf_op jit(solution)/shard_map/all_gather | solution.py:546
  93.1 5.7 %own_expert.1 = (bf16[128,2048]{1,0:T(8,128)(2,1)S(1)}, bf16[8,3072,256]{2,1,0:T(8,128)(2,1)S(1)}) custom-call(bf16[128,2176]{1,0:T(8,128)(2,1)S(1)} %all-gather.rows_ref, bf16[8,3072,256]{2,1,0:T(8,128)(2,1)} %bitcast.7), custom_call_target="tpu_custom_call" | custom-call | tf_op jit(solution)/shard_map/own_expert/pallas_call | solution.py:410
  98.8 3.5 %other_expert.2 = (bf16[128,2048]{1,0:T(8,128)(2,1)S(1)}, bf16[128,2048]{1,0:T(8,128)(2,1)S(1)}) custom-call(bf16[128,2176]{1,0:T(8,128)(2,1)S(1)} %collective-permute-done.refs_0_, bf16[128,2176]{1,0:T(8,128)(2,1)S(1)} %collective-permute-done.1.refs_1_, bf16[8,3072,256]{2,1,0:T(8,128)(2,1)S(1)} %get-tuple-element.20.refs_2_.refs_1_), custom_call_target="tpu_custom_call" | custom-call | tf_op jit(solution)/shard_map/other_expert/pallas_call | solution.py:430
  102.3 1.9 %collective-permute-start.2 = (bf16[128,2048]{1,0:T(8,128)(2,1)S(1)}, bf16[128,2048]{1,0:T(8,128)(2,1)S(1)}, u32[]{:S(2)}, u32[]{:S(2)}) collective-permute-start(bf16[128,2048]{1,0:T(8,128)(2,1)S(1)} %get-tuple-element.21), channel_id=1, source_target_pairs={{0,384},{128,0},{256,128},{384,256},{1,385},{129,1},{257,129},{385... | collective-permute-start | bytes 1572872 | tf_op jit(solution)/shard_map/ppermute | solution.py:525
  104.2 3.4 %collective-permute-start.3 = (bf16[128,2048]{1,0:T(8,128)(2,1)S(1)}, bf16[128,2048]{1,0:T(8,128)(2,1)S(1)}, u32[]{:S(2)}, u32[]{:S(2)}) collective-permute-start(bf16[128,2048]{1,0:T(8,128)(2,1)S(1)} %get-tuple-element.22), channel_id=1, source_target_pairs={{0,128},{128,256},{256,384},{384,0},{1,129},{129,257},{257,385},{3... | collective-permute-start | bytes 1572872 | tf_op jit(solution)/shard_map/ppermute | solution.py:525
  107.6 1.8 other_expert.3
  109.4 2.2 %collective-permute-start.5 = (bf16[128,2048]{1,0:T(8,128)(2,1)S(1)}, bf16[128,2048]{1,0:T(8,128)(2,1)S(1)}, u32[]{:S(2)}, u32[]{:S(2)}) collective-permute-start(bf16[128,2048]{1,0:T(8,128)(2,1)S(1)} %other_expert.3), channel_id=1, source_target_pairs={{0,256},{128,384},{256,0},{384,128},{1,257},{129,385},{257,1},{385... | collective-permute-start | bytes 1572872 | tf_op jit(solution)/shard_map/ppermute | solution.py:525
  111.6 1.8 collective-permute-done.2.refs_1_
  113.5 7.1 %collective-permute-done.3.refs_2_ = bf16[128,2048]{1,0:T(8,128)(2,1)S(1)} collective-permute-done((bf16[128,2048]{1,0:T(8,128)(2,1)S(1)}, bf16[128,2048]{1,0:T(8,128)(2,1)S(1)}, u32[]{:S(2)}, u32[]{:S(2)}) %collective-permute-start.3) | collective-permute-done | bytes 524320 | tf_op jit(solution)/shard_map/ppermute | solution.py:525
  120.6 0.8 collective-permute-done.5.refs_3_
  121.7 16.7 %all_to_all.22.parts_ref = bf16[4,32,2048]{2,1,0:T(8,128)(2,1)S(1)} all-to-all(bf16[4,32,2048]{2,1,0:T(8,128)(2,1)S(1)} %join.1), channel_id=1, replica_groups={{0,8,16,24},{32,40,48,56},{64,72,80,88},{96,104,112,120},{1,9,17,25},{3..., dimensions={0} | all-to-all | bytes 1048576 | tf_op jit(solution)/shard_map/all_to_all | solution.py:585
  138.5 41.9 %all_to_all.23.parts_ref = bf16[32,8,256]{2,1,0:T(8,128)(2,1)S(1)} all-to-all(bf16[32,8,256]{2,1,0:T(8,128)(2,1)S(1)} %fold.1), channel_id=1, replica_groups={{0,1,2,3,4,5,6,7,32,33,34,35,36,37,38,39,64,65,66,67,68,69,70,71,96,97,..., dimensions={0} | all-to-all | bytes 262144 | tf_op jit(solution)/shard_map/all_to_all | solution.py:586
  180.4 0.6 total.1
  (8 shorter events, 0.4 us)
Async XLA Ops:
  6.5 86.6 %all-gather.4.cloned.1.call-start = ((), (), s32[]{:S(2)}) async-start(), calls=%async_computation.4 | async-start | bytes 14155776 | tf_op jit(solution)/shard_map/all_gather | solution.py:546
  9.6 0.7 copy-start
  76.5 22.3 %collective-permute-start = (bf16[128,2176]{1,0:T(8,128)(2,1)S(1)}, bf16[128,2176]{1,0:T(8,128)(2,1)S(1)}, u32[]{:S(2)}, u32[]{:S(2)}) collective-permute-start(bf16[128,2176]{1,0:T(8,128)(2,1)S(1)} %all-gather.rows_ref), channel_id=1, source_target_pairs={{0,128},{128,256},{256,384},{384,0},{1,129},{129,257},{257,385},{3... | collective-permute-start | bytes 1671176 | tf_op jit(solution)/shard_map/ppermute | solution.py:525
  79.6 19.2 %collective-permute-start.1 = (bf16[128,2176]{1,0:T(8,128)(2,1)S(1)}, bf16[128,2176]{1,0:T(8,128)(2,1)S(1)}, u32[]{:S(2)}, u32[]{:S(2)}) collective-permute-start(bf16[128,2176]{1,0:T(8,128)(2,1)S(1)} %all-gather.rows_ref), channel_id=1, source_target_pairs={{0,384},{128,0},{256,128},{384,256},{1,385},{129,1},{257,129},{385... | collective-permute-start | bytes 1671176 | tf_op jit(solution)/shard_map/ppermute | solution.py:525
  83.0 24.6 %collective-permute-start.4 = (bf16[128,2176]{1,0:T(8,128)(2,1)S(1)}, bf16[128,2176]{1,0:T(8,128)(2,1)S(1)}, u32[]{:S(2)}, u32[]{:S(2)}) collective-permute-start(bf16[128,2176]{1,0:T(8,128)(2,1)S(1)} %all-gather.rows_ref), channel_id=1, source_target_pairs={{0,256},{128,384},{256,0},{384,128},{1,257},{129,385},{257,1},{385... | collective-permute-start | bytes 1671176 | tf_op jit(solution)/shard_map/ppermute | solution.py:525
  102.3 11.2 %collective-permute-start.2 = (bf16[128,2048]{1,0:T(8,128)(2,1)S(1)}, bf16[128,2048]{1,0:T(8,128)(2,1)S(1)}, u32[]{:S(2)}, u32[]{:S(2)}) collective-permute-start(bf16[128,2048]{1,0:T(8,128)(2,1)S(1)} %get-tuple-element.21), channel_id=1, source_target_pairs={{0,384},{128,0},{256,128},{384,256},{1,385},{129,1},{257,129},{385... | collective-permute-start | bytes 1572872 | tf_op jit(solution)/shard_map/ppermute | solution.py:525
  104.2 16.3 %collective-permute-start.3 = (bf16[128,2048]{1,0:T(8,128)(2,1)S(1)}, bf16[128,2048]{1,0:T(8,128)(2,1)S(1)}, u32[]{:S(2)}, u32[]{:S(2)}) collective-permute-start(bf16[128,2048]{1,0:T(8,128)(2,1)S(1)} %get-tuple-element.22), channel_id=1, source_target_pairs={{0,128},{128,256},{256,384},{384,0},{1,129},{129,257},{257,385},{3... | collective-permute-start | bytes 1572872 | tf_op jit(solution)/shard_map/ppermute | solution.py:525
  109.4 11.9 %collective-permute-start.5 = (bf16[128,2048]{1,0:T(8,128)(2,1)S(1)}, bf16[128,2048]{1,0:T(8,128)(2,1)S(1)}, u32[]{:S(2)}, u32[]{:S(2)}) collective-permute-start(bf16[128,2048]{1,0:T(8,128)(2,1)S(1)} %other_expert.3), channel_id=1, source_target_pairs={{0,256},{128,384},{256,0},{384,128},{1,257},{129,385},{257,1},{385... | collective-permute-start | bytes 1572872 | tf_op jit(solution)/shard_map/ppermute | solution.py:525
Sparse Core Ops, SparseCore 0:
  9.5 83.5 all-gather.3

commit v8 on v7

--- a/solution.py
+++ b/solution.py
@@ -559,9 +559,13 @@
     shares = lax.all_to_all(projected.reshape(SETS, TOK, D), "exp", 0, 0, tiled=True)
     residual, row = norm(shares, hidden, norm_gain, jnp.transpose(router), chosen)
     rows = lax.all_gather(row, "seq").reshape(seq_count * TOK, WIDE)
-    arrived = {by: shifted(rows, "kv", kv_count, by) for by in range(1, kv_count)}
+    arrived = {by: shifted(rows, "kv", kv_count, by) for by in (1, kv_count - 1)}
     own, kept = own_expert(rows, weights)
-    near = other_expert(kept, arrived[1], arrived[kv_count - 1])
+    later, one, last, own = lax.optimization_barrier(
+        (rows, arrived[1], arrived[kv_count - 1], own)
+    )
+    arrived.update({by: shifted(later, "kv", kv_count, by) for by in range(2, kv_count - 1)})
+    near = other_expert(kept, one, last)
     parts = [
         own,
         shifted(near[0], "kv", kv_count, -1),

time: 189 us -> 194 us (1.026)
  waiting for transfers between devices: 16.4 us -> 35 us
  blocking collectives: 119 us -> 107 us
    ppermute x6, waiting for transfers between devices: 9.75 us -> 24.9 us  [shifted(): lax.ppermute(value, axis, [(i, (i + by) % count) for i in range(count)])]
    all_to_all x1, blocking collectives: 41.9 us -> 30.6 us  [local(): lax.all_to_all(fold(back), ('seq', 'exp'), 0, 0, tiled=True, axis_index_g...]
    all_gather x1, waiting for transfers between devices: 6.63 us -> 10.1 us  [local(): weights = lax.all_gather(pack(gate_w, up_w, down_w), 'exp')]
  transfers between devices with their start and end apart: 7 -> 7, of which waited for: 4 -> 5; matrix products, arithmetic and copies ran while one was open for 0% -> 0% of each run, Pallas kernels for 9% -> 9%
where the time goes in v8:
time: 194 us; the launch traced here: 193 us
  blocking collectives  107 us (55%)
  waiting for transfers between devices  35 us (18%)
  Pallas kernels  20.2 us (10%)
  starting transfers between devices  16.1 us (8%)
  between operations  14.2 us (7%)
    all_gather x1, blocking collectives, local(): rows = lax.all_gather(row, 'seq').reshape(seq_count * TOK, WIDE)  31.5 us
    all_to_all x1, blocking collectives, local(): lax.all_to_all(fold(back), ('seq', 'exp'), 0, 0, tiled=True, axis_index_g...  30.6 us
    ppermute x6, waiting for transfers between devices, shifted(): lax.ppermute(value, axis, [(i, (i + by) % count) for i in range(count)])  24.9 us
    all_to_all x1, blocking collectives, local(): parts = lax.all_to_all(partials, 'exp', 0, 0, tiled=True)  16.6 us
    all_to_all x1, blocking collectives, local(): back = lax.all_to_all(back, 'seq', 0, 0, tiled=True, axis_index_groups=runs)  16.2 us
    ppermute x6, starting transfers between devices, shifted(): lax.ppermute(value, axis, [(i, (i + by) % count) for i in range(count)])  16.1 us
    all_to_all x1, blocking collectives, local(): lax.all_to_all(projected.reshape(SETS, TOK, D), 'exp', 0, 0, tiled=True)  12.3 us
    all_gather x1, waiting for transfers between devices, local(): weights = lax.all_gather(pack(gate_w, up_w, down_w), 'exp')  10.1 us
  transfers between devices with their start and end apart: 7, of which 5 were waited for; matrix products, arithmetic and copies ran while one was open for 0% of the time, Pallas kernels for 9%

profile of v8, /device:TPU:1, one launch (start us, length us, event | category | flops | bytes accessed | tf_op | source)
XLA Modules:
  0.0 193.4 jit_solution(415280215849142508)
XLA Ops:
  6.5 2.4 %pack.1 = bf16[3072,256]{1,0:T(8,128)(2,1)} custom-call(bf16[1,2048,128]{2,1,0:T(8,128)(2,1)} %gate_ref.1, bf16[1,2048,128]{2,1,0:T(8,128)(2,1)} %up_ref.1, bf16[1,128,2048]{2,1,0:T(8,128)(2,1)} %down_ref.1), custom_call_target="tpu_custom_call" | custom-call | tf_op jit(solution)/shard_map/pack/pallas_call | solution.py:337
  9.6 0.6 copy-done
  10.2 3.8 %attention.1 = (bf16[8,72,256]{2,1,0:T(8,128)(2,1)S(1)}, bf16[256,2048]{1,0:T(8,128)(2,1)S(1)}, f32[8,64]{1,0:T(8,128)S(1)}) custom-call(s32[12]{0:T(128)S(1)} %bitcast.6, s32[1]{0:T(128)S(6)} %copy.15.lens, bf16[1,64,2048]{2,1,0:T(8,128)(2,1)} %q_hbm.1, s32[1,64]{1,0:T(1,128)} %parents_hbm.1, bf16[2,1,8,2048]{3,2,1,0:T(8,128)(2,1)} %draft_hbm.1, ...), custom_call_target="tpu_custom_call" | custom-call | tf_op jit(solution)/shard_map/attention/pallas_call | solution.py:166
  14.1 16.6 %all_to_all.20.parts_ref = bf16[8,72,256]{2,1,0:T(8,128)(2,1)S(1)} all-to-all(bf16[8,72,256]{2,1,0:T(8,128)(2,1)S(1)} %get-tuple-element.18), channel_id=1, replica_groups=mesh['kv'=4,'seq'=16,'exp'=8] {'exp'}, dimensions={0} | all-to-all | bytes 589824 | tf_op jit(solution)/shard_map/all_to_all | solution.py:557
  31.3 12.3 %all_to_all.21.parts_ref = bf16[8,8,2048]{2,1,0:T(8,128)(2,1)S(1)} all-to-all(bf16[8,8,2048]{2,1,0:T(8,128)(2,1)S(1)} %bitcast.5), channel_id=1, replica_groups=mesh['kv'=4,'seq'=16,'exp'=8] {'exp'}, dimensions={0} | all-to-all | bytes 524288 | tf_op jit(solution)/shard_map/all_to_all | solution.py:559
  43.6 1.4 norm.1
  45.0 31.5 %all-gather.rows_ref = bf16[128,2176]{1,0:T(8,128)(2,1)S(1)} all-gather(bf16[8,2176]{1,0:T(8,128)(2,1)S(1)} %get-tuple-element.22), channel_id=2, replica_groups=mesh['kv'=4,'seq'=16,'exp'=8] {'seq'}, dimensions={0}, use_global_device_ids=true | all-gather | bytes 591872 | tf_op jit(solution)/shard_map/all_gather | solution.py:561
  76.5 3.1 %collective-permute-start = (bf16[128,2176]{1,0:T(8,128)(2,1)S(1)}, bf16[128,2176]{1,0:T(8,128)(2,1)S(1)}, u32[]{:S(2)}, u32[]{:S(2)}) collective-permute-start(bf16[128,2176]{1,0:T(8,128)(2,1)S(1)} %all-gather.rows_ref), channel_id=1, source_target_pairs={{0,128},{128,256},{256,384},{384,0},{1,129},{129,257},{257,385},{3... | collective-permute-start | bytes 1671176 | tf_op jit(solution)/shard_map/ppermute | solution.py:525
  79.6 3.4 %collective-permute-start.1 = (bf16[128,2176]{1,0:T(8,128)(2,1)S(1)}, bf16[128,2176]{1,0:T(8,128)(2,1)S(1)}, u32[]{:S(2)}, u32[]{:S(2)}) collective-permute-start(bf16[128,2176]{1,0:T(8,128)(2,1)S(1)} %all-gather.rows_ref), channel_id=1, source_target_pairs={{0,384},{128,0},{256,128},{384,256},{1,385},{129,1},{257,129},{385... | collective-permute-start | bytes 1671176 | tf_op jit(solution)/shard_map/ppermute | solution.py:525
  83.0 10.1 %all-gather.4.cloned.1.call-done = bf16[24576,256]{1,0:T(8,128)(2,1)} async-done(((bf16[3072,256]{1,0:T(8,128)(2,1)}), bf16[24576,256]{1,0:T(8,128)(2,1)}) %all-gather.4.cloned.1.call-update) | async-done | bytes 12582928 | tf_op jit(solution)/shard_map/all_gather | solution.py:546
  93.1 5.7 %own_expert.1 = (bf16[128,2048]{1,0:T(8,128)(2,1)S(1)}, bf16[8,3072,256]{2,1,0:T(8,128)(2,1)S(1)}) custom-call(bf16[128,2176]{1,0:T(8,128)(2,1)S(1)} %all-gather.rows_ref, bf16[8,3072,256]{2,1,0:T(8,128)(2,1)} %bitcast.7), custom_call_target="tpu_custom_call" | custom-call | tf_op jit(solution)/shard_map/own_expert/pallas_call | solution.py:410
  98.8 2.2 %collective-permute-start.4 = (bf16[128,2176]{1,0:T(8,128)(2,1)S(1)}, bf16[128,2176]{1,0:T(8,128)(2,1)S(1)}, u32[]{:S(2)}, u32[]{:S(2)}) collective-permute-start(bf16[128,2176]{1,0:T(8,128)(2,1)S(1)} %all-gather.rows_ref), channel_id=1, source_target_pairs={{0,256},{128,384},{256,0},{384,128},{1,257},{129,385},{257,1},{385... | collective-permute-start | bytes 1671176 | tf_op jit(solution)/shard_map/ppermute | solution.py:525
  101.0 3.5 %other_expert.2 = (bf16[128,2048]{1,0:T(8,128)(2,1)S(1)}, bf16[128,2048]{1,0:T(8,128)(2,1)S(1)}) custom-call(bf16[128,2176]{1,0:T(8,128)(2,1)S(1)} %collective-permute-done.refs_0_, bf16[128,2176]{1,0:T(8,128)(2,1)S(1)} %collective-permute-done.1.refs_1_, bf16[8,3072,256]{2,1,0:T(8,128)(2,1)S(1)} %get-tuple-element.27.refs_2_.refs_1_), custom_call_target="tpu_custom_call" | custom-call | tf_op jit(solution)/shard_map/other_expert/pallas_call | solution.py:430
  104.5 2.8 %collective-permute-start.2 = (bf16[128,2048]{1,0:T(8,128)(2,1)S(1)}, bf16[128,2048]{1,0:T(8,128)(2,1)S(1)}, u32[]{:S(2)}, u32[]{:S(2)}) collective-permute-start(bf16[128,2048]{1,0:T(8,128)(2,1)S(1)} %get-tuple-element.28), channel_id=1, source_target_pairs={{0,384},{128,0},{256,128},{384,256},{1,385},{129,1},{257,129},{385... | collective-permute-start | bytes 1572872 | tf_op jit(solution)/shard_map/ppermute | solution.py:525
  107.3 2.5 %collective-permute-start.3 = (bf16[128,2048]{1,0:T(8,128)(2,1)S(1)}, bf16[128,2048]{1,0:T(8,128)(2,1)S(1)}, u32[]{:S(2)}, u32[]{:S(2)}) collective-permute-start(bf16[128,2048]{1,0:T(8,128)(2,1)S(1)} %get-tuple-element.29), channel_id=1, source_target_pairs={{0,128},{128,256},{256,384},{384,0},{1,129},{129,257},{257,385},{3... | collective-permute-start | bytes 1572872 | tf_op jit(solution)/shard_map/ppermute | solution.py:525
  109.8 6.4 %collective-permute-done.4.refs_0_ = bf16[128,2176]{1,0:T(8,128)(2,1)S(1)} collective-permute-done((bf16[128,2176]{1,0:T(8,128)(2,1)S(1)}, bf16[128,2176]{1,0:T(8,128)(2,1)S(1)}, u32[]{:S(2)}, u32[]{:S(2)}) %collective-permute-start.4) | collective-permute-done | bytes 557088 | tf_op jit(solution)/shard_map/ppermute | solution.py:525
  116.2 1.8 other_expert.3
  118.1 2.2 %collective-permute-start.5 = (bf16[128,2048]{1,0:T(8,128)(2,1)S(1)}, bf16[128,2048]{1,0:T(8,128)(2,1)S(1)}, u32[]{:S(2)}, u32[]{:S(2)}) collective-permute-start(bf16[128,2048]{1,0:T(8,128)(2,1)S(1)} %other_expert.3), channel_id=1, source_target_pairs={{0,256},{128,384},{256,0},{384,128},{1,257},{129,385},{257,1},{385... | collective-permute-start | bytes 1572872 | tf_op jit(solution)/shard_map/ppermute | solution.py:525
  120.3 4.7 %collective-permute-done.2.refs_1_ = bf16[128,2048]{1,0:T(8,128)(2,1)S(1)} collective-permute-done((bf16[128,2048]{1,0:T(8,128)(2,1)S(1)}, bf16[128,2048]{1,0:T(8,128)(2,1)S(1)}, u32[]{:S(2)}, u32[]{:S(2)}) %collective-permute-start.2) | collective-permute-done | bytes 524320 | tf_op jit(solution)/shard_map/ppermute | solution.py:525
  124.9 3.6 %collective-permute-done.3.refs_2_ = bf16[128,2048]{1,0:T(8,128)(2,1)S(1)} collective-permute-done((bf16[128,2048]{1,0:T(8,128)(2,1)S(1)}, bf16[128,2048]{1,0:T(8,128)(2,1)S(1)}, u32[]{:S(2)}, u32[]{:S(2)}) %collective-permute-start.3) | collective-permute-done | bytes 524320 | tf_op jit(solution)/shard_map/ppermute | solution.py:525
  128.5 10.2 %collective-permute-done.5.refs_3_ = bf16[128,2048]{1,0:T(8,128)(2,1)S(1)} collective-permute-done((bf16[128,2048]{1,0:T(8,128)(2,1)S(1)}, bf16[128,2048]{1,0:T(8,128)(2,1)S(1)}, u32[]{:S(2)}, u32[]{:S(2)}) %collective-permute-start.5) | collective-permute-done | bytes 524320 | tf_op jit(solution)/shard_map/ppermute | solution.py:525
  139.0 16.2 %all_to_all.22.parts_ref = bf16[4,32,2048]{2,1,0:T(8,128)(2,1)S(1)} all-to-all(bf16[4,32,2048]{2,1,0:T(8,128)(2,1)S(1)} %join.1), channel_id=1, replica_groups={{0,8,16,24},{32,40,48,56},{64,72,80,88},{96,104,112,120},{1,9,17,25},{3..., dimensions={0} | all-to-all | bytes 1048576 | tf_op jit(solution)/shard_map/all_to_all | solution.py:589
  155.3 30.6 %all_to_all.23.parts_ref = bf16[32,8,256]{2,1,0:T(8,128)(2,1)S(1)} all-to-all(bf16[32,8,256]{2,1,0:T(8,128)(2,1)S(1)} %fold.1), channel_id=1, replica_groups={{0,1,2,3,4,5,6,7,32,33,34,35,36,37,38,39,64,65,66,67,68,69,70,71,96,97,..., dimensions={0} | all-to-all | bytes 262144 | tf_op jit(solution)/shard_map/all_to_all | solution.py:590
  185.9 0.6 total.1
  (8 shorter events, 1.1 us)
Async XLA Ops:
  6.5 86.6 %all-gather.4.cloned.1.call-start = ((), (), s32[]{:S(2)}) async-start(), calls=%async_computation.4 | async-start | bytes 14155776 | tf_op jit(solution)/shard_map/all_gather | solution.py:546
  9.6 0.7 copy-start
  76.5 22.3 %collective-permute-start = (bf16[128,2176]{1,0:T(8,128)(2,1)S(1)}, bf16[128,2176]{1,0:T(8,128)(2,1)S(1)}, u32[]{:S(2)}, u32[]{:S(2)}) collective-permute-start(bf16[128,2176]{1,0:T(8,128)(2,1)S(1)} %all-gather.rows_ref), channel_id=1, source_target_pairs={{0,128},{128,256},{256,384},{384,0},{1,129},{129,257},{257,385},{3... | collective-permute-start | bytes 1671176 | tf_op jit(solution)/shard_map/ppermute | solution.py:525
  79.6 19.2 %collective-permute-start.1 = (bf16[128,2176]{1,0:T(8,128)(2,1)S(1)}, bf16[128,2176]{1,0:T(8,128)(2,1)S(1)}, u32[]{:S(2)}, u32[]{:S(2)}) collective-permute-start(bf16[128,2176]{1,0:T(8,128)(2,1)S(1)} %all-gather.rows_ref), channel_id=1, source_target_pairs={{0,384},{128,0},{256,128},{384,256},{1,385},{129,1},{257,129},{385... | collective-permute-start | bytes 1671176 | tf_op jit(solution)/shard_map/ppermute | solution.py:525
  98.8 17.4 %collective-permute-start.4 = (bf16[128,2176]{1,0:T(8,128)(2,1)S(1)}, bf16[128,2176]{1,0:T(8,128)(2,1)S(1)}, u32[]{:S(2)}, u32[]{:S(2)}) collective-permute-start(bf16[128,2176]{1,0:T(8,128)(2,1)S(1)} %all-gather.rows_ref), channel_id=1, source_target_pairs={{0,256},{128,384},{256,0},{384,128},{1,257},{129,385},{257,1},{385... | collective-permute-start | bytes 1671176 | tf_op jit(solution)/shard_map/ppermute | solution.py:525
  104.5 20.4 %collective-permute-start.2 = (bf16[128,2048]{1,0:T(8,128)(2,1)S(1)}, bf16[128,2048]{1,0:T(8,128)(2,1)S(1)}, u32[]{:S(2)}, u32[]{:S(2)}) collective-permute-start(bf16[128,2048]{1,0:T(8,128)(2,1)S(1)} %get-tuple-element.28), channel_id=1, source_target_pairs={{0,384},{128,0},{256,128},{384,256},{1,385},{129,1},{257,129},{385... | collective-permute-start | bytes 1572872 | tf_op jit(solution)/shard_map/ppermute | solution.py:525
  107.3 21.2 %collective-permute-start.3 = (bf16[128,2048]{1,0:T(8,128)(2,1)S(1)}, bf16[128,2048]{1,0:T(8,128)(2,1)S(1)}, u32[]{:S(2)}, u32[]{:S(2)}) collective-permute-start(bf16[128,2048]{1,0:T(8,128)(2,1)S(1)} %get-tuple-element.29), channel_id=1, source_target_pairs={{0,128},{128,256},{256,384},{384,0},{1,129},{129,257},{257,385},{3... | collective-permute-start | bytes 1572872 | tf_op jit(solution)/shard_map/ppermute | solution.py:525
  118.1 20.6 %collective-permute-start.5 = (bf16[128,2048]{1,0:T(8,128)(2,1)S(1)}, bf16[128,2048]{1,0:T(8,128)(2,1)S(1)}, u32[]{:S(2)}, u32[]{:S(2)}) collective-permute-start(bf16[128,2048]{1,0:T(8,128)(2,1)S(1)} %other_expert.3), channel_id=1, source_target_pairs={{0,256},{128,384},{256,0},{384,128},{1,257},{129,385},{257,1},{385... | collective-permute-start | bytes 1572872 | tf_op jit(solution)/shard_map/ppermute | solution.py:525
Sparse Core Ops, SparseCore 0:
  9.5 83.5 all-gather.3

commit v9 on v8

--- a/solution.py
+++ b/solution.py
@@ -561,19 +561,24 @@
     rows = lax.all_gather(row, "seq").reshape(seq_count * TOK, WIDE)
     arrived = {by: shifted(rows, "kv", kv_count, by) for by in (1, kv_count - 1)}
     own, kept = own_expert(rows, weights)
-    later, one, last, own = lax.optimization_barrier(
-        (rows, arrived[1], arrived[kv_count - 1], own)
-    )
-    arrived.update({by: shifted(later, "kv", kv_count, by) for by in range(2, kv_count - 1)})
+    one, last, own = lax.optimization_barrier((arrived[1], arrived[kv_count - 1], own))
     near = other_expert(kept, one, last)
     parts = [
         own,
         shifted(near[0], "kv", kv_count, -1),
         shifted(near[1], "kv", kv_count, 1),
     ]
-    for by in range(2, kv_count - 1):
-        (far,) = other_expert(kept, arrived[by])
-        parts.append(shifted(far, "kv", kv_count, -by))
+    relayed = last
+    for by in range(kv_count - 2, 1, -1):
+        relayed = shifted(relayed, "kv", kv_count, -1)
+        relayed, near = lax.optimization_barrier((relayed, near))
+        (far,) = other_expert(kept, relayed)
+        half = D // 2
+        straight = shifted(far[:, :half], "kv", kv_count, -by)
+        around = far[:, half:]
+        for hop in range(by):
+            around = shifted(around, "kv", kv_count, -1)
+        parts.append(jnp.concatenate([straight, around], axis=1))
     run = 4
     far_count = seq_count // run
     runs = [[far * run + near for near in range(run)] for far in range(far_count)]

time: 194 us -> 206 us (1.062)
  starting transfers between devices: 16.1 us -> 23.3 us
    ppermute x6 -> x8, starting transfers between devices: 16.1 us -> 23.3 us  [shifted(): lax.ppermute(value, axis, [(i, (i + by) % count) for i in range(count)])]
    ppermute x6 -> x8, waiting for transfers between devices: 24.9 us -> 26.7 us  [shifted(): lax.ppermute(value, axis, [(i, (i + by) % count) for i in range(count)])]
  transfers between devices with their start and end apart: 7 -> 9, of which waited for: 5 -> 4; matrix products, arithmetic and copies ran while one was open for 0% -> 0% of each run, Pallas kernels for 9% -> 7%
where the time goes in v9:
time: 206 us; the launch traced here: 204 us
  blocking collectives  109 us (53%)
  waiting for transfers between devices  36.8 us (18%)
  starting transfers between devices  23.3 us (11%)
  Pallas kernels  20.2 us (10%)
  between operations  14.2 us (7%)
    all_gather x1, blocking collectives, local(): rows = lax.all_gather(row, 'seq').reshape(seq_count * TOK, WIDE)  31.5 us
    all_to_all x1, blocking collectives, local(): lax.all_to_all(fold(back), ('seq', 'exp'), 0, 0, tiled=True, axis_index_g...  30.8 us
    ppermute x8, waiting for transfers between devices, shifted(): lax.ppermute(value, axis, [(i, (i + by) % count) for i in range(count)])  26.7 us
    ppermute x8, starting transfers between devices, shifted(): lax.ppermute(value, axis, [(i, (i + by) % count) for i in range(count)])  23.3 us
    all_to_all x1, blocking collectives, local(): back = lax.all_to_all(back, 'seq', 0, 0, tiled=True, axis_index_groups=runs)  17.5 us
    all_to_all x1, blocking collectives, local(): parts = lax.all_to_all(partials, 'exp', 0, 0, tiled=True)  16.6 us
    all_to_all x1, blocking collectives, local(): lax.all_to_all(projected.reshape(SETS, TOK, D), 'exp', 0, 0, tiled=True)  12.3 us
    all_gather x1, waiting for transfers between devices, local(): weights = lax.all_gather(pack(gate_w, up_w, down_w), 'exp')  10.1 us
  transfers between devices with their start and end apart: 9, of which 4 were waited for; matrix products, arithmetic and copies ran while one was open for 0% of the time, Pallas kernels for 7%

profile of v9, /device:TPU:1, one launch (start us, length us, event | category | flops | bytes accessed | tf_op | source)
XLA Modules:
  0.0 203.9 jit_solution(265453980558359883)
XLA Ops:
  6.5 2.4 %pack.1 = bf16[3072,256]{1,0:T(8,128)(2,1)} custom-call(bf16[1,2048,128]{2,1,0:T(8,128)(2,1)} %gate_ref.1, bf16[1,2048,128]{2,1,0:T(8,128)(2,1)} %up_ref.1, bf16[1,128,2048]{2,1,0:T(8,128)(2,1)} %down_ref.1), custom_call_target="tpu_custom_call" | custom-call | tf_op jit(solution)/shard_map/pack/pallas_call | solution.py:337
  9.6 0.6 copy-done
  10.2 3.8 %attention.1 = (bf16[8,72,256]{2,1,0:T(8,128)(2,1)S(1)}, bf16[256,2048]{1,0:T(8,128)(2,1)S(1)}, f32[8,64]{1,0:T(8,128)S(1)}) custom-call(s32[12]{0:T(128)S(1)} %bitcast.6, s32[1]{0:T(128)S(6)} %copy.15.lens, bf16[1,64,2048]{2,1,0:T(8,128)(2,1)} %q_hbm.1, s32[1,64]{1,0:T(1,128)} %parents_hbm.1, bf16[2,1,8,2048]{3,2,1,0:T(8,128)(2,1)} %draft_hbm.1, ...), custom_call_target="tpu_custom_call" | custom-call | tf_op jit(solution)/shard_map/attention/pallas_call | solution.py:166
  14.0 16.6 %all_to_all.20.parts_ref = bf16[8,72,256]{2,1,0:T(8,128)(2,1)S(1)} all-to-all(bf16[8,72,256]{2,1,0:T(8,128)(2,1)S(1)} %get-tuple-element.18), channel_id=1, replica_groups=mesh['kv'=4,'seq'=16,'exp'=8] {'exp'}, dimensions={0} | all-to-all | bytes 589824 | tf_op jit(solution)/shard_map/all_to_all | solution.py:557
  31.2 12.3 %all_to_all.21.parts_ref = bf16[8,8,2048]{2,1,0:T(8,128)(2,1)S(1)} all-to-all(bf16[8,8,2048]{2,1,0:T(8,128)(2,1)S(1)} %bitcast.5), channel_id=1, replica_groups=mesh['kv'=4,'seq'=16,'exp'=8] {'exp'}, dimensions={0} | all-to-all | bytes 524288 | tf_op jit(solution)/shard_map/all_to_all | solution.py:559
  43.6 1.4 norm.1
  45.0 31.5 %all-gather.rows_ref = bf16[128,2176]{1,0:T(8,128)(2,1)S(1)} all-gather(bf16[8,2176]{1,0:T(8,128)(2,1)S(1)} %get-tuple-element.22), channel_id=2, replica_groups=mesh['kv'=4,'seq'=16,'exp'=8] {'seq'}, dimensions={0}, use_global_device_ids=true | all-gather | bytes 591872 | tf_op jit(solution)/shard_map/all_gather | solution.py:561
  76.5 3.1 %collective-permute-start = (bf16[128,2176]{1,0:T(8,128)(2,1)S(1)}, bf16[128,2176]{1,0:T(8,128)(2,1)S(1)}, u32[]{:S(2)}, u32[]{:S(2)}) collective-permute-start(bf16[128,2176]{1,0:T(8,128)(2,1)S(1)} %all-gather.rows_ref), channel_id=1, source_target_pairs={{0,128},{128,256},{256,384},{384,0},{1,129},{129,257},{257,385},{3... | collective-permute-start | bytes 1671176 | tf_op jit(solution)/shard_map/ppermute | solution.py:525
  79.6 3.4 %collective-permute-start.1 = (bf16[128,2176]{1,0:T(8,128)(2,1)S(1)}, bf16[128,2176]{1,0:T(8,128)(2,1)S(1)}, u32[]{:S(2)}, u32[]{:S(2)}) collective-permute-start(bf16[128,2176]{1,0:T(8,128)(2,1)S(1)} %all-gather.rows_ref), channel_id=1, source_target_pairs={{0,384},{128,0},{256,128},{384,256},{1,385},{129,1},{257,129},{385... | collective-permute-start | bytes 1671176 | tf_op jit(solution)/shard_map/ppermute | solution.py:525
  83.0 10.1 %all-gather.4.cloned.1.call-done = bf16[24576,256]{1,0:T(8,128)(2,1)} async-done(((bf16[3072,256]{1,0:T(8,128)(2,1)}), bf16[24576,256]{1,0:T(8,128)(2,1)}) %all-gather.4.cloned.1.call-update) | async-done | bytes 12582928 | tf_op jit(solution)/shard_map/all_gather | solution.py:546
  93.1 5.7 %own_expert.1 = (bf16[128,2048]{1,0:T(8,128)(2,1)S(1)}, bf16[8,3072,256]{2,1,0:T(8,128)(2,1)S(1)}) custom-call(bf16[128,2176]{1,0:T(8,128)(2,1)S(1)} %all-gather.rows_ref, bf16[8,3072,256]{2,1,0:T(8,128)(2,1)} %bitcast.7), custom_call_target="tpu_custom_call" | custom-call | tf_op jit(solution)/shard_map/own_expert/pallas_call | solution.py:410
  98.8 1.9 collective-permute-start.4
  100.7 3.5 %other_expert.2 = (bf16[128,2048]{1,0:T(8,128)(2,1)S(1)}, bf16[128,2048]{1,0:T(8,128)(2,1)S(1)}) custom-call(bf16[128,2176]{1,0:T(8,128)(2,1)S(1)} %collective-permute-done.refs_0_, bf16[128,2176]{1,0:T(8,128)(2,1)S(1)} %collective-permute-done.1.refs_1_, bf16[8,3072,256]{2,1,0:T(8,128)(2,1)S(1)} %get-tuple-element.27.refs_2_.refs_1_), custom_call_target="tpu_custom_call" | custom-call | tf_op jit(solution)/shard_map/other_expert/pallas_call | solution.py:430
  104.2 10.5 %collective-permute-done.4.refs_0_ = bf16[128,2176]{1,0:T(8,128)(2,1)S(1)} collective-permute-done((bf16[128,2176]{1,0:T(8,128)(2,1)S(1)}, bf16[128,2176]{1,0:T(8,128)(2,1)S(1)}, u32[]{:S(2)}, u32[]{:S(2)}) %collective-permute-start.4) | collective-permute-done | bytes 557088 | tf_op jit(solution)/shard_map/ppermute | solution.py:525
  114.7 1.8 other_expert.3
  116.6 3.0 %collective-permute-start.6 = (bf16[128,1024]{1,0:T(8,128)(2,1)S(1)}, bf16[128,1024]{1,0:T(8,128)(2,1)S(1)}, u32[]{:S(2)}, u32[]{:S(2)}) collective-permute-start(bf16[128,1024]{1,0:T(8,128)(2,1)S(1)} %get-tuple-element.32), channel_id=1, source_target_pairs={{0,384},{128,0},{256,128},{384,256},{1,385},{129,1},{257,129},{385... | collective-permute-start | bytes 786440 | tf_op jit(solution)/shard_map/ppermute | solution.py:525
  119.5 1.9 collective-permute-start.2
  121.5 3.4 %collective-permute-start.3 = (bf16[128,2048]{1,0:T(8,128)(2,1)S(1)}, bf16[128,2048]{1,0:T(8,128)(2,1)S(1)}, u32[]{:S(2)}, u32[]{:S(2)}) collective-permute-start(bf16[128,2048]{1,0:T(8,128)(2,1)S(1)} %get-tuple-element.29), channel_id=1, source_target_pairs={{0,128},{128,256},{256,384},{384,0},{1,129},{129,257},{257,385},{3... | collective-permute-start | bytes 1572872 | tf_op jit(solution)/shard_map/ppermute | solution.py:525
  124.8 2.6 %collective-permute-start.5 = (bf16[128,1024]{1,0:T(8,128)(2,1)S(1)}, bf16[128,1024]{1,0:T(8,128)(2,1)S(1)}, u32[]{:S(2)}, u32[]{:S(2)}) collective-permute-start(bf16[128,1024]{1,0:T(8,128)(2,1)S(1)} %get-tuple-element.31), channel_id=1, source_target_pairs={{0,256},{128,384},{256,0},{384,128},{1,257},{129,385},{257,1},{385... | collective-permute-start | bytes 786440 | tf_op jit(solution)/shard_map/ppermute | solution.py:525
  127.5 4.0 %collective-permute-start.7 = (bf16[128,1024]{1,0:T(8,128)(2,1)S(1)}, bf16[128,1024]{1,0:T(8,128)(2,1)S(1)}, u32[]{:S(2)}, u32[]{:S(2)}) collective-permute-start(bf16[128,1024]{1,0:T(8,128)(2,1)S(1)} %collective-permute-done.6), channel_id=1, source_target_pairs={{0,384},{128,0},{256,128},{384,256},{1,385},{129,1},{257,129},{385... | collective-permute-start | bytes 786440 | tf_op jit(solution)/shard_map/ppermute | solution.py:525
  131.5 10.3 %collective-permute-done.5 = bf16[128,1024]{1,0:T(8,128)(2,1)S(1)} collective-permute-done((bf16[128,1024]{1,0:T(8,128)(2,1)S(1)}, bf16[128,1024]{1,0:T(8,128)(2,1)S(1)}, u32[]{:S(2)}, u32[]{:S(2)}) %collective-permute-start.5) | collective-permute-done | bytes 262176 | tf_op jit(solution)/shard_map/ppermute | solution.py:525
  141.8 5.9 %collective-permute-done.7 = bf16[128,1024]{1,0:T(8,128)(2,1)S(1)} collective-permute-done((bf16[128,1024]{1,0:T(8,128)(2,1)S(1)}, bf16[128,1024]{1,0:T(8,128)(2,1)S(1)}, u32[]{:S(2)}, u32[]{:S(2)}) %collective-permute-start.7) | collective-permute-done | bytes 262176 | tf_op jit(solution)/shard_map/ppermute | solution.py:525
  148.1 17.5 %all_to_all.22.parts_ref = bf16[4,32,2048]{2,1,0:T(8,128)(2,1)S(1)} all-to-all(bf16[4,32,2048]{2,1,0:T(8,128)(2,1)S(1)} %join.1), channel_id=1, replica_groups={{0,8,16,24},{32,40,48,56},{64,72,80,88},{96,104,112,120},{1,9,17,25},{3..., dimensions={0} | all-to-all | bytes 1048576 | tf_op jit(solution)/shard_map/all_to_all | solution.py:594
  165.6 30.8 %all_to_all.23.parts_ref = bf16[32,8,256]{2,1,0:T(8,128)(2,1)S(1)} all-to-all(bf16[32,8,256]{2,1,0:T(8,128)(2,1)S(1)} %fold.1), channel_id=1, replica_groups={{0,1,2,3,4,5,6,7,32,33,34,35,36,37,38,39,64,65,66,67,68,69,70,71,96,97,..., dimensions={0} | all-to-all | bytes 262144 | tf_op jit(solution)/shard_map/all_to_all | solution.py:595
  (14 shorter events, 1.8 us)
Async XLA Ops:
  6.5 86.6 %all-gather.4.cloned.1.call-start = ((), (), s32[]{:S(2)}) async-start(), calls=%async_computation.4 | async-start | bytes 14155776 | tf_op jit(solution)/shard_map/all_gather | solution.py:546
  9.6 0.7 copy-start
  76.5 22.3 %collective-permute-start = (bf16[128,2176]{1,0:T(8,128)(2,1)S(1)}, bf16[128,2176]{1,0:T(8,128)(2,1)S(1)}, u32[]{:S(2)}, u32[]{:S(2)}) collective-permute-start(bf16[128,2176]{1,0:T(8,128)(2,1)S(1)} %all-gather.rows_ref), channel_id=1, source_target_pairs={{0,128},{128,256},{256,384},{384,0},{1,129},{129,257},{257,385},{3... | collective-permute-start | bytes 1671176 | tf_op jit(solution)/shard_map/ppermute | solution.py:525
  79.6 19.2 %collective-permute-start.1 = (bf16[128,2176]{1,0:T(8,128)(2,1)S(1)}, bf16[128,2176]{1,0:T(8,128)(2,1)S(1)}, u32[]{:S(2)}, u32[]{:S(2)}) collective-permute-start(bf16[128,2176]{1,0:T(8,128)(2,1)S(1)} %all-gather.rows_ref), channel_id=1, source_target_pairs={{0,384},{128,0},{256,128},{384,256},{1,385},{129,1},{257,129},{385... | collective-permute-start | bytes 1671176 | tf_op jit(solution)/shard_map/ppermute | solution.py:525
  98.8 15.9 %collective-permute-start.4 = (bf16[128,2176]{1,0:T(8,128)(2,1)S(1)}, bf16[128,2176]{1,0:T(8,128)(2,1)S(1)}, u32[]{:S(2)}, u32[]{:S(2)}) collective-permute-start(bf16[128,2176]{1,0:T(8,128)(2,1)S(1)} %collective-permute-done.1.refs_1_), channel_id=1, source_target_pairs={{0,384},{128,0},{256,128},{384,256},{1,385},{129,1},{257,129},{385... | collective-permute-start | bytes 1671176 | tf_op jit(solution)/shard_map/ppermute | solution.py:525
  116.6 10.9 %collective-permute-start.6 = (bf16[128,1024]{1,0:T(8,128)(2,1)S(1)}, bf16[128,1024]{1,0:T(8,128)(2,1)S(1)}, u32[]{:S(2)}, u32[]{:S(2)}) collective-permute-start(bf16[128,1024]{1,0:T(8,128)(2,1)S(1)} %get-tuple-element.32), channel_id=1, source_target_pairs={{0,384},{128,0},{256,128},{384,256},{1,385},{129,1},{257,129},{385... | collective-permute-start | bytes 786440 | tf_op jit(solution)/shard_map/ppermute | solution.py:525
  119.5 28.2 %collective-permute-start.2 = (bf16[128,2048]{1,0:T(8,128)(2,1)S(1)}, bf16[128,2048]{1,0:T(8,128)(2,1)S(1)}, u32[]{:S(2)}, u32[]{:S(2)}) collective-permute-start(bf16[128,2048]{1,0:T(8,128)(2,1)S(1)} %get-tuple-element.28), channel_id=1, source_target_pairs={{0,384},{128,0},{256,128},{384,256},{1,385},{129,1},{257,129},{385... | collective-permute-start | bytes 1572872 | tf_op jit(solution)/shard_map/ppermute | solution.py:525
  121.5 26.3 %collective-permute-start.3 = (bf16[128,2048]{1,0:T(8,128)(2,1)S(1)}, bf16[128,2048]{1,0:T(8,128)(2,1)S(1)}, u32[]{:S(2)}, u32[]{:S(2)}) collective-permute-start(bf16[128,2048]{1,0:T(8,128)(2,1)S(1)} %get-tuple-element.29), channel_id=1, source_target_pairs={{0,128},{128,256},{256,384},{384,0},{1,129},{129,257},{257,385},{3... | collective-permute-start | bytes 1572872 | tf_op jit(solution)/shard_map/ppermute | solution.py:525
  124.8 17.0 %collective-permute-start.5 = (bf16[128,1024]{1,0:T(8,128)(2,1)S(1)}, bf16[128,1024]{1,0:T(8,128)(2,1)S(1)}, u32[]{:S(2)}, u32[]{:S(2)}) collective-permute-start(bf16[128,1024]{1,0:T(8,128)(2,1)S(1)} %get-tuple-element.31), channel_id=1, source_target_pairs={{0,256},{128,384},{256,0},{384,128},{1,257},{129,385},{257,1},{385... | collective-permute-start | bytes 786440 | tf_op jit(solution)/shard_map/ppermute | solution.py:525
  127.5 20.2 %collective-permute-start.7 = (bf16[128,1024]{1,0:T(8,128)(2,1)S(1)}, bf16[128,1024]{1,0:T(8,128)(2,1)S(1)}, u32[]{:S(2)}, u32[]{:S(2)}) collective-permute-start(bf16[128,1024]{1,0:T(8,128)(2,1)S(1)} %collective-permute-done.6), channel_id=1, source_target_pairs={{0,384},{128,0},{256,128},{384,256},{1,385},{129,1},{257,129},{385... | collective-permute-start | bytes 786440 | tf_op jit(solution)/shard_map/ppermute | solution.py:525
Sparse Core Ops, SparseCore 0:
  9.5 83.5 all-gather.3
